TPU v7x, 32 devices: a whole 2x2x4 slice. The times are simulated.
32 devices in a mesh: grp: 4 (over x, core), rep: 8 (over z, y).
Axes of the slice: x: 2, y: 2, z: 4, core: 2. Of those that a mesh axis runs over, the one named last changes fastest.
Arguments:
- query_input: bfloat16 [64, 32, 768], P(('grp', 'rep')), may hold values from -6 to 6
- passage_input: bfloat16 [64, 256, 768], P(('grp', 'rep')), may hold values from -6 to 6
- query_length: int32 [64], P(('grp', 'rep')), may hold values from 2 to 30
- passage_length: int32 [64], P(('grp', 'rep')), may hold values from 32 to 200
- cluster_index: int32 [64], replicated, may hold values from 0 to 1
- margin_bin: int32 [64], P(('grp', 'rep')), may hold values from 0 to 9
- positive_index: int32 [64], P(('grp', 'rep')), may hold values from 0 to 63, each once
- query_cotangent: bfloat16 [64, 32, 768], P(('grp', 'rep')), may hold values from -0.29882812 to 0.29882812
- passage_cotangent: bfloat16 [64, 256, 768], P(('grp', 'rep')), may hold values from -0.29882812 to 0.29882812
- query_weight: bfloat16 [2, 768, 768], replicated, may hold values from -0.21875 to 0.21875
- query_bias: bfloat16 [2, 768], replicated, may hold values from -3 to 3
- key_weight: bfloat16 [2, 768, 768], replicated, may hold values from -0.21875 to 0.21875
- value_weight: bfloat16 [2, 768, 768], replicated, may hold values from -0.21875 to 0.21875
- value_bias: bfloat16 [2, 768], replicated, may hold values from -2 to 2
- mix_weight: bfloat16 [2, 768, 768], replicated, may hold values from -0.875 to 0.875
- mix_bias: bfloat16 [2, 768], replicated, may hold values from -2 to 2
- norm_gain: bfloat16 [2, 768], replicated, may hold values from 0.5 to 1.5
- norm_shift: bfloat16 [2, 768], replicated, may hold values from -1.1953125 to 1.1953125
- expand_weight: bfloat16 [2, 768, 3072], replicated, may hold values from -0.21875 to 0.21875
- expand_bias: bfloat16 [2, 3072], replicated, may hold values from -3 to 3
- reduce_weight: bfloat16 [2, 3072, 768], replicated, may hold values from -0.109375 to 0.109375
- reduce_bias: bfloat16 [2, 768], replicated, may hold values from -2 to 2
- final_gain: bfloat16 [2, 768], replicated, may hold values from 0.5 to 1.5
- final_shift: bfloat16 [2, 768], replicated, may hold values from -1.1953125 to 1.1953125
Outputs:
- query_output: bfloat16 [64, 32, 768], P(('grp', 'rep'))
- passage_output: bfloat16 [64, 256, 768], P(('grp', 'rep'))
- query_loss: float32 [64], P(('grp', 'rep'))
- query_input_gradient: float32 [64, 32, 768], P(('grp', 'rep'))
- passage_input_gradient: float32 [64, 256, 768], P(('grp', 'rep'))
- query_weight_gradient: float32 [2, 768, 768], P(None, 'grp')
- query_bias_gradient: float32 [2, 768], P(None, 'grp')
- key_weight_gradient: float32 [2, 768, 768], P(None, 'grp')
- value_weight_gradient: float32 [2, 768, 768], P(None, 'grp')
- value_bias_gradient: float32 [2, 768], P(None, 'grp')
- mix_weight_gradient: float32 [2, 768, 768], P(None, 'grp')
- mix_bias_gradient: float32 [2, 768], P(None, 'grp')
- norm_gain_gradient: float32 [2, 768], P(None, 'grp')
- norm_shift_gradient: float32 [2, 768], P(None, 'grp')
- expand_weight_gradient: float32 [2, 768, 3072], P(None, 'grp')
- expand_bias_gradient: float32 [2, 3072], P(None, 'grp')
- reduce_weight_gradient: float32 [2, 3072, 768], P(None, 'grp')
- reduce_bias_gradient: float32 [2, 768], P(None, 'grp')
- final_gain_gradient: float32 [2, 768], P(None, 'grp')
- final_shift_gradient: float32 [2, 768], P(None, 'grp')
Inputs may be any that keep to these rules, and one draw needn't show every extreme that they name: `positive_index`: each passage is the positive of exactly one query.
All inputs are finite; a program needn't handle non-finite values.
Results may differ from a plain program's by a relative error of at most 0.028.
Values may be sent and summed in bfloat16 or wider, within the bound.
A program may use at most 256 MiB of HBM per device.

v0:
```python
import math

import jax
import jax.numpy as jnp
from jax import lax
from jax.sharding import PartitionSpec as P

HEADS = 12
DH = 64
LAYERS = 2
NBINS = 10


def narrow(values):
    return values.astype(jnp.bfloat16)


def product(former, latter):
    return jnp.dot(former, latter, preferred_element_type=jnp.float32)


def contract_rows(former, latter):
    return lax.dot_general(
        former, latter, (((0,), (0,)), ((), ())), preferred_element_type=jnp.float32
    )


def contract_last(former, latter):
    return lax.dot_general(
        former, latter, (((1,), (1,)), ((), ())), preferred_element_type=jnp.float32
    )


def column_total(values):
    return jnp.sum(values.astype(jnp.float32), axis=0)


def norm_forward(summed, gain_vector, shift_vector):
    average = jnp.mean(summed, axis=-1, keepdims=True)
    centred = summed - average
    scaled = lax.rsqrt(jnp.mean(centred * centred, axis=-1, keepdims=True) + 1e-12)
    unit_rows = centred * scaled
    return (unit_rows * gain_vector + shift_vector, unit_rows, scaled)


def norm_backward(upstream, unit_rows, scaled, gain_vector):
    delta_unit = upstream * gain_vector
    delta_summed = scaled * (
        delta_unit
        - jnp.mean(delta_unit, axis=-1, keepdims=True)
        - unit_rows * jnp.mean(delta_unit * unit_rows, axis=-1, keepdims=True)
    )
    return (delta_summed, jnp.sum(upstream * unit_rows, axis=0), jnp.sum(upstream, axis=0))


def gelu_slope(expanded):
    cumulative = 0.5 * (1.0 + lax.erf(expanded * (1.0 / math.sqrt(2.0))))
    density = jnp.exp(-0.5 * expanded * expanded) * (1.0 / math.sqrt(2.0 * math.pi))
    return cumulative + expanded * density


def split_heads(flat, group_count, length):
    return flat.reshape(group_count, length, HEADS, DH)


def group_spans(layout):
    spans = []
    offset = 0
    for group_count, length in layout:
        spans.append((offset, group_count, length))
        offset = offset + group_count * length
    return spans


def head_scores(query_part, key_part, keep_mask):
    scores = (
        jnp.einsum("bqhd,bkhd->bhqk", query_part, key_part, preferred_element_type=jnp.float32)
        * 0.125
    )
    return jnp.where(keep_mask[:, None, None, :], scores, -1e30)


def attend_forward(query_part, key_part, value_part, keep_mask):
    scores = head_scores(query_part, key_part, keep_mask)
    peak_score = jnp.max(scores, axis=-1, keepdims=True)
    normalizer = peak_score + jnp.log(jnp.sum(jnp.exp(scores - peak_score), axis=-1, keepdims=True))
    attention = narrow(jnp.exp(scores - normalizer))
    context = jnp.einsum(
        "bhqk,bkhd->bqhd", attention, value_part, preferred_element_type=jnp.float32
    )
    return (narrow(context), normalizer)


def attend_backward(query_part, key_part, value_part, keep_mask, normalizer, delta_context):
    scores = head_scores(query_part, key_part, keep_mask)
    attention = jnp.exp(scores - normalizer)
    delta_value = jnp.einsum(
        "bhqk,bqhd->bkhd", narrow(attention), delta_context, preferred_element_type=jnp.float32
    )
    delta_attention = jnp.einsum(
        "bqhd,bkhd->bhqk", delta_context, value_part, preferred_element_type=jnp.float32
    )
    delta_scores = narrow(
        attention * (delta_attention - jnp.sum(attention * delta_attention, axis=-1, keepdims=True))
    )
    delta_query = (
        jnp.einsum("bhqk,bkhd->bqhd", delta_scores, key_part, preferred_element_type=jnp.float32)
        * 0.125
    )
    delta_key = (
        jnp.einsum("bhqk,bqhd->bkhd", delta_scores, query_part, preferred_element_type=jnp.float32)
        * 0.125
    )
    return (delta_query, delta_key, delta_value)


def layer_forward(hidden, keep_masks, layout, params):
    (
        query_weight,
        query_bias,
        key_weight,
        value_weight,
        value_bias,
        mix_weight,
        mix_bias,
        norm_gain,
        norm_shift,
        expand_weight,
        expand_bias,
        reduce_weight,
        reduce_bias,
        final_gain,
        final_shift,
    ) = params
    query_heads = narrow(product(hidden, query_weight) + query_bias)
    key_heads = narrow(product(hidden, key_weight))
    value_heads = narrow(product(hidden, value_weight) + value_bias)
    contexts = []
    normalizers = []
    for keep_mask, (offset, group_count, length) in zip(keep_masks, group_spans(layout)):
        row_span = group_count * length
        pieces = [
            split_heads(array[offset : offset + row_span], group_count, length)
            for array in (query_heads, key_heads, value_heads)
        ]
        context, normalizer = attend_forward(pieces[0], pieces[1], pieces[2], keep_mask)
        contexts.append(context.reshape(row_span, -1))
        normalizers.append(normalizer)
    context = jnp.concatenate(contexts, axis=0)
    summed_one = hidden.astype(jnp.float32) + product(context, mix_weight) + mix_bias
    middle_full, unit_one, scale_one = norm_forward(summed_one, norm_gain, norm_shift)
    middle = narrow(middle_full)
    expanded = product(middle, expand_weight) + expand_bias
    active = narrow(jax.nn.gelu(expanded, approximate=False))
    summed_two = middle.astype(jnp.float32) + product(active, reduce_weight) + reduce_bias
    result_full, unit_two, scale_two = norm_forward(summed_two, final_gain, final_shift)
    stored = (
        hidden,
        query_heads,
        key_heads,
        value_heads,
        normalizers,
        context,
        unit_one,
        scale_one,
        middle,
        expanded,
        active,
        unit_two,
        scale_two,
    )
    return (narrow(result_full), stored)


def layer_backward(upstream, stored, keep_masks, layout, params):
    (
        query_weight,
        query_bias,
        key_weight,
        value_weight,
        value_bias,
        mix_weight,
        mix_bias,
        norm_gain,
        norm_shift,
        expand_weight,
        expand_bias,
        reduce_weight,
        reduce_bias,
        final_gain,
        final_shift,
    ) = params
    (
        hidden,
        query_heads,
        key_heads,
        value_heads,
        normalizers,
        context,
        unit_one,
        scale_one,
        middle,
        expanded,
        active,
        unit_two,
        scale_two,
    ) = stored
    delta_two, delta_final_gain, delta_final_shift = norm_backward(
        upstream, unit_two, scale_two, final_gain
    )
    delta_branch = narrow(delta_two)
    delta_reduce_weight = contract_rows(active, delta_branch)
    delta_reduce_bias = column_total(delta_branch)
    delta_expanded = narrow(contract_last(delta_branch, reduce_weight) * gelu_slope(expanded))
    delta_expand_weight = contract_rows(middle, delta_expanded)
    delta_expand_bias = column_total(delta_expanded)
    delta_middle = delta_two + contract_last(delta_expanded, expand_weight)
    delta_one, delta_norm_gain, delta_norm_shift = norm_backward(
        delta_middle, unit_one, scale_one, norm_gain
    )
    delta_mix = narrow(delta_one)
    delta_mix_weight = contract_rows(context, delta_mix)
    delta_mix_bias = column_total(delta_mix)
    delta_context = narrow(contract_last(delta_mix, mix_weight))
    collected = ([], [], [])
    for keep_mask, normalizer, (offset, group_count, length) in zip(
        keep_masks, normalizers, group_spans(layout)
    ):
        row_span = group_count * length
        pieces = [
            split_heads(array[offset : offset + row_span], group_count, length)
            for array in (query_heads, key_heads, value_heads, delta_context)
        ]
        results = attend_backward(pieces[0], pieces[1], pieces[2], keep_mask, normalizer, pieces[3])
        for bucket, gradient in zip(collected, results):
            bucket.append(narrow(gradient.reshape(row_span, -1)))
    delta_query = jnp.concatenate(collected[0], axis=0)
    delta_key = jnp.concatenate(collected[1], axis=0)
    delta_value = jnp.concatenate(collected[2], axis=0)
    delta_hidden = (
        delta_one
        + contract_last(delta_query, query_weight)
        + contract_last(delta_key, key_weight)
        + contract_last(delta_value, value_weight)
    )
    gradients = (
        contract_rows(hidden, delta_query),
        column_total(delta_query),
        contract_rows(hidden, delta_key),
        contract_rows(hidden, delta_value),
        column_total(delta_value),
        delta_mix_weight,
        delta_mix_bias,
        delta_norm_gain,
        delta_norm_shift,
        delta_expand_weight,
        delta_expand_bias,
        delta_reduce_weight,
        delta_reduce_bias,
        delta_final_gain,
        delta_final_shift,
    )
    return (delta_hidden, gradients)


def reduce_layer(gradients):
    shards = (
        lax.psum_scatter(
            gradients[0].astype(jnp.bfloat16), "grp", scatter_dimension=0, tiled=True
        ).astype(jnp.float32),
        lax.psum_scatter(
            gradients[1].astype(jnp.bfloat16), "grp", scatter_dimension=0, tiled=True
        ).astype(jnp.float32),
        lax.psum_scatter(
            gradients[2].astype(jnp.bfloat16), "grp", scatter_dimension=0, tiled=True
        ).astype(jnp.float32),
        lax.psum_scatter(
            gradients[3].astype(jnp.bfloat16), "grp", scatter_dimension=0, tiled=True
        ).astype(jnp.float32),
        lax.psum_scatter(
            gradients[4].astype(jnp.bfloat16), "grp", scatter_dimension=0, tiled=True
        ).astype(jnp.float32),
        lax.psum_scatter(
            gradients[5].astype(jnp.bfloat16), "grp", scatter_dimension=0, tiled=True
        ).astype(jnp.float32),
        lax.psum_scatter(
            gradients[6].astype(jnp.bfloat16), "grp", scatter_dimension=0, tiled=True
        ).astype(jnp.float32),
        lax.psum_scatter(
            gradients[7].astype(jnp.bfloat16), "grp", scatter_dimension=0, tiled=True
        ).astype(jnp.float32),
        lax.psum_scatter(
            gradients[8].astype(jnp.bfloat16), "grp", scatter_dimension=0, tiled=True
        ).astype(jnp.float32),
        lax.psum_scatter(
            gradients[9].astype(jnp.bfloat16), "grp", scatter_dimension=0, tiled=True
        ).astype(jnp.float32),
        lax.psum_scatter(
            gradients[10].astype(jnp.bfloat16), "grp", scatter_dimension=0, tiled=True
        ).astype(jnp.float32),
        lax.psum_scatter(
            gradients[11].astype(jnp.bfloat16), "grp", scatter_dimension=0, tiled=True
        ).astype(jnp.float32),
        lax.psum_scatter(
            gradients[12].astype(jnp.bfloat16), "grp", scatter_dimension=0, tiled=True
        ).astype(jnp.float32),
        lax.psum_scatter(
            gradients[13].astype(jnp.bfloat16), "grp", scatter_dimension=0, tiled=True
        ).astype(jnp.float32),
        lax.psum_scatter(
            gradients[14].astype(jnp.bfloat16), "grp", scatter_dimension=0, tiled=True
        ).astype(jnp.float32),
    )
    reduced = lax.psum(
        (
            shards[0],
            shards[1],
            shards[2],
            shards[3],
            shards[4],
            shards[5],
            shards[6],
            shards[7],
            shards[8],
            shards[9],
            shards[10],
            shards[11],
            shards[12],
            shards[13],
            shards[14],
        ),
        "rep",
    )
    return list(reduced)


def per_device(
    query_input,
    passage_input,
    query_length,
    passage_length,
    cluster_index,
    margin_bin,
    positive_index,
    query_cotangent,
    passage_cotangent,
    query_weight,
    query_bias,
    key_weight,
    value_weight,
    value_bias,
    mix_weight,
    mix_bias,
    norm_gain,
    norm_shift,
    expand_weight,
    expand_bias,
    reduce_weight,
    reduce_bias,
    final_gain,
    final_shift,
):
    params = (
        query_weight,
        query_bias,
        key_weight,
        value_weight,
        value_bias,
        mix_weight,
        mix_bias,
        norm_gain,
        norm_shift,
        expand_weight,
        expand_bias,
        reduce_weight,
        reduce_bias,
        final_gain,
        final_shift,
    )
    batch_size, query_len, model_width = query_input.shape
    passage_len = passage_input.shape[1]
    layout = ((batch_size, query_len), (batch_size, passage_len))
    keep_masks = (
        lax.broadcasted_iota(jnp.int32, (batch_size, query_len), 1) < query_length[:, None],
        lax.broadcasted_iota(jnp.int32, (batch_size, passage_len), 1) < passage_length[:, None],
    )
    query_span = batch_size * query_len
    hidden = jnp.concatenate(
        [
            query_input.reshape(query_span, model_width),
            passage_input.reshape(batch_size * passage_len, model_width),
        ],
        axis=0,
    )
    stored_layers = []
    for layer_index in range(LAYERS):
        layer_params = tuple((array[layer_index] for array in params))
        hidden, stored = layer_forward(hidden, keep_masks, layout, layer_params)
        stored_layers.append(stored)
    query_output = hidden[:query_span].reshape(batch_size, query_len, model_width)
    passage_output = hidden[query_span:].reshape(batch_size, passage_len, model_width)
    query_first = query_output[:, 0, :]
    passage_first = passage_output[:, 0, :]
    every_passage = lax.all_gather(passage_first, ("grp", "rep"), axis=0, tiled=True)
    start_row = lax.axis_index(("grp", "rep")) * batch_size
    own_cluster = lax.dynamic_slice_in_dim(cluster_index, start_row, batch_size)
    score_scale = 2.0 / math.sqrt(model_width)
    logits = contract_last(query_first, every_passage) * score_scale
    columns = lax.broadcasted_iota(jnp.int32, logits.shape, 1)
    chosen_mask = columns == positive_index[:, None]
    allowed = (cluster_index[None, :] == own_cluster[:, None]) | chosen_mask
    masked = jnp.where(allowed, logits, -1e30)
    peak_score = jnp.max(masked, axis=1, keepdims=True)
    normalizer = peak_score + jnp.log(jnp.sum(jnp.exp(masked - peak_score), axis=1, keepdims=True))
    chosen = jnp.sum(jnp.where(chosen_mask, logits, 0.0), axis=1)
    margin_weight = (margin_bin + 1).astype(jnp.float32) / NBINS
    query_loss = margin_weight * (normalizer[:, 0] - chosen)
    delta_logits = narrow(
        margin_weight[:, None]
        * (jnp.where(allowed, jnp.exp(masked - normalizer), 0.0) - chosen_mask.astype(jnp.float32))
    )
    delta_query_first = product(delta_logits, every_passage) * score_scale
    delta_passage_first = lax.psum_scatter(
        contract_rows(delta_logits, query_first) * score_scale,
        ("grp", "rep"),
        scatter_dimension=0,
        tiled=True,
    )
    query_upstream = query_cotangent.astype(jnp.float32).at[:, 0, :].add(delta_query_first)
    passage_upstream = passage_cotangent.astype(jnp.float32).at[:, 0, :].add(delta_passage_first)
    upstream = jnp.concatenate(
        [
            query_upstream.reshape(query_span, model_width),
            passage_upstream.reshape(batch_size * passage_len, model_width),
        ],
        axis=0,
    )
    per_layer = []
    for layer_index in reversed(range(LAYERS)):
        layer_params = tuple((array[layer_index] for array in params))
        upstream, layer_grads = layer_backward(
            upstream, stored_layers[layer_index], keep_masks, layout, layer_params
        )
        per_layer.append(reduce_layer(layer_grads))
    per_layer = per_layer[::-1]
    reduced = [
        jnp.stack([per_layer[layer_index][slot] for layer_index in range(LAYERS)])
        for slot in range(15)
    ]
    query_input_gradient = upstream[:query_span].reshape(batch_size, query_len, model_width)
    passage_input_gradient = upstream[query_span:].reshape(batch_size, passage_len, model_width)
    return (
        query_output,
        passage_output,
        query_loss,
        query_input_gradient,
        passage_input_gradient,
        reduced[0],
        reduced[1],
        reduced[2],
        reduced[3],
        reduced[4],
        reduced[5],
        reduced[6],
        reduced[7],
        reduced[8],
        reduced[9],
        reduced[10],
        reduced[11],
        reduced[12],
        reduced[13],
        reduced[14],
    )


def solution(mesh):
    placed = (
        P(("grp", "rep"), None, None),
        P(("grp", "rep"), None, None),
        P(("grp", "rep")),
        P(("grp", "rep")),
        P(),
        P(("grp", "rep")),
        P(("grp", "rep")),
        P(("grp", "rep"), None, None),
        P(("grp", "rep"), None, None),
        P(),
        P(),
        P(),
        P(),
        P(),
        P(),
        P(),
        P(),
        P(),
        P(),
        P(),
        P(),
        P(),
        P(),
        P(),
    )
    return jax.shard_map(
        per_device,
        mesh=mesh,
        in_specs=placed,
        out_specs=(
            P(("grp", "rep"), None, None),
            P(("grp", "rep"), None, None),
            P(("grp", "rep")),
            P(("grp", "rep"), None, None),
            P(("grp", "rep"), None, None),
            P(None, "grp", None),
            P(None, "grp"),
            P(None, "grp", None),
            P(None, "grp", None),
            P(None, "grp"),
            P(None, "grp", None),
            P(None, "grp"),
            P(None, "grp"),
            P(None, "grp"),
            P(None, "grp", None),
            P(None, "grp"),
            P(None, "grp", None),
            P(None, "grp"),
            P(None, "grp"),
            P(None, "grp"),
        ),
        check_vma=False,
    )
```

profile of v0, /device:TPU:0, one launch (start us, length us, event | category | flops | bytes accessed | tf_op | source)
XLA Modules:
  0.0 1238.2 jit_solution(1331082715908673952)
XLA Ops:
  8.1 2.6 add_convert_fusion.7
  16.9 3.4 reshape.403
  21.7 2.2 reshape.404
  40.2 20.3 %fusion.2 = (bf16[576,3072]{1,0:T(8,128)(2,1)S(1)}, f32[576,3072]{1,0:T(8,128)}) fusion(f32[3072]{0:T(1024)S(1)} %bitcast.341, bf16[2,768,3072]{2,1,0:T(8,128)(2,1)S(1)} %bitcast.366, f32[576,768]{1,0:T(8,128)S(1)} %get-tuple-element.145, f32[768]{0:T(1024)S(1)} %get-tuple-element.68, f32[768]{0:T(1024)S(1)} %get-tuple-element.192, ...), kind=kOutput, calls=%fused_computation.6 | convolution fusion | flops 2836905984 | bytes 17133568 | tf_op jit(solution)/shard_map/dot_general | solution.py:19
  60.6 3.1 fusion.213
  72.1 2.2 reshape.412
  76.5 2.9 reshape.411
  93.0 19.9 %fusion.5 = (bf16[576,3072]{1,0:T(8,128)(2,1)S(1)}, f32[576,3072]{1,0:T(8,128)}) fusion(f32[3072]{0:T(1024)S(1)} %bitcast.343, bf16[2,768,3072]{2,1,0:T(8,128)(2,1)S(1)} %bitcast.368, f32[576,768]{1,0:T(8,128)S(1)} %get-tuple-element.155, f32[768]{0:T(1024)S(1)} %copy-done.167, f32[768]{0:T(1024)S(1)} %copy-done.134, f32[576]{0:T(1024)S(1)} %add_rsqrt_fusion.1, ...), kind=kOutput, calls=%fused_computation.9 | convolution fusion | flops 2836905984 | bytes 17133568 | tf_op jit(solution)/shard_map/dot_general | solution.py:19
  112.9 3.1 fusion.216
  117.1 71.1 %all-gather = bf16[64,1,768]{2,1,0:T(2,128)(2,1)S(1)} all-gather(bf16[2,1,768]{2,1,0:T(2,128)(2,1)S(1)} %slice.297), channel_id=2, replica_groups=mesh['grp'=4,'rep'=8] {'grp','rep'}, dimensions={0}, use_global_device_ids=true | all-gather | bytes 101376 | tf_op jit(solution)/shard_map/all_gather | solution.py:404
  190.5 1.9 copy_convert_fusion
  194.1 115.5 %all-reduce.25.cloned.1.call-done = f32[64,768]{1,0:T(8,128)} async-done(((f32[64,768]{1,0:T(8,128)}), f32[64,768]{1,0:T(8,128)}) %all-reduce.25.cloned.1.call-update) | async-done | bytes 196624
  313.2 9.2 fusion.225
  322.5 3.9 multiply_reduce_fusion.4
  327.6 2.2 convolution_convert_fusion.4
  330.3 2.2 convolution_convert_fusion.13
  334.9 5.4 fusion.222
  342.2 2.5 convolution_convert_fusion.6
  346.3 5.1 multiply_reduce_fusion.1
  351.4 1.9 multiply_convert_fusion.1
  356.4 2.4 convolution_convert_fusion.8
  359.1 2.5 fusion.217
  363.7 2.1 fusion.218
  371.9 2.6 multiply_reduce_fusion.3
  375.7 2.4 convolution_convert_fusion.10
  378.2 1.8 convert_reduce_fusion.17
  380.1 9.2 fusion.226
  389.3 7.7 multiply_reduce_fusion.5
  398.2 2.2 convolution_convert_fusion.5
  400.9 2.2 convolution_convert_fusion.12
  404.9 5.1 fusion.224
  411.9 2.4 convolution_convert_fusion.7
  416.8 4.9 multiply_reduce_fusion
  421.8 1.9 multiply_convert_fusion
  426.7 2.4 convolution_convert_fusion.9
  429.4 2.5 fusion.219
  434.0 2.5 fusion.220
  437.7 2.4 convolution_convert_fusion.11
  440.2 7.7 convolution_convert_fusion
  449.5 8.0 convolution_convert_fusion.2
  458.9 7.8 convolution_convert_fusion.3
  468.2 7.8 convolution_convert_fusion.1
  476.3 1.8 bitcast_convert_fusion.4
  478.1 1.9 bitcast_convert_fusion.6
  480.0 1.9 bitcast_convert_fusion.8
  485.5 13.9 %reduce-scatter.21.cloned.1.call-done = bf16[192,768]{1,0:T(8,128)(2,1)} async-done(((bf16[768,768]{1,0:T(8,128)(2,1)}), bf16[192,768]{1,0:T(8,128)(2,1)}) %reduce-scatter.21.cloned.1.call-update) | async-done | bytes 294928 | tf_op jit(solution)/shard_map/reduce_scatter | solution.py:277
  499.4 1.8 bitcast_convert_fusion.7
  501.2 27.1 %reduce-scatter.17.cloned.1.call-done = bf16[192,768]{1,0:T(8,128)(2,1)} async-done(((bf16[768,768]{1,0:T(8,128)(2,1)}), bf16[192,768]{1,0:T(8,128)(2,1)}) %reduce-scatter.17.cloned.1.call-update) | async-done | bytes 294928 | tf_op jit(solution)/shard_map/reduce_scatter | solution.py:274
  530.1 27.3 %reduce-scatter.13.cloned.1.call-done = bf16[192,768]{1,0:T(8,128)(2,1)} async-done(((bf16[768,768]{1,0:T(8,128)(2,1)}), bf16[192,768]{1,0:T(8,128)(2,1)}) %reduce-scatter.13.cloned.1.call-update) | async-done | bytes 294928 | tf_op jit(solution)/shard_map/reduce_scatter | solution.py:268
  559.2 48.4 %reduce-scatter.35.cloned.1.call-done = bf16[768,768]{1,0:T(8,128)(2,1)} async-done(((bf16[3072,768]{1,0:T(8,128)(2,1)}), bf16[768,768]{1,0:T(8,128)(2,1)}) %reduce-scatter.35.cloned.1.call-update) | async-done | bytes 1179664 | tf_op jit(solution)/shard_map/reduce_scatter | solution.py:301
  607.6 2.8 bitcast_convert_fusion
  610.4 48.3 %reduce-scatter.31.cloned.1.call-done = bf16[192,3072]{1,0:T(8,128)(2,1)} async-done(((bf16[768,3072]{1,0:T(8,128)(2,1)}), bf16[192,3072]{1,0:T(8,128)(2,1)}) %reduce-scatter.31.cloned.1.call-update) | async-done | bytes 1179664 | tf_op jit(solution)/shard_map/reduce_scatter | solution.py:295
  658.7 2.9 bitcast_convert_fusion.2
  661.6 47.9 %reduce-scatter.29.cloned.1.call-done = bf16[192,3072]{1,0:T(8,128)(2,1)} async-done(((bf16[768,3072]{1,0:T(8,128)(2,1)}), bf16[192,3072]{1,0:T(8,128)(2,1)}) %reduce-scatter.29.cloned.1.call-update) | async-done | bytes 1179664 | tf_op jit(solution)/shard_map/reduce_scatter | solution.py:295
  709.6 2.9 bitcast_convert_fusion.3
  712.5 47.6 %reduce-scatter.33.cloned.1.call-done = bf16[768,768]{1,0:T(8,128)(2,1)} async-done(((bf16[3072,768]{1,0:T(8,128)(2,1)}), bf16[768,768]{1,0:T(8,128)(2,1)}) %reduce-scatter.33.cloned.1.call-update) | async-done | bytes 1179664 | tf_op jit(solution)/shard_map/reduce_scatter | solution.py:301
  760.1 2.8 bitcast_convert_fusion.1
  766.2 2.8 fusion.86
  775.6 11.4 all-reduce.21
  788.4 39.7 %all-reduce.19 = (f32[1,192]{1,0:T(1,128)S(1)}, f32[1,192]{1,0:T(1,128)S(1)}, f32[1,192]{1,0:T(1,128)S(1)}, f32[1,192]{1,0:T(1,128)S(1)}, f32[1,192]{1,0:T(1,128...) all-reduce(f32[1,192]{1,0:T(1,128)S(1)} %bitcast.345, ...), channel_id=1, replica_groups=mesh['grp'=4,'rep'=8] {'rep'}, use_global_device_ids=true, to_apply=%region_43.44 | all-reduce | flops 4608 | bytes 36864 | tf_op jit(solution)/shard_map/psum | solution.py:314
  833.3 384.6 %all-reduce.27.cloned.1.call-done = (f32[1,192,768]{2,1,0:T(8,128)}, f32[1,192,768]{2,1,0:T(8,128)}, f32[1,192,768]{2,1,0:T(8,128)}, f32[1,192,768]{2,1,0:T(8,12...) async-done(((f32[1,192,768]{2,1,0:T(8,128)}, ...) | async-done | bytes 14155792 | tf_op jit(solution)/shard_map/psum | solution.py:314
  1217.9 2.5 pad_maximum_fusion.3
  1224.8 2.9 pad_maximum_fusion
  1228.9 2.5 pad_maximum_fusion.1
  (716 shorter events, 122.2 us)
Async XLA Ops:
  7.2 302.5 %all-reduce.25.cloned.1.call-start = ((), (), s32[]{:S(2)}) async-start(), calls=%async_computation.24 | async-start | bytes 393216
  13.7 6.8 slice-start.9
  13.9 72.4 %copy-start.108 = (pred[2,256]{1,0:T(4,128)(4,1)}, pred[2,256]{1,0:T(4,128)(4,1)S(1)}, u32[]{:S(2)}) copy-start(pred[2,256]{1,0:T(4,128)(4,1)S(1)} %iota_compare_fusion) | copy-start | bytes 1540
  15.7 24.4 %copy-start.151 = (f32[1,3072]{1,0:T(1,128)}, f32[1,3072]{1,0:T(1,128)S(1)}, u32[]{:S(2)}) copy-start(f32[1,3072]{1,0:T(1,128)S(1)} %get-tuple-element.138) | copy-start | bytes 36868
  16.9 7.1 slice-start.8
  29.2 6.8 copy-start.97
  33.4 6.8 slice-start.22
  33.4 6.8 slice-start.23
  37.8 22.8 %slice-start.16 = ((s8[9437184]{0:T(1024)(128)(4,1)}), s8[4194304]{0:T(1024)(128)(4,1)S(1)}, s32[]{:S(2)}) async-start(s8[9437184]{0:T(1024)(128)(4,1)} %bitcast.361), calls=%async_computation.42 | async-start | bytes 8388608
  39.1 21.4 %copy-start.18 = (f32[576,768]{1,0:T(8,128)}, f32[576,768]{1,0:T(8,128)S(1)}, u32[]{:S(2)}) copy-start(f32[576,768]{1,0:T(8,128)S(1)} %get-tuple-element.145) | copy-start | bytes 5308420
  39.1 21.4 %copy-start.126 = (f32[576]{0:T(1024)}, f32[576]{0:T(1024)S(1)}, u32[]{:S(2)}) copy-start(f32[576]{0:T(1024)S(1)} %broadcast_multiply_fusion.11) | copy-start | bytes 6916
  39.5 21.0 %copy-start.138 = (f32[576]{0:T(1024)}, f32[576]{0:T(1024)S(1)}, u32[]{:S(2)}) copy-start(f32[576]{0:T(1024)S(1)} %add_rsqrt_fusion.3) | copy-start | bytes 6916
  40.2 20.4 %copy-start.132 = (f32[768]{0:T(1024)}, f32[768]{0:T(1024)S(1)}, u32[]{:S(2)}) copy-start(f32[768]{0:T(1024)S(1)} %get-tuple-element.192) | copy-start | bytes 9220
  40.2 20.4 %copy-start.165 = (f32[768]{0:T(1024)}, f32[768]{0:T(1024)S(1)}, u32[]{:S(2)}) copy-start(f32[768]{0:T(1024)S(1)} %get-tuple-element.68) | copy-start | bytes 9220
  40.2 20.4 %slice-start.17 = ((s8[9437184]{0:T(1024)(128)(4,1)}), s8[4194304]{0:T(1024)(128)(4,1)S(1)}, s32[]{:S(2)}) async-start(s8[9437184]{0:T(1024)(128)(4,1)} %bitcast.361), calls=%async_computation.43 | async-start | bytes 8388608
  40.2 20.4 %slice-start.18 = ((s8[9437184]{0:T(1024)(128)(4,1)}), s8[1048576]{0:T(1024)(128)(4,1)S(1)}, s32[]{:S(2)}) async-start(s8[9437184]{0:T(1024)(128)(4,1)} %bitcast.361), calls=%async_computation.44 | async-start | bytes 2097152
  64.3 52.2 %copy-start.121 = (f32[768]{0:T(1024)}, f32[768]{0:T(1024)S(1)}, u32[]{:S(2)}) copy-start(f32[768]{0:T(1024)S(1)} %get-tuple-element.195) | copy-start | bytes 9220
  72.1 7.4 slice-start.14
  74.3 9.0 copy-start.16
  83.3 7.3 copy-start.103
  84.9 8.0 slice-start.25
  91.1 21.8 %slice-start.19 = ((s8[9437184]{0:T(1024)(128)(4,1)}), s8[4194304]{0:T(1024)(128)(4,1)S(1)}, s32[]{:S(2)}) async-start(s8[9437184]{0:T(1024)(128)(4,1)} %bitcast.363), calls=%async_computation.45 | async-start | bytes 8388608
  92.5 20.4 %copy-start.21 = (f32[576,768]{1,0:T(8,128)}, f32[576,768]{1,0:T(8,128)S(1)}, u32[]{:S(2)}) copy-start(f32[576,768]{1,0:T(8,128)S(1)} %get-tuple-element.155) | copy-start | bytes 5308420
  92.5 20.4 %copy-start.128 = (f32[576]{0:T(1024)}, f32[576]{0:T(1024)S(1)}, u32[]{:S(2)}) copy-start(f32[576]{0:T(1024)S(1)} %broadcast_multiply_fusion.9) | copy-start | bytes 6916
  92.9 20.0 %copy-start.141 = (f32[576]{0:T(1024)}, f32[576]{0:T(1024)S(1)}, u32[]{:S(2)}) copy-start(f32[576]{0:T(1024)S(1)} %add_rsqrt_fusion.1) | copy-start | bytes 6916
  92.9 20.0 %copy-start.173 = (f32[768]{0:T(1024)S(1)}, f32[768]{0:T(1024)}, u32[]{:S(2)}) copy-start(f32[768]{0:T(1024)} %get-tuple-element.63) | copy-start | bytes 9220
  92.9 20.0 %slice-start.20 = ((s8[9437184]{0:T(1024)(128)(4,1)}), s8[4194304]{0:T(1024)(128)(4,1)S(1)}, s32[]{:S(2)}) async-start(s8[9437184]{0:T(1024)(128)(4,1)} %bitcast.363), calls=%async_computation.46 | async-start | bytes 8388608
  93.0 20.0 %slice-start.21 = ((s8[9437184]{0:T(1024)(128)(4,1)}), s8[1048576]{0:T(1024)(128)(4,1)S(1)}, s32[]{:S(2)}) async-start(s8[9437184]{0:T(1024)(128)(4,1)} %bitcast.363), calls=%async_computation.47 | async-start | bytes 2097152
  116.4 71.7 %copy-start.205 = (s32[64]{0:T(128)S(1)}, s32[64]{0:T(128)}, u32[]{:S(2)}) copy-start(s32[64]{0:T(128)} %param.32) | copy-start | bytes 772
  116.4 71.8 %copy-start.175 = (s32[2]{0:T(128)S(1)}, s32[2]{0:T(128)}, u32[]{:S(2)}) copy-start(s32[2]{0:T(128)} %param.34) | copy-start | bytes 28
  116.5 72.3 %copy-start.183 = (s32[2]{0:T(128)S(1)}, s32[2]{0:T(128)}, u32[]{:S(2)}) copy-start(s32[2]{0:T(128)} %param.33) | copy-start | bytes 28
  116.5 73.9 %copy-start.116 = (bf16[2,32,768]{2,1,0:T(8,128)(2,1)S(1)}, bf16[2,32,768]{2,1,0:T(8,128)(2,1)}, u32[]{:S(2)}) copy-start(bf16[2,32,768]{2,1,0:T(8,128)(2,1)} %param.35) | copy-start | bytes 294916
  116.9 73.4 %copy-start.111 = (bf16[64,768]{1,0:T(8,128)(2,1)}, bf16[64,768]{1,0:T(8,128)(2,1)S(1)}, u32[]{:S(2)}) copy-start(bf16[64,768]{1,0:T(8,128)(2,1)S(1)} %slice.294) | copy-start | bytes 294916
  117.0 73.4 %copy-start.70 = (bf16[512,768]{1,0:T(8,128)(2,1)}, bf16[512,768]{1,0:T(8,128)(2,1)S(1)}, u32[]{:S(2)}) copy-start(bf16[512,768]{1,0:T(8,128)(2,1)S(1)} %slice.295) | copy-start | bytes 2359300
  190.3 286.0 %reduce-scatter.27.cloned.1.call-start = ((), (), s32[]{:S(2)}) async-start(), calls=%async_computation.19 | async-start | bytes 1474560 | tf_op jit(solution)/shard_map/reduce_scatter | solution.py:283
  311.9 10.5 slice-start.28
  313.1 9.3 copy-start.53
  313.1 9.3 copy-start.22
  313.1 9.3 copy-start.129
  313.1 9.3 copy-start.135
  313.1 9.3 copy-start.142
  313.1 9.3 slice-start.29
  313.1 9.3 slice-start.30
  329.8 148.3 %reduce-scatter.23.cloned.1.call-start = ((), (), s32[]{:S(2)}) async-start(), calls=%async_computation.17 | async-start | bytes 1474560 | tf_op jit(solution)/shard_map/reduce_scatter | solution.py:277
  333.1 7.2 copy-start.44
  344.7 135.3 %reduce-scatter.19.cloned.1.call-start = ((), (), s32[]{:S(2)}) async-start(), calls=%async_computation.15 | async-start | bytes 1474560 | tf_op jit(solution)/shard_map/reduce_scatter | solution.py:274
  356.4 7.3 copy-start.7
  358.8 123.0 %reduce-scatter.15.cloned.1.call-start = ((), (), s32[]{:S(2)}) async-start(), calls=%async_computation.13 | async-start | bytes 1474560 | tf_op jit(solution)/shard_map/reduce_scatter | solution.py:268
  378.2 105.5 %reduce-scatter.25.cloned.1.call-start = ((), (), s32[]{:S(2)}) async-start(), calls=%async_computation.18 | async-start | bytes 1474560 | tf_op jit(solution)/shard_map/reduce_scatter | solution.py:283
  380.1 9.2 copy-start.55
  380.1 9.2 copy-start.19
  380.1 9.2 copy-start.127
  380.1 9.2 copy-start.133
  380.1 9.2 copy-start.139
  389.3 7.8 copy-start.208
  400.4 98.9 %reduce-scatter.21.cloned.1.call-start = ((), (), s32[]{:S(2)}) async-start(), calls=%async_computation.16 | async-start | bytes 1474560 | tf_op jit(solution)/shard_map/reduce_scatter | solution.py:277
  414.4 113.9 %reduce-scatter.17.cloned.1.call-start = ((), (), s32[]{:S(2)}) async-start(), calls=%async_computation.14 | async-start | bytes 1474560 | tf_op jit(solution)/shard_map/reduce_scatter | solution.py:274
  426.7 7.3 copy-start.5
  429.2 128.2 %reduce-scatter.13.cloned.1.call-start = ((), (), s32[]{:S(2)}) async-start(), calls=%async_computation.12 | async-start | bytes 1474560 | tf_op jit(solution)/shard_map/reduce_scatter | solution.py:268
  440.2 167.4 %reduce-scatter.35.cloned.1.call-start = ((), (), s32[]{:S(2)}) async-start(), calls=%async_computation.23 | async-start | bytes 5898240 | tf_op jit(solution)/shard_map/reduce_scatter | solution.py:301
  448.0 210.7 %reduce-scatter.31.cloned.1.call-start = ((), (), s32[]{:S(2)}) async-start(), calls=%async_computation.21 | async-start | bytes 5898240 | tf_op jit(solution)/shard_map/reduce_scatter | solution.py:295
  457.5 252.1 %reduce-scatter.29.cloned.1.call-start = ((), (), s32[]{:S(2)}) async-start(), calls=%async_computation.20 | async-start | bytes 5898240 | tf_op jit(solution)/shard_map/reduce_scatter | solution.py:295
  466.7 293.4 %reduce-scatter.33.cloned.1.call-start = ((), (), s32[]{:S(2)}) async-start(), calls=%async_computation.22 | async-start | bytes 5898240 | tf_op jit(solution)/shard_map/reduce_scatter | solution.py:301
  476.0 741.9 %all-reduce.27.cloned.1.call-start = ((), (), s32[]{:S(2)}) async-start(), calls=%async_computation.25 | async-start | bytes 28311552 | tf_op jit(solution)/shard_map/psum | solution.py:314
  (192 other events, 453.6 us)
Sparse Core Ops, SparseCore 0:
  190.4 119.2 all-reduce.24
  329.9 26.6 reduce-scatter.26
  359.3 25.6 reduce-scatter.22
  388.1 25.7 reduce-scatter.18
  417.0 25.7 reduce-scatter.14
  445.2 25.7 reduce-scatter.24
  473.6 25.7 reduce-scatter.20
  502.5 25.7 reduce-scatter.16
  531.6 25.7 reduce-scatter.12
  559.7 47.8 reduce-scatter.34
  610.9 47.7 reduce-scatter.30
  661.7 47.8 reduce-scatter.28
  712.3 47.8 reduce-scatter.32
  768.1 449.7 all-reduce.26
where the time goes:
time: 1240 us
  waiting for transfers between devices  761 us (61%)
  matrix products  198 us (16%)
  blocking collectives  122 us (10%)
  other arithmetic  68.7 us (6%)
  local copies, waits for them, and re-layouts  68.2 us (6%)
  between operations  18.6 us (2%)
    psum x1, waiting for transfers between devices, reduce_layer(): lax.psum((shards[0], shards[1], shards[2], shards[3], shards[4], shards[5...  385 us
    unnamed x15, waiting for transfers between devices  116 us
    reduce_scatter x2, waiting for transfers between devices, reduce_layer(): lax.psum_scatter(gradients[9].astype(jnp.bfloat16), 'grp', scatter_dimens...  96.2 us
    reduce_scatter x2, waiting for transfers between devices, reduce_layer(): lax.psum_scatter(gradients[11].astype(jnp.bfloat16), 'grp', scatter_dimen...  96.1 us
    all_gather x1, blocking collectives, per_device(): lax.all_gather(passage_first, ('grp', 'rep'), axis=0, tiled=True)  71.1 us
    dot_general x13, matrix products, product(): return jnp.dot(former, latter, preferred_element_type=jnp.float32)  56.9 us
    dot_general x13, matrix products, contract_rows(): lax.dot_general(former, latter, (((0,), (0,)), ((), ())), preferred_eleme...  51.3 us
    dot_general x13, matrix products, contract_last(): lax.dot_general(former, latter, (((1,), (1,)), ((), ())), preferred_eleme...  45.9 us
  transfers between devices with their start and end apart: 14, of which 9 were waited for; matrix products, arithmetic and copies ran while one was open for 14% of the time, Pallas kernels for 0%

commit v1 on v0

--- a/solution.py
+++ b/solution.py
@@ -1,8 +1,11 @@
+import functools
 import math
 
 import jax
 import jax.numpy as jnp
 from jax import lax
+from jax.experimental import pallas as pl
+from jax.experimental.pallas import tpu as pltpu
 from jax.sharding import PartitionSpec as P
 
 HEADS = 12
@@ -209,17 +212,14 @@
         upstream, unit_two, scale_two, final_gain
     )
     delta_branch = narrow(delta_two)
-    delta_reduce_weight = contract_rows(active, delta_branch)
     delta_reduce_bias = column_total(delta_branch)
     delta_expanded = narrow(contract_last(delta_branch, reduce_weight) * gelu_slope(expanded))
-    delta_expand_weight = contract_rows(middle, delta_expanded)
     delta_expand_bias = column_total(delta_expanded)
     delta_middle = delta_two + contract_last(delta_expanded, expand_weight)
     delta_one, delta_norm_gain, delta_norm_shift = norm_backward(
         delta_middle, unit_one, scale_one, norm_gain
     )
     delta_mix = narrow(delta_one)
-    delta_mix_weight = contract_rows(context, delta_mix)
     delta_mix_bias = column_total(delta_mix)
     delta_context = narrow(contract_last(delta_mix, mix_weight))
     collected = ([], [], [])
@@ -243,95 +243,588 @@
         + contract_last(delta_key, key_weight)
         + contract_last(delta_value, value_weight)
     )
-    gradients = (
-        contract_rows(hidden, delta_query),
+    operands = (
+        active,
+        delta_branch,
+        middle,
+        delta_expanded,
+        hidden,
+        context,
+        delta_query,
+        delta_key,
+        delta_value,
+        delta_mix,
+    )
+    vectors = (
         column_total(delta_query),
-        contract_rows(hidden, delta_key),
-        contract_rows(hidden, delta_value),
         column_total(delta_value),
-        delta_mix_weight,
         delta_mix_bias,
         delta_norm_gain,
         delta_norm_shift,
-        delta_expand_weight,
         delta_expand_bias,
-        delta_reduce_weight,
         delta_reduce_bias,
         delta_final_gain,
         delta_final_shift,
     )
-    return (delta_hidden, gradients)
-
-
-def reduce_layer(gradients):
-    shards = (
-        lax.psum_scatter(
-            gradients[0].astype(jnp.bfloat16), "grp", scatter_dimension=0, tiled=True
-        ).astype(jnp.float32),
-        lax.psum_scatter(
-            gradients[1].astype(jnp.bfloat16), "grp", scatter_dimension=0, tiled=True
-        ).astype(jnp.float32),
-        lax.psum_scatter(
-            gradients[2].astype(jnp.bfloat16), "grp", scatter_dimension=0, tiled=True
-        ).astype(jnp.float32),
-        lax.psum_scatter(
-            gradients[3].astype(jnp.bfloat16), "grp", scatter_dimension=0, tiled=True
-        ).astype(jnp.float32),
-        lax.psum_scatter(
-            gradients[4].astype(jnp.bfloat16), "grp", scatter_dimension=0, tiled=True
-        ).astype(jnp.float32),
-        lax.psum_scatter(
-            gradients[5].astype(jnp.bfloat16), "grp", scatter_dimension=0, tiled=True
-        ).astype(jnp.float32),
-        lax.psum_scatter(
-            gradients[6].astype(jnp.bfloat16), "grp", scatter_dimension=0, tiled=True
-        ).astype(jnp.float32),
-        lax.psum_scatter(
-            gradients[7].astype(jnp.bfloat16), "grp", scatter_dimension=0, tiled=True
-        ).astype(jnp.float32),
-        lax.psum_scatter(
-            gradients[8].astype(jnp.bfloat16), "grp", scatter_dimension=0, tiled=True
-        ).astype(jnp.float32),
-        lax.psum_scatter(
-            gradients[9].astype(jnp.bfloat16), "grp", scatter_dimension=0, tiled=True
-        ).astype(jnp.float32),
-        lax.psum_scatter(
-            gradients[10].astype(jnp.bfloat16), "grp", scatter_dimension=0, tiled=True
-        ).astype(jnp.float32),
-        lax.psum_scatter(
-            gradients[11].astype(jnp.bfloat16), "grp", scatter_dimension=0, tiled=True
-        ).astype(jnp.float32),
-        lax.psum_scatter(
-            gradients[12].astype(jnp.bfloat16), "grp", scatter_dimension=0, tiled=True
-        ).astype(jnp.float32),
-        lax.psum_scatter(
-            gradients[13].astype(jnp.bfloat16), "grp", scatter_dimension=0, tiled=True
-        ).astype(jnp.float32),
-        lax.psum_scatter(
-            gradients[14].astype(jnp.bfloat16), "grp", scatter_dimension=0, tiled=True
-        ).astype(jnp.float32),
-    )
-    reduced = lax.psum(
-        (
-            shards[0],
-            shards[1],
-            shards[2],
-            shards[3],
-            shards[4],
-            shards[5],
-            shards[6],
-            shards[7],
-            shards[8],
-            shards[9],
-            shards[10],
-            shards[11],
-            shards[12],
-            shards[13],
-            shards[14],
+    return (delta_hidden, operands, vectors)
+
+
+CORE_FLIP = [(0, 1), (1, 0), (2, 3), (3, 2)]
+SIDE_FLIP = [(0, 2), (2, 0), (1, 3), (3, 1)]
+
+
+def wide(values):
+    return values.astype(jnp.float32)
+
+
+def pick(array, index):
+    return lax.dynamic_index_in_dim(array, index, 0, keepdims=False)
+
+
+def reduce_chunk(chunk):
+    rep_total = lax.axis_size("rep")
+    group = lax.axis_index("grp")
+    side, core = group // 2, group % 2
+    parts = chunk.reshape((2, 2) + chunk.shape[1:])
+    got = lax.ppermute(
+        lax.dynamic_index_in_dim(parts, 1 - core, 1, keepdims=False), "grp", CORE_FLIP
+    )
+    mine = lax.dynamic_index_in_dim(parts, core, 1, keepdims=False)
+    got = lax.ppermute(
+        narrow(wide(pick(mine, 1 - side)) + wide(pick(got, 1 - side))), "grp", SIDE_FLIP
+    ), narrow(wide(pick(mine, side)) + wide(pick(got, side)))
+    summed = narrow(wide(got[0]) + wide(got[1]))
+    rows, columns = summed.shape
+    if rep_total != 8:
+        part = lax.psum_scatter(summed, "rep", scatter_dimension=0, tiled=True)
+        return wide(lax.all_gather(part, "rep", axis=0, tiled=True))
+    rep = lax.axis_index("rep")
+    deep, near = rep // 2, rep % 2
+    flip = [(i, i ^ 1) for i in range(8)]
+    shifts = [[(i, (i + 2 * k) % 8) for i in range(8)] for k in range(4)]
+    halves = summed.reshape(2, rows // 2, columns)
+    got = lax.ppermute(pick(halves, 1 - near), "rep", flip)
+    half = narrow(wide(pick(halves, near)) + wide(got)).reshape(4, rows // 8, columns)
+    total = wide(pick(half, deep))
+    for k in range(1, 4):
+        total = total + wide(lax.ppermute(pick(half, (deep + k) % 4), "rep", shifts[k]))
+    piece = narrow(total)
+    pieces = [piece] + [lax.ppermute(piece, "rep", shifts[k]) for k in range(1, 4)]
+    joined = jnp.zeros((4,) + piece.shape, jnp.bfloat16)
+    for k in range(4):
+        joined = lax.dynamic_update_index_in_dim(joined, pieces[k], (deep - k) % 4, 0)
+    other = lax.ppermute(joined, "rep", flip)
+    own = joined.reshape(rows // 2, columns)
+    other = other.reshape(rows // 2, columns)
+    first = jnp.where(near == 0, own, other)
+    second = jnp.where(near == 0, other, own)
+    return wide(jnp.concatenate([first, second], axis=0))
+
+
+def reduce_small(small):
+    group = lax.axis_index("grp")
+    side, core = group // 2, group % 2
+    parts = small.reshape(2, 2, -1)
+    got = lax.ppermute(
+        lax.dynamic_index_in_dim(parts, 1 - core, 1, keepdims=False), "grp", CORE_FLIP
+    )
+    pair = lax.dynamic_index_in_dim(parts, core, 1, keepdims=False) + got
+    total = pick(pair, side) + lax.ppermute(pick(pair, 1 - side), "grp", SIDE_FLIP)
+    rep_total = lax.axis_size("rep")
+    step = 1
+    while step < rep_total:
+        total = total + lax.ppermute(total, "rep", [(i, i ^ step) for i in range(rep_total)])
+        step = step * 2
+    return total
+
+
+def remote(source, target, send_sem, recv_sem, grp, rep):
+    return pltpu.make_async_remote_copy(
+        src_ref=source,
+        dst_ref=target,
+        send_sem=send_sem,
+        recv_sem=recv_sem,
+        device_id=(grp, rep),
+        device_id_type=pl.DeviceIdType.MESH,
+    )
+
+
+def gather_kernel(block_ref, out_ref, send_near, recv_near, send_far, recv_far):
+    groups, reps = out_ref.shape[:2]
+    grp, rep = lax.axis_index("grp"), lax.axis_index("rep")
+    barrier = pltpu.get_barrier_semaphore()
+
+    @pl.loop(1, reps)
+    def _(k):
+        pl.semaphore_signal(
+            barrier, inc=1, device_id=(grp, (rep + k) % reps), device_id_type=pl.DeviceIdType.MESH
+        )
+
+    for k in range(1, groups):
+        pl.semaphore_signal(
+            barrier, inc=1, device_id=((grp + k) % groups, rep), device_id_type=pl.DeviceIdType.MESH
+        )
+    out_ref[grp, rep] = block_ref[...]
+    pl.semaphore_wait(barrier, reps + groups - 2)
+
+    def near(k):
+        mine = out_ref.at[grp, rep]
+        return remote(mine, mine, send_near.at[k], recv_near.at[k], grp, (rep + k) % reps)
+
+    def far(k):
+        row = out_ref.at[grp]
+        return remote(row, row, send_far.at[k], recv_far.at[k], (grp + k) % groups, rep)
+
+    @pl.loop(1, reps)
+    def _(k):
+        near(k).start()
+
+    @pl.loop(1, reps)
+    def _(k):
+        near(k).wait_recv()
+
+    for k in range(1, groups):
+        far(k).start()
+    for k in range(1, groups):
+        far(k).wait_recv()
+
+    @pl.loop(1, reps)
+    def _(k):
+        near(k).wait_send()
+
+    for k in range(1, groups):
+        far(k).wait_send()
+
+
+def gather_blocks(block):
+    groups, reps = lax.axis_size("grp"), lax.axis_size("rep")
+    return pl.pallas_call(
+        gather_kernel,
+        out_shape=jax.ShapeDtypeStruct((groups, reps) + block.shape, block.dtype),
+        in_specs=[pl.BlockSpec(memory_space=pltpu.VMEM)],
+        out_specs=pl.BlockSpec(memory_space=pltpu.VMEM),
+        scratch_shapes=[
+            pltpu.SemaphoreType.DMA((reps,)),
+            pltpu.SemaphoreType.DMA((reps,)),
+            pltpu.SemaphoreType.DMA((groups,)),
+            pltpu.SemaphoreType.DMA((groups,)),
+        ],
+        compiler_params=pltpu.CompilerParams(collective_id=1, has_side_effects=True),
+    )(block)
+
+
+CHUNKS = 12
+OPERANDS = 10
+
+
+def exchange_kernel(*refs):
+    operands = refs[: 2 * OPERANDS]
+    (
+        small_ref,
+        out_ref,
+        small_out,
+        big,
+        slim,
+        buf,
+        keep,
+        side_out,
+        core_in,
+        side_in,
+        near_in,
+        deep_in,
+        piece,
+        small_buf,
+        small_core,
+        small_side,
+        small_near,
+        small_deep,
+        load_sem,
+        core_sem,
+        side_sem,
+        near_sem,
+        deep_send,
+        deep_recv,
+        back_send,
+        back_recv,
+        local_sem,
+        last_sem,
+        small_sem,
+        small_send,
+        small_recv,
+    ) = refs[2 * OPERANDS :]
+    depth = deep_in.shape[1] + 1
+    width = keep.shape[2]
+    quarter = width // 4
+    rows = keep.shape[1]
+    half_rows = rows // 2
+    piece_rows = half_rows // depth
+    grp, rep = lax.axis_index("grp"), lax.axis_index("rep")
+    side, core = grp // 2, grp % 2
+    deep, near = rep // 2, rep % 2
+    sibling = (2 * side + (1 - core), rep)
+    across = (2 * (1 - side) + core, rep)
+    beside = (grp, 2 * deep + (1 - near))
+
+    def behind(k):
+        return (grp, 2 * ((deep + k) % depth) + near)
+
+    peers = [sibling, across, beside] + [behind(k) for k in range(1, depth)]
+    barrier = pltpu.get_barrier_semaphore()
+    for peer in peers:
+        pl.semaphore_signal(barrier, inc=1, device_id=peer, device_id_type=pl.DeviceIdType.MESH)
+
+    def loads(group):
+        slot = group % 2
+        layer = operands[OPERANDS * (group // 3) : OPERANDS * (group // 3 + 1)]
+        active, branch, middle, expanded, hidden, context, query, key, value, mix = layer
+        whole = pl.ds(0, 4 * width)
+        if group % 3 == 0:
+            pairs = [(active, big, whole), (branch, slim, pl.ds(0, width))]
+        elif group % 3 == 1:
+            pairs = [(expanded, big, whole), (middle, slim, pl.ds(0, width))]
+        else:
+            pairs = [
+                (array, big, pl.ds(place * width, width))
+                for place, array in enumerate((query, key, value, mix))
+            ]
+            pairs += [(hidden, slim, pl.ds(0, width)), (context, slim, pl.ds(width, width))]
+        return [
+            pltpu.make_async_copy(array, target.at[slot, :, columns], load_sem.at[slot, place])
+            for place, (array, target, columns) in enumerate(pairs)
+        ]
+
+    for copy in loads(0):
+        copy.start()
+    pl.semaphore_wait(barrier, len(peers))
+
+    def core_copy(t):
+        return remote(
+            buf.at[t % 2, :, 1 - core], core_in.at[t], core_sem.at[0, t], core_sem.at[1, t], *sibling
+        )
+
+    def side_copy(t):
+        return remote(
+            side_out.at[t % 3], side_in.at[t], side_sem.at[0, t], side_sem.at[1, t], *across
+        )
+
+    def near_copy(t):
+        far_half = keep.at[t, pl.ds(pl.multiple_of((1 - near) * half_rows, 16), half_rows)]
+        return remote(far_half, near_in.at[t], near_sem.at[0, t], near_sem.at[1, t], *beside)
+
+    def piece_of(position):
+        return pl.ds(pl.multiple_of(near * half_rows + position * piece_rows, 16), piece_rows)
+
+    def deep_copy(t, k):
+        return remote(
+            keep.at[t, piece_of((deep + k) % depth)],
+            deep_in.at[t, k - 1],
+            deep_send.at[k - 1, t],
+            deep_recv.at[k - 1, t],
+            *behind(k),
+        )
+
+    def back_copy(t, k):
+        return remote(
+            piece.at[t],
+            out_ref.at[t, piece_of(deep)],
+            back_send.at[k - 1, t],
+            back_recv.at[k - 1, t],
+            *behind(k),
+        )
+
+    def local_copy(t):
+        return pltpu.make_async_copy(piece.at[t], out_ref.at[t, piece_of(deep)], local_sem.at[t])
+
+    def last_copy(t):
+        half = out_ref.at[t, pl.ds(pl.multiple_of(near * half_rows, 16), half_rows)]
+        return remote(half, half, last_sem.at[0, t], last_sem.at[1, t], *beside)
+
+    def add_rows(target, first, second, total):
+        step = 48
+
+        @pl.loop(0, total // step)
+        def _(i):
+            at = pl.ds(pl.multiple_of(i * step, 16), step)
+            target(at, narrow(wide(first(at)) + wide(second(at))))
+
+    def make_terms(t):
+        group, part = t // 2, t % 2
+        slot = group % 2
+
+        @pl.when(part == 0)
+        def _():
+            for static in range(CHUNKS // 2):
+
+                @pl.when(group == static)
+                def _():
+                    for copy in loads(static):
+                        copy.wait()
+                    if static + 1 < CHUNKS // 2:
+                        for copy in loads(static + 1):
+                            copy.start()
+
+        tall = group % 3 == 0
+
+        @pl.when(tall)
+        def _():
+            @pl.loop(0, 4)
+            def _(i):
+                columns = pl.ds(pl.multiple_of(i * width + part * rows, 128), rows)
+                terms = contract_rows(big[slot, :, columns], slim[slot, :, pl.ds(0, width)])
+                buf[t % 2, i // 2, i % 2] = narrow(terms)
+
+        @pl.when(jnp.logical_not(tall))
+        def _():
+            @pl.loop(0, 4)
+            def _(i):
+                unit, half = i // 2, i % 2
+                mixing = jnp.where((group % 3 == 2) & (part == 1) & (unit == 1), width, 0)
+                rows_at = pl.ds(pl.multiple_of(mixing + half * (2 * quarter), 128), 2 * quarter)
+                columns = pl.ds(pl.multiple_of((2 * part + unit) * width, 128), width)
+                terms = narrow(contract_rows(slim[slot, :, rows_at], big[slot, :, columns]))
+                place = pl.ds(pl.multiple_of(unit * quarter, 16), quarter)
+                buf[t % 2, half, 0, place] = terms[:quarter]
+                buf[t % 2, half, 1, place] = terms[quarter:]
+
+        core_copy(t).start()
+
+    def after_core(t):
+        core_copy(t).wait()
+
+        def to_side(at, values):
+            side_out[t % 3, at] = values
+
+        add_rows(
+            to_side,
+            lambda at: buf[t % 2, 1 - side, core, at],
+            lambda at: core_in[t, 1 - side, at],
+            rows,
+        )
+        side_copy(t).start()
+
+        def to_keep(at, values):
+            keep[t, at] = values
+
+        add_rows(
+            to_keep,
+            lambda at: buf[t % 2, side, core, at],
+            lambda at: core_in[t, side, at],
+            rows,
+        )
+
+    def after_side(t):
+        side_copy(t).wait()
+        for half in (1 - near, near):
+
+            def shifted(at):
+                return pl.ds(pl.multiple_of(half * half_rows + at.start, 16), at.size)
+
+            def to_keep(at, values):
+                keep[t, shifted(at)] = values
+
+            add_rows(
+                to_keep,
+                lambda at: keep[t, shifted(at)],
+                lambda at: side_in[t, shifted(at)],
+                half_rows,
+            )
+            if half is not near:
+                near_copy(t).start()
+
+    def after_near(t):
+        near_copy(t).wait()
+
+        def shifted(at):
+            return pl.ds(pl.multiple_of(near * half_rows + at.start, 16), at.size)
+
+        def to_keep(at, values):
+            keep[t, shifted(at)] = values
+
+        add_rows(
+            to_keep, lambda at: keep[t, shifted(at)], lambda at: near_in[t, at], half_rows
+        )
+        for k in range(1, depth):
+            deep_copy(t, k).start()
+
+    def after_deep(t):
+        total = wide(keep[t, piece_of(deep)])
+        for k in range(1, depth):
+            deep_copy(t, k).wait_recv()
+        for k in range(1, depth):
+            total = total + wide(deep_in[t, k - 1])
+        piece[t] = narrow(total)
+        local_copy(t).start()
+        for k in range(1, depth):
+            back_copy(t, k).start()
+
+    def after_back(t):
+        local_copy(t).wait()
+        for k in range(1, depth):
+            back_copy(t, k).wait_recv()
+        last_copy(t).start()
+
+    def small_to_core():
+        return remote(
+            small_ref.at[:, 1 - core], small_core, small_sem.at[0], small_sem.at[1], *sibling
+        )
+
+    def small_to_side():
+        return remote(
+            small_buf.at[1 - side], small_side, small_sem.at[2], small_sem.at[3], *across
+        )
+
+    def small_to_near():
+        return remote(small_buf.at[side], small_near, small_sem.at[4], small_sem.at[5], *beside)
+
+    def small_to_deep(k):
+        own = small_deep.at[deep]
+        return remote(own, own, small_send.at[k - 1], small_recv.at[k - 1], *behind(k))
+
+    small_to_core().start()
+
+    @pl.loop(0, CHUNKS + 5)
+    def _(t):
+        @pl.when(t < CHUNKS)
+        def _():
+            make_terms(t)
+
+        for lag, stage in enumerate((after_core, after_side, after_near, after_deep, after_back)):
+
+            @pl.when((t > lag) & (t < CHUNKS + lag + 1))
+            def _():
+                stage(t - lag - 1)
+
+        @pl.when(t == 0)
+        def _():
+            small_to_core().wait()
+            for half in range(2):
+                small_buf[half] = small_ref[half, core] + small_core[half]
+            small_to_side().start()
+
+        @pl.when(t == 1)
+        def _():
+            small_to_side().wait()
+            small_buf[side] = small_buf[side] + small_side[...]
+            small_to_near().start()
+
+        @pl.when(t == 2)
+        def _():
+            small_to_near().wait()
+            small_deep[deep] = small_buf[side] + small_near[...]
+            for k in range(1, depth):
+                small_to_deep(k).start()
+
+        @pl.when(t == 3)
+        def _():
+            for k in range(1, depth):
+                small_to_deep(k).wait()
+            total = small_deep[0]
+            for k in range(1, depth):
+                total = total + small_deep[k]
+            small_out[...] = total
+
+    @pl.loop(0, CHUNKS)
+    def _(t):
+        for k in range(1, depth):
+            deep_copy(t, k).wait_send()
+            back_copy(t, k).wait_send()
+        last_copy(t).wait()
+
+
+def exchange(layers, small):
+    tokens, width = layers[0][1].shape
+    depth = lax.axis_size("rep") // 2
+    rows = width // 2
+    bf16, f32 = jnp.bfloat16, jnp.float32
+    dma = pltpu.SemaphoreType.DMA
+    piece_rows = rows // 2 // depth
+    small_shape = small.shape[2:]
+    return pl.pallas_call(
+        exchange_kernel,
+        out_shape=(
+            jax.ShapeDtypeStruct((CHUNKS, rows, width), bf16),
+            jax.ShapeDtypeStruct(small_shape, f32),
         ),
-        "rep",
-    )
-    return list(reduced)
+        in_specs=[pl.BlockSpec(memory_space=pl.ANY)] * (2 * OPERANDS)
+        + [pl.BlockSpec(memory_space=pltpu.VMEM)],
+        out_specs=(pl.BlockSpec(memory_space=pl.ANY), pl.BlockSpec(memory_space=pltpu.VMEM)),
+        scratch_shapes=[
+            pltpu.VMEM((2, tokens, 4 * width), bf16),
+            pltpu.VMEM((2, tokens, 2 * width), bf16),
+            pltpu.VMEM((2, 2, 2, rows, width), bf16),
+            pltpu.VMEM((CHUNKS, rows, width), bf16),
+            pltpu.VMEM((3, rows, width), bf16),
+            pltpu.VMEM((CHUNKS, 2, rows, width), bf16),
+            pltpu.VMEM((CHUNKS, rows, width), bf16),
+            pltpu.VMEM((CHUNKS, rows // 2, width), bf16),
+            pltpu.VMEM((CHUNKS, depth - 1, piece_rows, width), bf16),
+            pltpu.VMEM((CHUNKS, piece_rows, width), bf16),
+            pltpu.VMEM((2,) + small_shape, f32),
+            pltpu.VMEM((2,) + small_shape, f32),
+            pltpu.VMEM(small_shape, f32),
+            pltpu.VMEM(small_shape, f32),
+            pltpu.VMEM((depth,) + small_shape, f32),
+            dma((2, 6)),
+            dma((2, CHUNKS)),
+            dma((2, CHUNKS)),
+            dma((2, CHUNKS)),
+            dma((depth - 1, CHUNKS)),
+            dma((depth - 1, CHUNKS)),
+            dma((depth - 1, CHUNKS)),
+            dma((depth - 1, CHUNKS)),
+            dma((CHUNKS,)),
+            dma((2, CHUNKS)),
+            dma((6,)),
+            dma((depth - 1,)),
+            dma((depth - 1,)),
+        ],
+        compiler_params=pltpu.CompilerParams(
+            collective_id=0, has_side_effects=True, vmem_limit_bytes=60 * 1024 * 1024
+        ),
+    )(*layers[0], *layers[1], small)
+
+
+def reduce_plain(layers):
+    results = []
+    for active, branch, middle, expanded, hidden, context, query, key, value, mix in layers:
+        quarter = lambda former, latter: (
+            lambda matrix: narrow(matrix).reshape(4, matrix.shape[0] // 4, matrix.shape[1])
+        )(contract_rows(former, latter))
+        square = jnp.concatenate(
+            [
+                quarter(hidden, query),
+                quarter(hidden, key),
+                quarter(hidden, value),
+                quarter(context, mix),
+            ],
+            axis=1,
+        )
+        square = reduce_chunk(square)
+        height = square.shape[0] // 4
+        results.append(
+            [square[place * height : (place + 1) * height] for place in range(4)]
+            + [reduce_chunk(quarter(middle, expanded)), reduce_chunk(quarter(active, branch))]
+        )
+    return [jnp.stack([results[1][i], results[0][i]]) for i in range(6)]
+
+
+def reduce_matrices(layers, small):
+    if lax.axis_size("rep") != 8:
+        return reduce_plain(layers), reduce_small(small)
+    size = small.shape[1]
+    small_rows = -(-size // 1024) * 8
+    padded = jnp.pad(small, ((0, 0), (0, small_rows * 128 - size)))
+    out, small_sum = exchange(layers, padded.reshape(2, 2, small_rows, 128))
+    width = out.shape[2]
+    out = wide(out).reshape(2, 12, width // 4, width)[::-1]
+    reduce_part = out[:, 0:4].reshape(2, width, width)
+    expand_part = jnp.swapaxes(out[:, 4:8], 1, 2).reshape(2, width // 4, 4 * width)
+    square = [out[:, 8 + place] for place in range(4)]
+    return square + [expand_part, reduce_part], small_sum.reshape(-1)[:size]
+
+
+SMALL = (1, 4, 6, 7, 8, 10, 12, 13, 14)
+MATRICES = (0, 2, 3, 5, 9, 11)
 
 
 def per_device(
@@ -401,31 +894,41 @@
     passage_output = hidden[query_span:].reshape(batch_size, passage_len, model_width)
     query_first = query_output[:, 0, :]
     passage_first = passage_output[:, 0, :]
-    every_passage = lax.all_gather(passage_first, ("grp", "rep"), axis=0, tiled=True)
+    facts = jnp.concatenate(
+        [margin_bin, positive_index // 128, positive_index % 128], axis=0
+    ).astype(jnp.bfloat16)
+    facts = jnp.pad(facts, (0, model_width - facts.shape[0]))
+    block = jnp.concatenate([query_first, passage_first, facts[None, :]], axis=0)
+    block = jnp.pad(block, ((0, 8 - block.shape[0]), (0, 0)))
+    total = cluster_index.shape[0]
+    every = gather_blocks(block).reshape(-1, 8, model_width)
+    every_query = every[:, :batch_size].reshape(total, model_width)
+    every_passage = every[:, batch_size : 2 * batch_size].reshape(total, model_width)
+    facts = every[:, 2 * batch_size, : 3 * batch_size].astype(jnp.int32)
+    facts = facts.reshape(-1, 3, batch_size)
+    every_margin = facts[:, 0].reshape(total)
+    every_positive = (facts[:, 1] * 128 + facts[:, 2]).reshape(total)
     start_row = lax.axis_index(("grp", "rep")) * batch_size
-    own_cluster = lax.dynamic_slice_in_dim(cluster_index, start_row, batch_size)
     score_scale = 2.0 / math.sqrt(model_width)
-    logits = contract_last(query_first, every_passage) * score_scale
+    logits = contract_last(every_query, every_passage) * score_scale
     columns = lax.broadcasted_iota(jnp.int32, logits.shape, 1)
-    chosen_mask = columns == positive_index[:, None]
-    allowed = (cluster_index[None, :] == own_cluster[:, None]) | chosen_mask
+    chosen_mask = columns == every_positive[:, None]
+    allowed = (cluster_index[None, :] == cluster_index[:, None]) | chosen_mask
     masked = jnp.where(allowed, logits, -1e30)
     peak_score = jnp.max(masked, axis=1, keepdims=True)
     normalizer = peak_score + jnp.log(jnp.sum(jnp.exp(masked - peak_score), axis=1, keepdims=True))
     chosen = jnp.sum(jnp.where(chosen_mask, logits, 0.0), axis=1)
-    margin_weight = (margin_bin + 1).astype(jnp.float32) / NBINS
-    query_loss = margin_weight * (normalizer[:, 0] - chosen)
+    margin_weight = (every_margin + 1).astype(jnp.float32) / NBINS
+    every_loss = margin_weight * (normalizer[:, 0] - chosen)
+    query_loss = lax.dynamic_slice_in_dim(every_loss, start_row, batch_size)
     delta_logits = narrow(
         margin_weight[:, None]
         * (jnp.where(allowed, jnp.exp(masked - normalizer), 0.0) - chosen_mask.astype(jnp.float32))
     )
-    delta_query_first = product(delta_logits, every_passage) * score_scale
-    delta_passage_first = lax.psum_scatter(
-        contract_rows(delta_logits, query_first) * score_scale,
-        ("grp", "rep"),
-        scatter_dimension=0,
-        tiled=True,
-    )
+    own_rows = lax.dynamic_slice_in_dim(delta_logits, start_row, batch_size, axis=0)
+    own_columns = lax.dynamic_slice_in_dim(delta_logits, start_row, batch_size, axis=1)
+    delta_query_first = product(own_rows, every_passage) * score_scale
+    delta_passage_first = contract_rows(own_columns, every_query) * score_scale
     query_upstream = query_cotangent.astype(jnp.float32).at[:, 0, :].add(delta_query_first)
     passage_upstream = passage_cotangent.astype(jnp.float32).at[:, 0, :].add(delta_passage_first)
     upstream = jnp.concatenate(
@@ -435,18 +938,26 @@
         ],
         axis=0,
     )
-    per_layer = []
+    operands = []
+    small = []
     for layer_index in reversed(range(LAYERS)):
         layer_params = tuple((array[layer_index] for array in params))
-        upstream, layer_grads = layer_backward(
+        upstream, layer_operands, vectors = layer_backward(
             upstream, stored_layers[layer_index], keep_masks, layout, layer_params
         )
-        per_layer.append(reduce_layer(layer_grads))
-    per_layer = per_layer[::-1]
-    reduced = [
-        jnp.stack([per_layer[layer_index][slot] for layer_index in range(LAYERS)])
-        for slot in range(15)
-    ]
+        operands.append(layer_operands)
+        small.append([vector.reshape(4, -1) for vector in vectors])
+    small = small[::-1]
+    matrices, flat = reduce_matrices(operands, jnp.concatenate(small[0] + small[1], axis=1))
+    reduced = [None] * 15
+    for slot, matrix in zip(MATRICES, matrices):
+        reduced[slot] = matrix
+    flat = flat.reshape(LAYERS, -1)
+    offset = 0
+    for slot, vector in zip(SMALL, small[0]):
+        size = vector.shape[1]
+        reduced[slot] = flat[:, offset : offset + size]
+        offset = offset + size
     query_input_gradient = upstream[:query_span].reshape(batch_size, query_len, model_width)
     passage_input_gradient = upstream[query_span:].reshape(batch_size, passage_len, model_width)
     return (

time: 1240 us -> 587 us (0.47)
  waiting for transfers between devices: 761 us -> 0 us
  Pallas kernels: 0 us -> 224 us
  blocking collectives: 122 us -> 0 us
  local copies, waits for them, and re-layouts: 68.2 us -> 117 us
  matrix products: 198 us -> 159 us
  between operations: 18.6 us -> 3.27 us
    psum x1 -> x0, waiting for transfers between devices: 385 us -> none  [reduce_layer(): lax.psum((shards[0], shards[1], shards[2], shards[3], shards[4], shards[5...]
    reduce_scatter x12 -> x0, waiting for transfers between devices: 260 us -> none  [the longest x2 96.2 us: reduce_layer(): lax.psum_scatter(gradients[9].astype(jnp.bfloat16), 'grp', scatter_dimens...]
    pallas_call x0 -> x2, Pallas kernels: none -> 224 us  [the longest x1 209 us: exchange(): pl.pallas_call(exchange_kernel, out_shape=(jax.ShapeDtypeStruct((CHUNKS,...]
    unnamed x15 -> x0, waiting for transfers between devices: 116 us -> none
    all_gather x1 -> x0, blocking collectives: 71.1 us -> none  [per_device(): lax.all_gather(passage_first, ('grp', 'rep'), axis=0, tiled=True)]
    dot_general x13 -> x1, matrix products: 51.3 us -> 1.63 us  [contract_rows(): lax.dot_general(former, latter, (((0,), (0,)), ((), ())), preferred_eleme...]
    another operation x27 -> x2, other arithmetic: 42.6 us -> 1.33 us  [per_device(): jnp.stack([per_layer[layer_index][slot] for layer_index in range(LAYERS)])]
    psum x1 -> x0, blocking collectives: 39.7 us -> none  [reduce_layer(): lax.psum((shards[0], shards[1], shards[2], shards[3], shards[4], shards[5...]
  transfers between devices with their start and end apart: 14 -> 0, of which waited for: 9 -> 0; matrix products, arithmetic and copies ran while one was open for 14% -> 0% of each run, Pallas kernels for 0% -> 0%
where the time goes in v1:
time: 587 us; the launch traced here: 577 us
  Pallas kernels  224 us (38%)
  matrix products  159 us (27%)
  local copies, waits for them, and re-layouts  117 us (20%)
  other arithmetic  73.7 us (13%)
    pallas_call x1, Pallas kernels, exchange(): pl.pallas_call(exchange_kernel, out_shape=(jax.ShapeDtypeStruct((CHUNKS,...  209 us
    dot_general x13, matrix products, product(): return jnp.dot(former, latter, preferred_element_type=jnp.float32)  66.8 us
    dot_general x13, matrix products, contract_last(): lax.dot_general(former, latter, (((1,), (1,)), ((), ())), preferred_eleme...  55.7 us
    unnamed x247, local copies, waits for them, and re-layouts  23.7 us
    convert_element_type x28, local copies, waits for them, and re-layouts, narrow(): return values.astype(jnp.bfloat16)  18.6 us
    reshape x17, local copies, waits for them, and re-layouts, per_device(): small.append([vector.reshape(4, -1) for vector in vectors])  16.8 us
    pallas_call x1, Pallas kernels, gather_blocks(): pl.pallas_call(gather_kernel, out_shape=jax.ShapeDtypeStruct((groups, rep...  15.3 us
    reduce_sum x8, other arithmetic, column_total(): return jnp.sum(values.astype(jnp.float32), axis=0)  13.6 us

profile of v1, /device:TPU:0, one launch (start us, length us, event | category | flops | bytes accessed | tf_op | source)
XLA Modules:
  0.0 577.2 jit_solution(12891447248442012367)
XLA Ops:
  13.2 1.7 copy_convert_fusion.1
  14.8 2.4 add_convert_fusion.7
  18.2 2.5 add_convert_fusion.6
  22.2 2.2 convolution_convert_fusion.3
  27.8 3.1 copy_convert_fusion
  30.9 1.8 fusion.32
  35.2 1.5 fusion.72
  38.1 2.2 fusion.211
  43.2 21.2 %fusion.2 = (bf16[576,3072]{1,0:T(8,128)(2,1)S(1)}, f32[576,3072]{1,0:T(8,128)}) fusion(f32[3072]{0:T(1024)S(1)} %bitcast.318, bf16[576,768]{1,0:T(8,128)(2,1)S(1)} %add_convert_fusion.5.refs_12_, bf16[2,768,3072]{2,1,0:T(8,128)(2,1)} %param.46), kind=kOutput, calls=%fused_computation.6 | convolution fusion | flops 2834694144 | bytes 16232448 | tf_op jit(solution)/shard_map/dot_general | solution.py:22
  64.5 3.0 fusion.212
  68.3 1.6 copy-done.99
  71.5 2.3 add_convert_fusion.3
  77.0 2.2 convolution_convert_fusion.2
  81.5 1.7 fusion.33
  85.9 1.5 fusion.73
  89.8 2.2 fusion.214
  93.0 20.9 %fusion.5 = (bf16[576,3072]{1,0:T(8,128)(2,1)S(1)}, f32[576,3072]{1,0:T(8,128)}) fusion(f32[3072]{0:T(1024)S(1)} %bitcast.320, bf16[576,768]{1,0:T(8,128)(2,1)S(1)} %add_convert_fusion.1.refs_2_, bf16[2,768,3072]{2,1,0:T(8,128)(2,1)} %param.46), kind=kOutput, calls=%fused_computation.9 | convolution fusion | flops 2834694144 | bytes 16232448 | tf_op jit(solution)/shard_map/dot_general | solution.py:22
  114.0 3.0 fusion.215
  119.4 15.3 %shard_map.383 = bf16[4,8,8,768]{3,2,1,0:T(8,128)(2,1)} custom-call(bf16[8,768]{1,0:T(8,128)(2,1)} %fusion.188.block_ref), custom_call_target="tpu_custom_call" | custom-call | tf_op jit(solution)/shard_map/pallas_call | solution.py:401
  134.8 1.5 slice.411
  136.2 1.9 fusion.208
  139.5 1.6 reshape.519
  151.5 1.6 reshape.518
  156.6 1.6 fusion.112
  158.2 1.7 fusion.115
  160.5 1.6 reduce_sum.450
  162.1 1.6 copy.149
  163.8 2.5 reduce_sum.451
  168.9 1.6 copy.151
  171.7 1.4 multiply_reduce_fusion.2
  175.8 3.9 convert_reduce_fusion.2
  179.8 9.9 %convert_reduce_fusion = (f32[3072]{0:T(1024)}, bf16[576,3072]{1,0:T(8,128)(2,1)}) fusion(f32[576,3072]{1,0:T(8,128)} %get-tuple-element.132, f32[3072]{0:T(1024)S(1)} %bitcast.321, bf16[576,768]{1,0:T(8,128)(2,1)S(1)} %get-tuple-element.82.refs_1_, bf16[2,3072,768]{2,1,0:T(8,128)(2,1)} %param.48), kind=kOutput, calls=%fused_computation.22 | convolution fusion | flops 2740909056 | bytes 16244736 | tf_op jit(solution)/shard_map/dot_general | solution.py:32
  192.4 8.5 %multiply_reduce_fusion.3 = (f32[768]{0:T(1024)}, f32[576]{0:T(1024)}, f32[576]{0:T(1024)}, f32[768]{0:T(1024)}, f32[576,768]{1,0:T(8,128)}) fusion(f32[576,768]{1,0:T(8,128)S(1)} %get-tuple-element.130, f32[576]{0:T(1024)} %copy-done.89, f32[576]{0:T(1024)} %copy-done.80, f32[768]{0:T(1024)} %get-tuple-element.153, f32[576,768]{1,0:T(8,128)S(1)} %copy-done.37, ...), kind=kOutput, calls=%fused_computation.94 | convolution fusion | flops 2722330112 | bytes 13588992 | tf_op jit(solution)/shard_map/dot_general | solution.py:32
  203.6 3.4 convert_reduce_fusion.3
  208.4 2.2 convolution_convert_fusion.1
  214.2 4.3 fusion.74
  221.6 4.9 multiply_reduce_fusion.1
  226.5 2.1 multiply_convert_fusion.1
  238.8 2.3 fusion.80
  244.4 2.6 multiply_reduce_fusion.4
  247.6 2.7 convert_reduce_fusion.6
  250.3 10.1 %convert_reduce_fusion.1 = (f32[3072]{0:T(1024)}, bf16[576,3072]{1,0:T(8,128)(2,1)}) fusion(f32[576,3072]{1,0:T(8,128)} %get-tuple-element.122, f32[3072]{0:T(1024)S(1)} %bitcast.319, bf16[576,768]{1,0:T(8,128)(2,1)S(1)} %get-tuple-element.88.refs_11_, bf16[2,3072,768]{2,1,0:T(8,128)(2,1)} %param.48), kind=kOutput, calls=%fused_computation.23 | convolution fusion | flops 2740909056 | bytes 16244736 | tf_op jit(solution)/shard_map/dot_general | solution.py:32
  263.8 8.5 %multiply_reduce_fusion.5 = (f32[768]{0:T(1024)}, f32[576]{0:T(1024)}, f32[576]{0:T(1024)S(1)}, f32[768]{0:T(1024)}, f32[576,768]{1,0:T(8,128)}) fusion(f32[576,768]{1,0:T(8,128)S(1)} %copy-done.5, f32[576]{0:T(1024)S(1)} %copy-done.88, f32[576]{0:T(1024)S(1)} %copy-done.77, f32[768]{0:T(1024)S(1)} %copy-done.85, f32[576,768]{1,0:T(8,128)S(1)} %get-tuple-element.89, ...), kind=kOutput, calls=%fused_computation.100 | convolution fusion | flops 2722330112 | bytes 13584384 | tf_op jit(solution)/shard_map/dot_general | solution.py:32
  274.4 3.0 convert_reduce_fusion.7
  279.3 2.4 convolution_convert_fusion
  283.6 2.2 reshape.527
  291.9 4.3 fusion.75
  299.3 5.4 multiply_reduce_fusion
  304.8 2.2 multiply_convert_fusion
  307.0 2.0 fusion.71
  312.9 1.9 copy.192
  315.9 2.3 copy.193
  319.0 1.5 concatenate.56
  322.1 2.1 pad_maximum_fusion.8.refs_17_
  324.2 3.7 fusion.90
  328.9 209.1 %shard_map.384 = (bf16[12,384,768]{2,1,0:T(8,128)(2,1)}, f32[40,128]{1,0:T(8,128)}) custom-call(bf16[576,3072]{1,0:T(8,128)(2,1)} %copy-done.21, bf16[576,768]{1,0:T(8,128)(2,1)} %copy-done.22, bf16[576,768]{1,0:T(8,128)(2,1)} %copy-done.28, bf16[576,3072]{1,0:T(8,128)(2,1)} %get-tuple-element.151.refs_3_, bf16[576,768]{1,0:T(8,128)(2,1)} %copy-done.26, ...), custom_call_target="tpu_custom_call" | custom-call | tf_op jit(solution)/shard_map/pallas_call | solution.py:742
  540.7 1.6 fusion.209
  542.3 2.3 fusion.93
  547.6 4.8 fusion.207
  552.4 4.8 slice.391
  557.2 2.8 reverse_bitcast_fusion
  560.0 2.9 copy.224
  562.9 6.8 %convert.32 = f32[2,12,192,768]{3,2,1,0:T(8,128)} convert(bf16[2,12,192,768]{3,2,1,0:T(8,128)(2,1)S(1)} %bitcast.275) | non-fusion elementwise | flops 3538944 | bytes 21233664 | tf_op jit(solution)/shard_map/reshape | solution.py:819
  569.7 2.6 slice_bitcast_fusion
  (440 shorter events, 126.7 us)
Async XLA Ops:
  3.3 81.5 %copy-start.62 = (pred[2,256]{1,0:T(4,128)(4,1)}, pred[2,256]{1,0:T(4,128)(4,1)S(1)}, u32[]{:S(2)}) copy-start(pred[2,256]{1,0:T(4,128)(4,1)S(1)} %iota_compare_fusion.3) | copy-start | bytes 1540
  10.3 30.3 %copy-start.84 = (f32[768]{0:T(1024)}, f32[768]{0:T(1024)S(1)}, u32[]{:S(2)}) copy-start(f32[768]{0:T(1024)S(1)} %get-tuple-element.152) | copy-start | bytes 9220
  11.7 56.2 %copy-start.72 = (f32[768]{0:T(1024)}, f32[768]{0:T(1024)S(1)}, u32[]{:S(2)}) copy-start(f32[768]{0:T(1024)S(1)} %get-tuple-element.154) | copy-start | bytes 9220
  13.1 30.1 %copy-start.92 = (f32[1,3072]{1,0:T(1,128)}, f32[1,3072]{1,0:T(1,128)S(1)}, u32[]{:S(2)}) copy-start(f32[1,3072]{1,0:T(1,128)S(1)} %get-tuple-element.112) | copy-start | bytes 36868
  17.8 16.3 %copy-start.29 = (bf16[2,256,12,64]{1,0,3,2:T(2,128)(2,1)}, bf16[2,256,12,64]{1,0,3,2:T(2,128)(2,1)S(1)}, u32[]{:S(2)}) copy-start(bf16[2,256,12,64]{1,0,3,2:T(2,128)(2,1)S(1)} %reshape.503) | copy-start | bytes 2359300
  18.2 8.5 %copy-start.39 = (bf16[2,32,12,64]{3,2,1,0:T(8,128)(2,1)}, bf16[2,32,12,64]{3,2,1,0:T(8,128)(2,1)S(1)}, u32[]{:S(2)}) copy-start(bf16[2,32,12,64]{3,2,1,0:T(8,128)(2,1)S(1)} %reshape.499) | copy-start | bytes 294916
  21.2 9.7 %copy-start.11 = (bf16[2,256,12,64]{1,0,3,2:T(2,128)(2,1)}, bf16[2,256,12,64]{1,0,3,2:T(2,128)(2,1)S(1)}, u32[]{:S(2)}) copy-start(bf16[2,256,12,64]{1,0,3,2:T(2,128)(2,1)S(1)} %reshape.504) | copy-start | bytes 2359300
  24.9 6.0 %copy-start.13 = (bf16[2,256,12,64]{1,0,3,2:T(2,128)(2,1)}, bf16[2,256,12,64]{1,0,3,2:T(2,128)(2,1)S(1)}, u32[]{:S(2)}) copy-start(bf16[2,256,12,64]{1,0,3,2:T(2,128)(2,1)S(1)} %reshape.505) | copy-start | bytes 2359300
  27.3 5.4 copy-start.54
  40.3 2.9 copy-start.76
  41.5 22.9 %slice-start.8 = ((s8[9437184]{0:T(1024)(128)(4,1)}), s8[4194304]{0:T(1024)(128)(4,1)S(1)}, s32[]{:S(2)}) async-start(s8[9437184]{0:T(1024)(128)(4,1)} %bitcast.324), calls=%async_computation.8 | async-start | bytes 8388608
  41.9 22.6 %copy-start.25 = (bf16[576,768]{1,0:T(8,128)(2,1)}, bf16[576,768]{1,0:T(8,128)(2,1)S(1)}, u32[]{:S(2)}) copy-start(bf16[576,768]{1,0:T(8,128)(2,1)S(1)} %add_convert_fusion.5.refs_12_) | copy-start | bytes 2654212
  43.2 21.3 %slice-start.9 = ((s8[9437184]{0:T(1024)(128)(4,1)}), s8[4194304]{0:T(1024)(128)(4,1)S(1)}, s32[]{:S(2)}) async-start(s8[9437184]{0:T(1024)(128)(4,1)} %bitcast.324), calls=%async_computation.9 | async-start | bytes 8388608
  43.2 21.3 %slice-start.10 = ((s8[9437184]{0:T(1024)(128)(4,1)}), s8[1048576]{0:T(1024)(128)(4,1)S(1)}, s32[]{:S(2)}) async-start(s8[9437184]{0:T(1024)(128)(4,1)} %bitcast.324), calls=%async_computation.10 | async-start | bytes 2097152
  64.4 3.1 copy-start.20
  67.5 3.2 copy-start.2
  67.6 3.2 copy-start.66
  69.9 7.1 %copy-start.26 = (bf16[576,768]{1,0:T(8,128)(2,1)}, bf16[576,768]{1,0:T(8,128)(2,1)S(1)}, u32[]{:S(2)}) copy-start(bf16[576,768]{1,0:T(8,128)(2,1)S(1)} %add_convert_fusion.4.refs_4_) | copy-start | bytes 2654212
  71.3 10.2 %copy-start.15 = (bf16[2,256,12,64]{1,0,3,2:T(2,128)(2,1)}, bf16[2,256,12,64]{1,0,3,2:T(2,128)(2,1)S(1)}, u32[]{:S(2)}) copy-start(bf16[2,256,12,64]{1,0,3,2:T(2,128)(2,1)S(1)} %reshape.512) | copy-start | bytes 2359300
  71.5 8.5 %copy-start.46 = (bf16[2,32,12,64]{3,2,1,0:T(8,128)(2,1)}, bf16[2,32,12,64]{3,2,1,0:T(8,128)(2,1)S(1)}, u32[]{:S(2)}) copy-start(bf16[2,32,12,64]{3,2,1,0:T(8,128)(2,1)S(1)} %reshape.508) | copy-start | bytes 294916
  77.0 3.4 copy-start.41
  79.8 3.5 copy-start.17
  80.0 3.3 copy-start.48
  81.5 7.2 %copy-start.57 = (bf16[64,768]{1,0:T(8,128)(2,1)}, bf16[64,768]{1,0:T(8,128)(2,1)S(1)}, u32[]{:S(2)}) copy-start(bf16[64,768]{1,0:T(8,128)(2,1)S(1)} %reshape.510) | copy-start | bytes 294916
  89.8 2.9 copy-start.91
  92.0 21.9 %slice-start.11 = ((s8[9437184]{0:T(1024)(128)(4,1)}), s8[4194304]{0:T(1024)(128)(4,1)S(1)}, s32[]{:S(2)}) async-start(s8[9437184]{0:T(1024)(128)(4,1)} %bitcast.326), calls=%async_computation.11 | async-start | bytes 8388608
  92.6 21.3 %copy-start.89 = (f32[576]{0:T(1024)}, f32[576]{0:T(1024)S(1)}, u32[]{:S(2)}) copy-start(f32[576]{0:T(1024)S(1)} %add_rsqrt_fusion.1) | copy-start | bytes 6916
  93.0 20.9 %copy-start.28 = (bf16[576,768]{1,0:T(8,128)(2,1)}, bf16[576,768]{1,0:T(8,128)(2,1)S(1)}, u32[]{:S(2)}) copy-start(bf16[576,768]{1,0:T(8,128)(2,1)S(1)} %add_convert_fusion.1.refs_2_) | copy-start | bytes 2654212
  93.0 21.0 %copy-start.97 = (f32[768]{0:T(1024)S(1)}, f32[768]{0:T(1024)}, u32[]{:S(2)}) copy-start(f32[768]{0:T(1024)} %get-tuple-element.69) | copy-start | bytes 9220
  93.0 21.0 %slice-start.12 = ((s8[9437184]{0:T(1024)(128)(4,1)}), s8[4194304]{0:T(1024)(128)(4,1)S(1)}, s32[]{:S(2)}) async-start(s8[9437184]{0:T(1024)(128)(4,1)} %bitcast.326), calls=%async_computation.12 | async-start | bytes 8388608
  93.0 20.9 %slice-start.13 = ((s8[9437184]{0:T(1024)(128)(4,1)}), s8[1048576]{0:T(1024)(128)(4,1)S(1)}, s32[]{:S(2)}) async-start(s8[9437184]{0:T(1024)(128)(4,1)} %bitcast.326), calls=%async_computation.13 | async-start | bytes 2097152
  113.9 3.1 copy-start.21
  114.0 3.4 copy-start.74
  114.0 3.4 copy-start.90
  175.8 3.9 copy-start.95
  179.7 9.9 %copy-start.22 = (bf16[576,768]{1,0:T(8,128)(2,1)}, bf16[576,768]{1,0:T(8,128)(2,1)S(1)}, u32[]{:S(2)}) copy-start(bf16[576,768]{1,0:T(8,128)(2,1)S(1)} %get-tuple-element.82.refs_1_) | copy-start | bytes 2654212
  179.8 12.6 %copy-start.37 = (f32[576,768]{1,0:T(8,128)S(1)}, f32[576,768]{1,0:T(8,128)}, u32[]{:S(2)}) copy-start(f32[576,768]{1,0:T(8,128)} %get-tuple-element.83) | copy-start | bytes 5308420
  203.6 4.1 copy-start.98
  207.0 3.6 copy-start.23
  220.7 5.8 %slice-start.2 = ((s8[6291456]{0:T(1024)(128)(4,1)}), s8[4194304]{0:T(1024)(128)(4,1)S(1)}, s32[]{:S(2)}) async-start(s8[6291456]{0:T(1024)(128)(4,1)} %bitcast.268), calls=%async_computation.2 | async-start | bytes 8388608
  221.6 4.9 slice-start.3
  234.5 3.3 copy-start.56
  238.8 3.3 copy-start.100
  250.3 10.2 %copy-start.24 = (bf16[576,768]{1,0:T(8,128)(2,1)}, bf16[576,768]{1,0:T(8,128)(2,1)S(1)}, u32[]{:S(2)}) copy-start(bf16[576,768]{1,0:T(8,128)(2,1)S(1)} %get-tuple-element.88.refs_11_) | copy-start | bytes 2654212
  250.3 13.5 %copy-start.5 = (f32[576,768]{1,0:T(8,128)S(1)}, f32[576,768]{1,0:T(8,128)}, u32[]{:S(2)}) copy-start(f32[576,768]{1,0:T(8,128)} %copy-done.4) | copy-start | bytes 5308420
  250.3 13.5 %copy-start.77 = (f32[576]{0:T(1024)S(1)}, f32[576]{0:T(1024)}, u32[]{:S(2)}) copy-start(f32[576]{0:T(1024)} %copy-done.76) | copy-start | bytes 6916
  250.3 13.5 %copy-start.85 = (f32[768]{0:T(1024)S(1)}, f32[768]{0:T(1024)}, u32[]{:S(2)}) copy-start(f32[768]{0:T(1024)} %copy-done.84) | copy-start | bytes 9220
  250.3 13.5 %copy-start.88 = (f32[576]{0:T(1024)S(1)}, f32[576]{0:T(1024)}, u32[]{:S(2)}) copy-start(f32[576]{0:T(1024)} %copy-done.87) | copy-start | bytes 6916
  282.4 4.7 copy-start.8
  282.4 4.7 copy-start.40
  282.4 4.7 copy-start.55
  285.9 6.0 %copy-start.33 = (bf16[2,256,12,64]{1,0,3,2:T(2,128)(2,1)}, bf16[2,256,12,64]{1,0,3,2:T(2,128)(2,1)S(1)}, u32[]{:S(2)}) copy-start(bf16[2,256,12,64]{1,0,3,2:T(2,128)(2,1)S(1)} %reshape.527) | copy-start | bytes 2359300
  288.3 3.4 copy-start.53
  288.3 3.6 copy-start.64
  298.4 6.4 %slice-start = ((s8[6291456]{0:T(1024)(128)(4,1)}), s8[4194304]{0:T(1024)(128)(4,1)S(1)}, s32[]{:S(2)}) async-start(s8[6291456]{0:T(1024)(128)(4,1)} %bitcast.266), calls=%async_computation | async-start | bytes 8388608
  299.3 5.4 slice-start.1
  299.3 5.4 copy-start.59
  314.8 4.2 copy-start.83
  540.7 3.9 copy-start.35
  540.7 3.9 copy-start.38
  542.3 5.3 slice-start.4
  544.7 2.9 slice-start.5
  557.2 5.7 slice-start.6
  560.0 2.9 slice-start.7
  (52 other events, 89.8 us)

commit v2 on v0

v2 whole, which is shorter than its diff:
```python
import functools
import math

import jax
import jax.numpy as jnp
from jax import lax
from jax.experimental import pallas as pl
from jax.experimental.pallas import tpu as pltpu
from jax.sharding import PartitionSpec as P

HEADS = 12
DH = 64
LAYERS = 2
NBINS = 10


def narrow(values):
    return values.astype(jnp.bfloat16)


def product(former, latter):
    return jnp.dot(former, latter, preferred_element_type=jnp.float32)


def contract_rows(former, latter):
    return lax.dot_general(
        former, latter, (((0,), (0,)), ((), ())), preferred_element_type=jnp.float32
    )


def contract_last(former, latter):
    return lax.dot_general(
        former, latter, (((1,), (1,)), ((), ())), preferred_element_type=jnp.float32
    )


def column_total(values):
    return jnp.sum(values.astype(jnp.float32), axis=0)


def norm_forward(summed, gain_vector, shift_vector):
    average = jnp.mean(summed, axis=-1, keepdims=True)
    centred = summed - average
    scaled = lax.rsqrt(jnp.mean(centred * centred, axis=-1, keepdims=True) + 1e-12)
    unit_rows = centred * scaled
    return (unit_rows * gain_vector + shift_vector, unit_rows, scaled)


def norm_backward(upstream, unit_rows, scaled, gain_vector):
    delta_unit = upstream * gain_vector
    delta_summed = scaled * (
        delta_unit
        - jnp.mean(delta_unit, axis=-1, keepdims=True)
        - unit_rows * jnp.mean(delta_unit * unit_rows, axis=-1, keepdims=True)
    )
    return (delta_summed, jnp.sum(upstream * unit_rows, axis=0), jnp.sum(upstream, axis=0))


def split_heads(flat, group_count, length):
    return flat.reshape(group_count, length, HEADS, DH)


def group_spans(layout):
    spans = []
    offset = 0
    for group_count, length in layout:
        spans.append((offset, group_count, length))
        offset = offset + group_count * length
    return spans


def attend_backward(query_part, key_part, value_part, shares, delta_context):
    attention = wide(shares)
    delta_value = jnp.einsum(
        "bhqk,bqhd->bkhd", narrow(attention), delta_context, preferred_element_type=jnp.float32
    )
    delta_attention = jnp.einsum(
        "bqhd,bkhd->bhqk", delta_context, value_part, preferred_element_type=jnp.float32
    )
    delta_scores = narrow(
        attention * (delta_attention - jnp.sum(attention * delta_attention, axis=-1, keepdims=True))
    )
    delta_query = (
        jnp.einsum("bhqk,bkhd->bqhd", delta_scores, key_part, preferred_element_type=jnp.float32)
        * 0.125
    )
    delta_key = (
        jnp.einsum("bhqk,bqhd->bkhd", delta_scores, query_part, preferred_element_type=jnp.float32)
        * 0.125
    )
    return (delta_query, delta_key, delta_value)


def layer_backward(upstream, stored, layout, params):
    (
        query_weight,
        query_bias,
        key_weight,
        value_weight,
        value_bias,
        mix_weight,
        mix_bias,
        norm_gain,
        norm_shift,
        expand_weight,
        expand_bias,
        reduce_weight,
        reduce_bias,
        final_gain,
        final_shift,
    ) = params
    (
        hidden,
        query_heads,
        key_heads,
        value_heads,
        shares,
        query_shares,
        context,
        unit_one,
        middle,
        slope,
        active,
        unit_two,
        scales,
    ) = stored
    scale_one, scale_two = scales[:, 0:1], scales[:, 1:2]
    unit_one, unit_two = wide(unit_one), wide(unit_two)
    (count, query_len), (_, passage_len) = layout
    pair_shares = shares.reshape(count, HEADS // 2, passage_len, 2, passage_len)
    pair_shares = pair_shares.transpose(0, 1, 3, 4, 2).reshape(
        count, HEADS, passage_len, passage_len
    )
    head_shares = query_shares.reshape(count, query_len, HEADS, count, query_len)
    head_shares = jnp.stack([head_shares[i, :, :, i] for i in range(count)])
    all_shares = (head_shares.transpose(0, 2, 3, 1), pair_shares)
    delta_two, delta_final_gain, delta_final_shift = norm_backward(
        upstream, unit_two, scale_two, final_gain
    )
    delta_branch = narrow(delta_two)
    delta_reduce_bias = column_total(delta_branch)
    delta_expanded = narrow(contract_last(delta_branch, reduce_weight) * wide(slope))
    delta_expand_bias = column_total(delta_expanded)
    delta_middle = delta_two + contract_last(delta_expanded, expand_weight)
    delta_one, delta_norm_gain, delta_norm_shift = norm_backward(
        delta_middle, unit_one, scale_one, norm_gain
    )
    delta_mix = narrow(delta_one)
    delta_mix_bias = column_total(delta_mix)
    delta_context = narrow(contract_last(delta_mix, mix_weight))
    collected = ([], [], [])
    for part_shares, (offset, group_count, length) in zip(all_shares, group_spans(layout)):
        row_span = group_count * length
        pieces = [
            split_heads(array[offset : offset + row_span], group_count, length)
            for array in (query_heads, key_heads, value_heads, delta_context)
        ]
        results = attend_backward(pieces[0], pieces[1], pieces[2], part_shares, pieces[3])
        for bucket, gradient in zip(collected, results):
            bucket.append(narrow(gradient.reshape(row_span, -1)))
    delta_query = jnp.concatenate(collected[0], axis=0)
    delta_key = jnp.concatenate(collected[1], axis=0)
    delta_value = jnp.concatenate(collected[2], axis=0)
    delta_hidden = (
        delta_one
        + contract_last(delta_query, query_weight)
        + contract_last(delta_key, key_weight)
        + contract_last(delta_value, value_weight)
    )
    operands = (
        active,
        delta_branch,
        middle,
        delta_expanded,
        hidden,
        context,
        delta_query,
        delta_key,
        delta_value,
        delta_mix,
    )
    vectors = (
        column_total(delta_query),
        column_total(delta_value),
        delta_mix_bias,
        delta_norm_gain,
        delta_norm_shift,
        delta_expand_bias,
        delta_reduce_bias,
        delta_final_gain,
        delta_final_shift,
    )
    return (delta_hidden, operands, vectors)


CORE_FLIP = [(0, 1), (1, 0), (2, 3), (3, 2)]
SIDE_FLIP = [(0, 2), (2, 0), (1, 3), (3, 1)]


def wide(values):
    return values.astype(jnp.float32)


def pick(array, index):
    return lax.dynamic_index_in_dim(array, index, 0, keepdims=False)


def reduce_chunk(chunk):
    rep_total = lax.axis_size("rep")
    group = lax.axis_index("grp")
    side, core = group // 2, group % 2
    parts = chunk.reshape((2, 2) + chunk.shape[1:])
    got = lax.ppermute(
        lax.dynamic_index_in_dim(parts, 1 - core, 1, keepdims=False), "grp", CORE_FLIP
    )
    mine = lax.dynamic_index_in_dim(parts, core, 1, keepdims=False)
    got = lax.ppermute(
        narrow(wide(pick(mine, 1 - side)) + wide(pick(got, 1 - side))), "grp", SIDE_FLIP
    ), narrow(wide(pick(mine, side)) + wide(pick(got, side)))
    summed = narrow(wide(got[0]) + wide(got[1]))
    rows, columns = summed.shape
    if rep_total != 8:
        part = lax.psum_scatter(summed, "rep", scatter_dimension=0, tiled=True)
        return wide(lax.all_gather(part, "rep", axis=0, tiled=True))
    rep = lax.axis_index("rep")
    deep, near = rep // 2, rep % 2
    flip = [(i, i ^ 1) for i in range(8)]
    shifts = [[(i, (i + 2 * k) % 8) for i in range(8)] for k in range(4)]
    halves = summed.reshape(2, rows // 2, columns)
    got = lax.ppermute(pick(halves, 1 - near), "rep", flip)
    half = narrow(wide(pick(halves, near)) + wide(got)).reshape(4, rows // 8, columns)
    total = wide(pick(half, deep))
    for k in range(1, 4):
        total = total + wide(lax.ppermute(pick(half, (deep + k) % 4), "rep", shifts[k]))
    piece = narrow(total)
    pieces = [piece] + [lax.ppermute(piece, "rep", shifts[k]) for k in range(1, 4)]
    joined = jnp.zeros((4,) + piece.shape, jnp.bfloat16)
    for k in range(4):
        joined = lax.dynamic_update_index_in_dim(joined, pieces[k], (deep - k) % 4, 0)
    other = lax.ppermute(joined, "rep", flip)
    own = joined.reshape(rows // 2, columns)
    other = other.reshape(rows // 2, columns)
    first = jnp.where(near == 0, own, other)
    second = jnp.where(near == 0, other, own)
    return wide(jnp.concatenate([first, second], axis=0))


def reduce_small(small):
    group = lax.axis_index("grp")
    side, core = group // 2, group % 2
    parts = small.reshape(2, 2, -1)
    got = lax.ppermute(
        lax.dynamic_index_in_dim(parts, 1 - core, 1, keepdims=False), "grp", CORE_FLIP
    )
    pair = lax.dynamic_index_in_dim(parts, core, 1, keepdims=False) + got
    total = pick(pair, side) + lax.ppermute(pick(pair, 1 - side), "grp", SIDE_FLIP)
    rep_total = lax.axis_size("rep")
    step = 1
    while step < rep_total:
        total = total + lax.ppermute(total, "rep", [(i, i ^ step) for i in range(rep_total)])
        step = step * 2
    return total


def remote(source, target, send_sem, recv_sem, grp, rep):
    return pltpu.make_async_remote_copy(
        src_ref=source,
        dst_ref=target,
        send_sem=send_sem,
        recv_sem=recv_sem,
        device_id=(grp, rep),
        device_id_type=pl.DeviceIdType.MESH,
    )


def gather_kernel(block_ref, out_ref, send_near, recv_near, send_far, recv_far):
    groups, reps = out_ref.shape[:2]
    grp, rep = lax.axis_index("grp"), lax.axis_index("rep")
    barrier = pltpu.get_barrier_semaphore()

    @pl.loop(1, reps)
    def _(k):
        pl.semaphore_signal(
            barrier, inc=1, device_id=(grp, (rep + k) % reps), device_id_type=pl.DeviceIdType.MESH
        )

    for k in range(1, groups):
        pl.semaphore_signal(
            barrier, inc=1, device_id=((grp + k) % groups, rep), device_id_type=pl.DeviceIdType.MESH
        )
    out_ref[grp, rep] = block_ref[...]
    pl.semaphore_wait(barrier, reps + groups - 2)

    def near(k):
        mine = out_ref.at[grp, rep]
        return remote(mine, mine, send_near.at[k], recv_near.at[k], grp, (rep + k) % reps)

    def far(k):
        row = out_ref.at[grp]
        return remote(row, row, send_far.at[k], recv_far.at[k], (grp + k) % groups, rep)

    @pl.loop(1, reps)
    def _(k):
        near(k).start()

    @pl.loop(1, reps)
    def _(k):
        near(k).wait_recv()

    for k in range(1, groups):
        far(k).start()
    for k in range(1, groups):
        far(k).wait_recv()

    @pl.loop(1, reps)
    def _(k):
        near(k).wait_send()

    for k in range(1, groups):
        far(k).wait_send()


def gather_blocks(block):
    groups, reps = lax.axis_size("grp"), lax.axis_size("rep")
    return pl.pallas_call(
        gather_kernel,
        out_shape=jax.ShapeDtypeStruct((groups, reps) + block.shape, block.dtype),
        in_specs=[pl.BlockSpec(memory_space=pltpu.VMEM)],
        out_specs=pl.BlockSpec(memory_space=pltpu.VMEM),
        scratch_shapes=[
            pltpu.SemaphoreType.DMA((reps,)),
            pltpu.SemaphoreType.DMA((reps,)),
            pltpu.SemaphoreType.DMA((groups,)),
            pltpu.SemaphoreType.DMA((groups,)),
        ],
        compiler_params=pltpu.CompilerParams(collective_id=1, has_side_effects=True),
    )(block)


def reduce_plain(layers):
    results = []
    for active, branch, middle, expanded, hidden, context, query, key, value, mix in layers:
        quarter = lambda former, latter: (
            lambda matrix: narrow(matrix).reshape(4, matrix.shape[0] // 4, matrix.shape[1])
        )(contract_rows(former, latter))
        square = jnp.concatenate(
            [
                quarter(hidden, query),
                quarter(hidden, key),
                quarter(hidden, value),
                quarter(context, mix),
            ],
            axis=1,
        )
        square = reduce_chunk(square)
        height = square.shape[0] // 4
        results.append(
            [square[place * height : (place + 1) * height] for place in range(4)]
            + [reduce_chunk(quarter(middle, expanded)), reduce_chunk(quarter(active, branch))]
        )
    return [jnp.stack([results[1][i], results[0][i]]) for i in range(6)]


SMALL = (1, 4, 6, 7, 8, 10, 12, 13, 14)
MATRICES = (0, 2, 3, 5, 9, 11)


LOG2E = 1.4426950408889634
V_QUERY, V_VALUE, V_MIX, V_GAIN, V_SHIFT, V_REDUCE, V_LAST_GAIN, V_LAST_SHIFT, V_EXPAND = range(9)
VECTOR_ROWS = 16
TILE = 256


def lane_masks(rows):
    lane = lax.broadcasted_iota(jnp.int32, (rows, 2 * DH), 1)
    return ((lane < DH).astype(jnp.float32).astype(jnp.bfloat16),
            (lane >= DH).astype(jnp.float32).astype(jnp.bfloat16))


def head_mask(head, width):
    lane = lax.broadcasted_iota(jnp.int32, (1, width), 1)
    return ((lane >= head * DH) & (lane < (head + 1) * DH))


def lanes(start, size=TILE):
    return pl.ds(pl.multiple_of(start, 128), size)


def sublanes(start, size):
    return pl.ds(pl.multiple_of(start, 16), size)


def softmax_rows(scores, bias):
    scaled = scores * (0.125 * LOG2E) + bias
    grown = jnp.exp2(scaled - jnp.max(scaled, axis=0, keepdims=True))
    return narrow(grown * (1.0 / jnp.sum(grown, axis=0, keepdims=True)))


def forward_kernel(
    lengths_ref,
    query_in,
    passage_in,
    wq_in,
    wk_in,
    wv_in,
    wm_in,
    we_in,
    wr_in,
    vec_ref,
    query_out,
    passage_out,
    hidden_out,
    q_out,
    k_out,
    v_out,
    pt_out,
    ptq_out,
    c_out,
    u1_out,
    m_out,
    slope_out,
    f_out,
    u2_out,
    r_out,
    wq,
    wk,
    wv,
    wm,
    we,
    wr,
    x,
    q,
    k,
    v,
    pt,
    ptq,
    c,
    u1,
    m,
    slope,
    f,
    u2,
    r,
    z,
    stack,
    weight_sem,
    in_sem,
    out_sem,
):
    width = x.shape[1]
    total = x.shape[0]
    sequences = lengths_ref.shape[0] // 2
    query_rows = query_in.shape[0]
    query_len = query_rows // sequences
    passage_len = (total - query_rows) // sequences
    pairs = width // (2 * DH)

    weights = ((wq_in, wq), (wk_in, wk), (wv_in, wv), (wm_in, wm), (we_in, we), (wr_in, wr))

    def weight_copy(which, layer):
        source, target = weights[which]
        return pltpu.make_async_copy(
            source.at[layer], target.at[layer], weight_sem.at[which, layer]
        )

    stored = (
        (x, hidden_out),
        (q, q_out),
        (k, k_out),
        (v, v_out),
        (pt, pt_out),
        (ptq, ptq_out),
        (c, c_out),
        (u1, u1_out),
        (m, m_out),
        (slope, slope_out),
        (f, f_out),
        (u2, u2_out),
        (r, r_out),
    )
    X, Q, K, V, PT, PTQ, C, U1, M, SLOPE, F, U2, R = range(13)

    def store(which, layer):
        source, target = stored[which]
        return pltpu.make_async_copy(source, target.at[layer], out_sem.at[which])

    def reuse(which, layer):
        @pl.when(layer > 0)
        def _():
            store(which, layer - 1).wait()

    first = pltpu.make_async_copy(query_in, x.at[pl.ds(0, query_rows)], in_sem.at[0])
    rest = pltpu.make_async_copy(
        passage_in, x.at[pl.ds(query_rows, total - query_rows)], in_sem.at[1]
    )
    first.start()
    rest.start()
    for layer in range(LAYERS):
        for which in range(6):
            weight_copy(which, layer).start()
    first.wait()
    rest.wait()

    def project(source, weight, layer, bias_row, target):
        @pl.loop(0, width // TILE)
        def _(i):
            value = product(source[...], weight[layer, :, lanes(i * TILE)])
            if bias_row is not None:
                value = value + vec_ref[layer, pl.ds(bias_row, 1), lanes(i * TILE)]
            target[:, lanes(i * TILE)] = narrow(value)

    def norm(layer, gain_row, shift_row, unit, target, scale_lane):
        step = 96
        gain = vec_ref[layer, pl.ds(gain_row, 1), :]
        shift = vec_ref[layer, pl.ds(shift_row, 1), :]

        @pl.loop(0, total // step)
        def _(i):
            at = sublanes(i * step, step)
            full, unit_rows, scaled = norm_forward(z[at, :], gain, shift)
            unit[at, :] = narrow(unit_rows)
            target[at, :] = narrow(full)
            r[at, scale_lane : scale_lane + 1] = scaled

    @pl.loop(0, LAYERS)
    def _(layer):
        store(X, layer).start()
        weight_copy(0, layer).wait()
        reuse(Q, layer)
        project(x, wq, layer, V_QUERY, q)
        store(Q, layer).start()
        weight_copy(1, layer).wait()
        reuse(K, layer)
        project(x, wk, layer, None, k)
        store(K, layer).start()
        weight_copy(2, layer).wait()
        reuse(V, layer)
        project(x, wv, layer, V_VALUE, v)
        store(V, layer).start()

        reuse(PT, layer)
        reuse(PTQ, layer)
        reuse(C, layer)

        for head in range(HEADS):
            mask = head_mask(head, width).astype(jnp.float32).astype(jnp.bfloat16)
            stack[head * query_rows : (head + 1) * query_rows, :] = q[:query_rows, :] * mask
        scores = contract_last(k[:query_rows, :], stack[...])
        key_slot = lax.broadcasted_iota(jnp.int32, scores.shape, 0)
        query_slot = lax.broadcasted_iota(jnp.int32, scores.shape, 1) % query_rows
        live = jnp.zeros(scores.shape, jnp.bool_)
        for s in range(sequences):
            low = s * query_len
            live = live | (
                (key_slot >= low)
                & (key_slot < low + lengths_ref[s])
                & (query_slot >= low)
                & (query_slot < low + query_len)
            )
        shares = softmax_rows(scores, jnp.where(live, 0.0, -1e30))
        ptq[...] = shares
        spread = contract_rows(shares, v[:query_rows, :])
        context = jnp.zeros((query_rows, width), jnp.float32)
        for head in range(HEADS):
            context = context + jnp.where(
                head_mask(head, width), spread[head * query_rows : (head + 1) * query_rows, :], 0.0
            )
        c[:query_rows, :] = narrow(context)

        @pl.loop(0, sequences * pairs)
        def _(i):
            s, pair = i // pairs, i % pairs
            rows = sublanes(query_rows + s * passage_len, passage_len)
            at = lanes(pair * 2 * DH, 2 * DH)
            even, odd = lane_masks(passage_len)
            q2, k2, v2 = q[rows, at], k[rows, at], v[rows, at]
            scores = contract_last(k2, jnp.concatenate([q2 * even, q2 * odd], axis=0))
            slot = lax.broadcasted_iota(jnp.int32, (passage_len, 1), 0)
            shares = softmax_rows(
                scores, jnp.where(slot < lengths_ref[sequences + s], 0.0, -1e30)
            )
            pt[i] = shares
            shares = jnp.concatenate([shares[:, :passage_len], shares[:, passage_len:]], axis=0)
            spread = contract_rows(jnp.concatenate([v2 * even, v2 * odd], axis=0), shares)
            c[rows, at] = narrow(spread.T)

        store(PT, layer).start()
        store(PTQ, layer).start()
        store(C, layer).start()

        weight_copy(3, layer).wait()

        @pl.loop(0, width // TILE)
        def _(i):
            at = lanes(i * TILE)
            z[:, at] = (
                wide(x[:, at])
                + product(c[...], wm[layer, :, at])
                + vec_ref[layer, pl.ds(V_MIX, 1), at]
            )

        reuse(U1, layer)
        reuse(M, layer)
        reuse(R, layer)
        norm(layer, V_GAIN, V_SHIFT, u1, m, 0)
        store(U1, layer).start()
        store(M, layer).start()

        weight_copy(4, layer).wait()
        reuse(SLOPE, layer)
        reuse(F, layer)

        @pl.loop(0, 4 * width // TILE)
        def _(i):
            at = lanes(i * TILE)
            tiles = width // TILE
            bias = vec_ref[layer, pl.ds(V_EXPAND + i // tiles, 1), lanes((i % tiles) * TILE)]
            value = product(m[...], we[layer, :, at]) + bias
            share = 0.5 * (1.0 + lax.erf(value * (1.0 / math.sqrt(2.0))))
            density = jnp.exp2(value * value * (-0.5 * LOG2E)) * (1.0 / math.sqrt(2.0 * math.pi))
            f[:, at] = narrow(value * share)
            slope[:, at] = narrow(share + value * density)

        store(SLOPE, layer).start()
        store(F, layer).start()

        weight_copy(5, layer).wait()

        @pl.loop(0, width // TILE)
        def _(i):
            at = lanes(i * TILE)
            z[:, at] = (
                wide(m[:, at])
                + product(f[...], wr[layer, :, at])
                + vec_ref[layer, pl.ds(V_REDUCE, 1), at]
            )

        store(X, layer).wait()
        reuse(U2, layer)
        norm(layer, V_LAST_GAIN, V_LAST_SHIFT, u2, x, 1)
        store(U2, layer).start()
        store(R, layer).start()

    last = LAYERS - 1
    first = pltpu.make_async_copy(x.at[pl.ds(0, query_rows)], query_out, in_sem.at[0])
    rest = pltpu.make_async_copy(
        x.at[pl.ds(query_rows, total - query_rows)], passage_out, in_sem.at[1]
    )
    first.start()
    rest.start()
    for which in range(1, 13):
        store(which, last).wait()
    first.wait()
    rest.wait()


def run_forward(lengths, query_input, passage_input, matrices, vectors):
    sequences, query_len, width = query_input.shape
    passage_len = passage_input.shape[1]
    query_rows, passage_rows = sequences * query_len, sequences * passage_len
    total = query_rows + passage_rows
    pairs = width // (2 * DH)
    bf16, f32 = jnp.bfloat16, jnp.float32
    arrays = (
        ((total, width), bf16),
        ((total, width), bf16),
        ((total, width), bf16),
        ((total, width), bf16),
        ((sequences * pairs, passage_len, 2 * passage_len), bf16),
        ((query_rows, HEADS * query_rows), bf16),
        ((total, width), bf16),
        ((total, width), bf16),
        ((total, width), bf16),
        ((total, 4 * width), bf16),
        ((total, 4 * width), bf16),
        ((total, width), bf16),
        ((total, 128), f32),
    )
    anywhere = pl.BlockSpec(memory_space=pl.ANY)
    return pl.pallas_call(
        forward_kernel,
        out_shape=(
            jax.ShapeDtypeStruct((query_rows, width), bf16),
            jax.ShapeDtypeStruct((passage_rows, width), bf16),
        )
        + tuple(jax.ShapeDtypeStruct((LAYERS,) + shape, dtype) for shape, dtype in arrays),
        in_specs=[pl.BlockSpec(memory_space=pltpu.SMEM)]
        + [anywhere] * 8
        + [pl.BlockSpec(memory_space=pltpu.VMEM)],
        out_specs=[anywhere] * 15,
        scratch_shapes=[pltpu.VMEM(matrix.shape, bf16) for matrix in matrices]
        + [pltpu.VMEM(shape, dtype) for shape, dtype in arrays]
        + [
            pltpu.VMEM((total, width), f32),
            pltpu.VMEM((HEADS * query_rows, width), bf16),
            pltpu.SemaphoreType.DMA((6, LAYERS)),
            pltpu.SemaphoreType.DMA((2,)),
            pltpu.SemaphoreType.DMA((13,)),
        ],
        compiler_params=pltpu.CompilerParams(vmem_limit_bytes=60 * 1024 * 1024),
    )(
        lengths,
        query_input.reshape(query_rows, width),
        passage_input.reshape(passage_rows, width),
        *matrices,
        vectors,
    )


def pack_vectors(query_bias, value_bias, mix_bias, norm_gain, norm_shift, reduce_bias, final_gain, final_shift, expand_bias):
    width = query_bias.shape[1]
    rows = [query_bias, value_bias, mix_bias, norm_gain, norm_shift, reduce_bias, final_gain, final_shift]
    packed = jnp.concatenate(
        [jnp.stack(rows, axis=1), expand_bias.reshape(LAYERS, -1, width)], axis=1
    )
    packed = jnp.pad(packed, ((0, 0), (0, VECTOR_ROWS - packed.shape[1]), (0, 0)))
    return packed.astype(jnp.float32)


CHUNKS = 12
PARTS = 6
S_QUERY, S_VALUE, S_MIX, S_GAIN, S_SHIFT, S_REDUCE, S_LAST_GAIN, S_LAST_SHIFT, S_EXPAND = range(9)
CORE_SLOTS, SIDE_SLOTS, NEAR_SLOTS, KEEP_SLOTS = 3, 4, 4, 6
BLOCK = 16


def one_hot(shape, hit):
    row = lax.broadcasted_iota(jnp.int32, shape, 0)
    column = lax.broadcasted_iota(jnp.int32, shape, 1)
    return narrow(jnp.where(hit(row, column), 1.0, 0.0))


def backward_kernel(
    margin_ref,
    positive_ref,
    cluster_row,
    cluster_column,
    vec_ref,
    query_out,
    passage_out,
    query_cot,
    passage_cot,
    wq_in,
    wk_in,
    wv_in,
    wm_in,
    we_in,
    wr_in,
    hidden_in,
    q_in,
    k_in,
    v_in,
    pt_in,
    ptq_in,
    c_in,
    u1_in,
    m_in,
    slope_in,
    f_in,
    u2_in,
    r_in,
    out_ref,
    small_out,
    loss_out,
    query_grad,
    passage_grad,
    buf,
    keep,
    side_out,
    core_in,
    side_in,
    near_in,
    deep_in,
    piece,
    small,
    small_core,
    small_side,
    small_near,
    small_deep,
    first,
    blocks,
    dz,
    dy,
    du,
    quad,
    pair_in,
    middle,
    unit,
    active,
    dc,
    pt,
    ptq,
    stack,
    r,
    w,
    gather_near,
    gather_far,
    first_sem,
    load_sem,
    weight_sem,
    core_sem,
    side_sem,
    near_sem,
    deep_send,
    deep_recv,
    back_send,
    back_recv,
    local_sem,
    last_sem,
    small_sem,
    small_send,
    small_recv,
    core_free,
    side_free,
    near_free,
):
    groups, reps = blocks.shape[:2]
    depth = reps // 2
    rows, width = keep.shape[1:]
    quarter = width // 4
    half_rows = rows // 2
    piece_rows = half_rows // depth
    total = dz.shape[0]
    sequences = margin_ref.shape[0]
    query_rows = query_out.shape[0]
    query_len = query_rows // sequences
    passage_len = (total - query_rows) // sequences
    pairs = width // (2 * DH)
    passage_rows = pl.ds(query_rows, total - query_rows)
    everyone = cluster_row.shape[1]

    grp, rep = lax.axis_index("grp"), lax.axis_index("rep")
    side, core = grp // 2, grp % 2
    deep, near = rep // 2, rep % 2
    sibling = (2 * side + (1 - core), rep)
    across = (2 * (1 - side) + core, rep)
    beside = (grp, 2 * deep + (1 - near))

    def behind(k):
        return (grp, 2 * ((deep + k) % depth) + near)

    def signal(semaphore, peer):
        pl.semaphore_signal(
            semaphore, inc=1, device_id=peer, device_id_type=pl.DeviceIdType.MESH
        )

    barrier = pltpu.get_barrier_semaphore()
    for k in range(1, reps):
        signal(barrier, (grp, (rep + k) % reps))
    for k in range(1, groups):
        signal(barrier, ((grp + k) % groups, rep))

    firsts = [
        pltpu.make_async_copy(
            source.at[pl.ds(s * length, BLOCK)],
            first.at[pl.ds((place * sequences + s) * BLOCK, BLOCK)],
            first_sem.at[place * sequences + s],
        )
        for place, (source, length) in enumerate(
            ((query_out, query_len), (passage_out, passage_len))
        )
        for s in range(sequences)
    ]
    for copy in firsts:
        copy.start()

    loaded = {
        "f": (f_in, active),
        "u2": (u2_in, unit.at[0]),
        "slope": (slope_in, du),
        "m": (m_in, middle),
        "u1": (u1_in, unit.at[1]),
        "c": (c_in, pair_in.at[1]),
        "q": (q_in, quad.at[0]),
        "k": (k_in, quad.at[1]),
        "v": (v_in, quad.at[2]),
        "pt": (pt_in, pt),
        "ptq": (ptq_in, ptq),
        "x": (hidden_in, pair_in.at[0]),
    }
    places = {name: place for place, name in enumerate(loaded)}

    def load(name, layer):
        source, target = loaded[name]
        return pltpu.make_async_copy(source.at[layer], target, load_sem.at[places[name]])

    def weight_loads(kind, layer, slot):
        squares = []
        for j in range(4):
            block = pl.ds(j * width, width)
            if kind == 0:
                source = wr_in.at[layer, block]
            elif kind == 1:
                source = we_in.at[layer, :, block]
            else:
                source = (wq_in, wk_in, wv_in, wm_in)[j].at[layer]
            squares.append(
                pltpu.make_async_copy(source, w.at[slot, j], weight_sem.at[slot, j])
            )
        return squares

    def start_weights(kind, layer, slot):
        for copy in weight_loads(kind, layer, slot):
            copy.start()

    def wait_weights(kind, layer, slot):
        for copy in weight_loads(kind, layer, slot):
            copy.wait()

    last = LAYERS - 1
    cots = [
        pltpu.make_async_copy(query_cot, dy.at[pl.ds(0, query_rows)], first_sem.at[4]),
        pltpu.make_async_copy(passage_cot, dy.at[passage_rows], first_sem.at[5]),
        pltpu.make_async_copy(r_in, r, first_sem.at[6]),
    ]
    for copy in cots:
        copy.start()
    for name in ("u2", "f"):
        load(name, last).start()
    start_weights(0, last, 0)
    for name in ("slope", "m", "u1", "c", "q", "k", "v", "pt", "ptq", "x"):
        load(name, last).start()
    start_weights(1, last, 1)

    for copy in firsts:
        copy.wait()
    chosen_rows = product(
        one_hot((BLOCK, first.shape[0]), lambda i, j: j == i * BLOCK), first[...]
    )
    row = lax.broadcasted_iota(jnp.int32, chosen_rows.shape, 0)
    lane = lax.broadcasted_iota(jnp.int32, chosen_rows.shape, 1)
    for s in range(sequences):
        positive = positive_ref[s]
        facts = (margin_ref[s], positive // 128, positive % 128)
        for place, fact in enumerate(facts):
            at = (row == 2 * sequences) & (lane == place * sequences + s)
            chosen_rows = jnp.where(at, fact.astype(jnp.float32), chosen_rows)
    blocks[grp, rep] = narrow(chosen_rows)

    def to_near(k):
        mine = blocks.at[grp, rep]
        return remote(
            mine, mine, gather_near.at[0, k], gather_near.at[1, k], grp, (rep + k) % reps
        )

    def to_far(k):
        line = blocks.at[grp]
        return remote(
            line, line, gather_far.at[0, k], gather_far.at[1, k], (grp + k) % groups, rep
        )

    pl.semaphore_wait(barrier, reps + groups - 2)

    @pl.loop(1, reps)
    def _(k):
        to_near(k).start()

    for copy in cots:
        copy.wait()
    small[...] = jnp.zeros_like(small)

    @pl.loop(0, total // 96)
    def _(i):
        at = sublanes(i * 96, 96)
        dz[at, :] = wide(dy[at, :])

    @pl.loop(1, reps)
    def _(k):
        to_near(k).wait_recv()

    for k in range(1, groups):
        to_far(k).start()
    for k in range(1, groups):
        to_far(k).wait_recv()

    gathered = blocks[...].reshape(groups * reps * BLOCK, width)

    def taken(offset):
        return product(
            one_hot(
                (everyone, gathered.shape[0]),
                lambda i, j: j == BLOCK * (i // sequences) + offset(i),
            ),
            gathered,
        )

    every_query = narrow(taken(lambda i: i % sequences))
    every_passage = narrow(taken(lambda i: sequences + i % sequences))
    facts = taken(lambda i: 2 * sequences)[:, :128]
    query_at = lax.broadcasted_iota(jnp.int32, facts.shape, 0) % sequences
    lane_at = lax.broadcasted_iota(jnp.int32, facts.shape, 1)

    def fact(place):
        hit = lane_at == place * sequences + query_at
        return jnp.sum(jnp.where(hit, facts, 0.0), axis=1, keepdims=True)

    margin_weight = (fact(0) + 1.0) / NBINS
    every_positive = fact(1) * 128.0 + fact(2)
    score_scale = 2.0 / math.sqrt(width)
    logits = contract_last(every_query, every_passage) * score_scale
    columns = lax.broadcasted_iota(jnp.int32, logits.shape, 1).astype(jnp.float32)
    chosen_mask = columns == every_positive
    allowed = (cluster_row[...] == cluster_column[...]) | chosen_mask
    masked = jnp.where(allowed, logits, -1e30)
    peak = jnp.max(masked, axis=1, keepdims=True)
    normalizer = peak + jnp.log(jnp.sum(jnp.exp(masked - peak), axis=1, keepdims=True))
    chosen = jnp.sum(jnp.where(chosen_mask, logits, 0.0), axis=1, keepdims=True)
    loss = margin_weight * (normalizer - chosen)
    share = jnp.where(allowed, jnp.exp(masked - normalizer), 0.0)
    delta_logits = narrow(margin_weight * (share - jnp.where(chosen_mask, 1.0, 0.0)))
    start = (grp * reps + rep) * sequences
    loss_row = lax.broadcasted_iota(jnp.int32, (everyone, 128), 0)
    loss_lane = lax.broadcasted_iota(jnp.int32, (everyone, 128), 1)
    loss_out[...] = jnp.broadcast_to(
        jnp.sum(jnp.where(loss_row == start + loss_lane, loss, 0.0), axis=0, keepdims=True),
        loss_out.shape,
    )
    own = one_hot((BLOCK, everyone), lambda i, j: (j == start + i) & (i < sequences))
    own_rows = narrow(product(own, delta_logits))
    own_columns = narrow(contract_last(own, delta_logits))
    delta_firsts = (
        product(own_rows, every_passage) * score_scale,
        product(own_columns, every_query) * score_scale,
    )
    eight = lax.broadcasted_iota(jnp.int32, (8, width), 0)
    for place, (base, length) in enumerate(((0, query_len), (query_rows, passage_len))):
        for s in range(sequences):
            at = pl.ds(base + s * length, 8)
            dz[at, :] = dz[at, :] + jnp.where(
                eight == 0, delta_firsts[place][s : s + 1, :], 0.0
            )

    def core_copy(t):
        return remote(
            buf.at[t % 2, :, 1 - core],
            core_in.at[t % CORE_SLOTS],
            core_sem.at[0, t],
            core_sem.at[1, t],
            *sibling,
        )

    def side_copy(t):
        return remote(
            side_out.at[t % 3],
            side_in.at[t % SIDE_SLOTS],
            side_sem.at[0, t],
            side_sem.at[1, t],
            *across,
        )

    def near_copy(t):
        return remote(
            keep.at[t % KEEP_SLOTS, sublanes((1 - near) * half_rows, half_rows)],
            near_in.at[t % NEAR_SLOTS],
            near_sem.at[0, t],
            near_sem.at[1, t],
            *beside,
        )

    def piece_of(position):
        return sublanes(near * half_rows + position * piece_rows, piece_rows)

    def deep_copy(t, k):
        return remote(
            keep.at[t % KEEP_SLOTS, piece_of((deep + k) % depth)],
            deep_in.at[t, k - 1],
            deep_send.at[k - 1, t],
            deep_recv.at[k - 1, t],
            *behind(k),
        )

    def chunk_place(t):
        step, part = t // PARTS, t % PARTS
        return (part // 2) * 4 + (last - step) * 2 + part % 2

    def back_copy(t, k):
        return remote(
            piece.at[t],
            out_ref.at[chunk_place(t), piece_of(deep)],
            back_send.at[k - 1, t],
            back_recv.at[k - 1, t],
            *behind(k),
        )

    def local_copy(t):
        return pltpu.make_async_copy(
            piece.at[t], out_ref.at[chunk_place(t), piece_of(deep)], local_sem.at[t]
        )

    def last_copy(t):
        half = out_ref.at[chunk_place(t), sublanes(near * half_rows, half_rows)]
        return remote(half, half, last_sem.at[0, t], last_sem.at[1, t], *beside)

    def add_rows(target, former, latter, count):
        step = 48

        @pl.loop(0, count // step)
        def _(i):
            def at(first_row):
                return sublanes(first_row + i * step, step)

            (to, to_row), (one, one_row), (two, two_row) = target, former, latter
            to[at(to_row), :] = narrow(wide(one[at(one_row), :]) + wide(two[at(two_row), :]))

    def after_core(t):
        core_copy(t).wait()
        slot = t % CORE_SLOTS
        add_rows(
            (side_out.at[t % 3], 0),
            (buf.at[t % 2, 1 - side, core], 0),
            (core_in.at[slot, 1 - side], 0),
            rows,
        )

        @pl.when(t >= SIDE_SLOTS)
        def _():
            pl.semaphore_wait(side_free, 1)

        side_copy(t).start()
        add_rows(
            (keep.at[t % KEEP_SLOTS], 0),
            (buf.at[t % 2, side, core], 0),
            (core_in.at[slot, side], 0),
            rows,
        )

        @pl.when(t + CORE_SLOTS < CHUNKS)
        def _():
            signal(core_free, sibling)

    def after_side(t):
        side_copy(t).wait()
        kept = keep.at[t % KEEP_SLOTS]
        came = side_in.at[t % SIDE_SLOTS]
        there, here = (1 - near) * half_rows, near * half_rows
        add_rows((kept, there), (kept, there), (came, there), half_rows)

        @pl.when(t >= NEAR_SLOTS)
        def _():
            pl.semaphore_wait(near_free, 1)

        near_copy(t).start()
        add_rows((kept, here), (kept, here), (came, here), half_rows)

        @pl.when(t + SIDE_SLOTS < CHUNKS)
        def _():
            signal(side_free, across)

    def after_near(t):
        near_copy(t).wait()
        kept = keep.at[t % KEEP_SLOTS]
        here = near * half_rows
        add_rows((kept, here), (kept, here), (near_in.at[t % NEAR_SLOTS], 0), half_rows)

        @pl.when(t + NEAR_SLOTS < CHUNKS)
        def _():
            signal(near_free, beside)

        for k in range(1, depth):
            deep_copy(t, k).start()

    def after_deep(t):
        summed = wide(keep[t % KEEP_SLOTS, piece_of(deep), :])
        for k in range(1, depth):
            deep_copy(t, k).wait()
        for k in range(1, depth):
            summed = summed + wide(deep_in[t, k - 1])
        piece[t] = narrow(summed)
        local_copy(t).start()
        for k in range(1, depth):
            back_copy(t, k).start()

    def after_back(t):
        local_copy(t).wait()
        for k in range(1, depth):
            back_copy(t, k).wait_recv()
        last_copy(t).start()

    def tally(layer, row_at, columns, values):
        at = (layer, pl.ds(row_at, 1), columns)
        small[at] = small[at] + jnp.sum(values, axis=0, keepdims=True)

    every_lane = pl.ds(0, width)

    def norm_back(layer, unit_at, scale_lane, gain_row, target, gain_to, shift_to, bias_to):
        step = 48
        gain = vec_ref[layer, pl.ds(gain_row, 1), :]

        @pl.loop(0, total // step)
        def _(i):
            at = sublanes(i * step, step)
            upstream = dz[at, :]
            unit_rows = wide(unit[unit_at, at, :])
            scaled = r[layer, at, scale_lane : scale_lane + 1]
            delta_unit = upstream * gain
            delta = scaled * (
                delta_unit
                - jnp.mean(delta_unit, axis=-1, keepdims=True)
                - unit_rows * jnp.mean(delta_unit * unit_rows, axis=-1, keepdims=True)
            )
            dz[at, :] = delta
            rounded = narrow(delta)
            target[at, :] = rounded
            tally(layer, gain_to, every_lane, upstream * unit_rows)
            tally(layer, shift_to, every_lane, upstream)
            tally(layer, bias_to, every_lane, wide(rounded))

    def expand_back(layer, slot):
        tiles = width // TILE

        @pl.loop(0, 4 * tiles)
        def _(i):
            at = lanes(i * TILE)
            block, tile = i // tiles, i % tiles
            weight = w[slot, block, sublanes(tile * TILE, TILE), :]
            value = narrow(contract_last(dy[...], weight) * wide(du[:, at]))
            du[:, at] = value
            tally(layer, S_EXPAND + block, lanes(tile * TILE), wide(value))

    def middle_back(slot):
        @pl.loop(0, width // TILE)
        def _(i):
            at = lanes(i * TILE)
            value = dz[:, at]
            for block in range(4):
                weight = w[slot, block, sublanes(i * TILE, TILE), :]
                value = value + contract_last(du[:, block * width : (block + 1) * width], weight)
            dz[:, at] = value

    def context_back(slot):
        @pl.loop(0, width // TILE)
        def _(i):
            weight = w[slot, 3, sublanes(i * TILE, TILE), :]
            dc[:, lanes(i * TILE)] = narrow(contract_last(quad[3], weight))

    def hidden_back(slot):
        @pl.loop(0, width // TILE)
        def _(i):
            at = lanes(i * TILE)
            value = dz[:, at]
            for place in range(3):
                weight = w[slot, place, sublanes(i * TILE, TILE), :]
                value = value + contract_last(quad[place], weight)
            dz[:, at] = value

    def score_back(shares, delta):
        shares = wide(shares)
        weighed = shares * delta
        return narrow(weighed - shares * jnp.sum(weighed, axis=0, keepdims=True))

    def attention_back(layer):
        query_span = pl.ds(0, query_rows)
        q2, k2, v2 = quad[0, query_span, :], quad[1, query_span, :], quad[2, query_span, :]

        def fill(rows_of):
            for head in range(HEADS):
                mask = narrow(jnp.where(head_mask(head, width), 1.0, 0.0))
                stack[head * query_rows : (head + 1) * query_rows, :] = rows_of * mask

        fill(dc[query_span, :])
        delta_value = narrow(product(ptq[...], stack[...]))
        delta_scores = score_back(ptq[...], contract_last(v2, stack[...]))
        fill(q2)
        delta_key = narrow(product(delta_scores, stack[...]) * 0.125)
        stack[...] = narrow(contract_rows(delta_scores, k2) * 0.125)
        delta_query = jnp.zeros((query_rows, width), jnp.float32)
        for head in range(HEADS):
            delta_query = delta_query + jnp.where(
                head_mask(head, width),
                wide(stack[head * query_rows : (head + 1) * query_rows, :]),
                0.0,
            )
        delta_query = narrow(delta_query)
        quad[0, query_span, :] = delta_query
        quad[1, query_span, :] = delta_key
        quad[2, query_span, :] = delta_value
        tally(layer, S_QUERY, every_lane, wide(delta_query))
        tally(layer, S_VALUE, every_lane, wide(delta_value))

        @pl.loop(0, sequences * pairs)
        def _(i):
            s, pair = i // pairs, i % pairs
            at_rows = sublanes(query_rows + s * passage_len, passage_len)
            at = lanes(pair * 2 * DH, 2 * DH)
            even, odd = lane_masks(passage_len)
            q2, k2, v2 = quad[0, at_rows, at], quad[1, at_rows, at], quad[2, at_rows, at]
            d2 = dc[at_rows, at]
            shares = pt[i]
            deltas = jnp.concatenate([d2 * even, d2 * odd], axis=0)
            delta_value = narrow(product(shares, deltas))
            delta_scores = score_back(shares, contract_last(v2, deltas))
            queries = jnp.concatenate([q2 * even, q2 * odd], axis=0)
            delta_key = narrow(product(delta_scores, queries) * 0.125)
            keys = jnp.concatenate([k2 * even, k2 * odd], axis=0)
            piled = jnp.concatenate(
                [delta_scores[:, :passage_len], delta_scores[:, passage_len:]], axis=0
            )
            delta_query = narrow((contract_rows(keys, piled) * 0.125).T)
            quad[0, at_rows, at] = delta_query
            quad[1, at_rows, at] = delta_key
            quad[2, at_rows, at] = delta_value
            tally(layer, S_QUERY, at, wide(delta_query))
            tally(layer, S_VALUE, at, wide(delta_value))

    def make_terms(t, part):
        tall = part < 2

        @pl.when(tall)
        def _():
            @pl.loop(0, 4)
            def _(i):
                columns = lanes(i * width + part * rows, rows)
                buf[t % 2, i // 2, i % 2] = narrow(contract_rows(active[:, columns], dy[...]))

        def split(i, terms):
            unit_at, half = i // 2, i % 2
            place = sublanes(unit_at * quarter, quarter)
            terms = narrow(terms)
            buf[t % 2, half, 0, place, :] = terms[:quarter]
            buf[t % 2, half, 1, place, :] = terms[quarter:]

        @pl.when((part == 2) | (part == 3))
        def _():
            @pl.loop(0, 4)
            def _(i):
                columns = lanes((2 * (part - 2) + i // 2) * width, width)
                split(
                    i,
                    contract_rows(
                        middle[:, lanes((i % 2) * 2 * quarter, 2 * quarter)], du[:, columns]
                    ),
                )

        @pl.when(part >= 4)
        def _():
            @pl.loop(0, 4)
            def _(i):
                which = 2 * (part - 4) + i // 2
                split(
                    i,
                    contract_rows(
                        pair_in[which // 3, :, lanes((i % 2) * 2 * quarter, 2 * quarter)],
                        quad[which],
                    ),
                )

        @pl.when(t >= CORE_SLOTS)
        def _():
            pl.semaphore_wait(core_free, 1)

        core_copy(t).start()

    def small_move(place, target, peer):
        return remote(
            small, target, small_sem.at[2 * place], small_sem.at[2 * place + 1], *peer
        )

    def small_to_deep(k):
        line = small_deep.at[deep]
        return remote(line, line, small_send.at[k - 1], small_recv.at[k - 1], *behind(k))

    def gradients_out():
        return (
            pltpu.make_async_copy(dz.at[pl.ds(0, query_rows)], query_grad, first_sem.at[4]),
            pltpu.make_async_copy(dz.at[passage_rows], passage_grad, first_sem.at[5]),
        )

    @pl.loop(0, CHUNKS + 5)
    def _(t):
        step, part = t // PARTS, t % PARTS
        layer = last - step
        slot = (3 * step) % 2
        busy = t < CHUNKS
        more = busy & (step < LAYERS - 1)

        @pl.when((t > 0) & (t <= CHUNKS))
        def _():
            after_core(t - 1)

        @pl.when(busy & (part == 0))
        def _():
            @pl.when(step > 0)
            def _():
                for name in ("c", "q", "k", "v", "x"):
                    load(name, layer).start()

            load("u2", layer).wait()
            norm_back(layer, 0, 1, V_LAST_GAIN, dy, S_LAST_GAIN, S_LAST_SHIFT, S_REDUCE)
            load("f", layer).wait()

        @pl.when(busy & (part == 4))
        def _():
            @pl.when(more)
            def _():
                for name in ("slope", "m", "u1"):
                    load(name, layer - 1).start()

            for name in ("c", "q", "k", "v", "pt", "ptq", "x"):
                load(name, layer).wait()
            attention_back(layer)

        @pl.when(busy & (part == 2))
        def _():
            load("m", layer).wait()

        @pl.when(busy)
        def _():
            make_terms(t, part)

        @pl.when(busy & (part == 1))
        def _():
            @pl.when(more)
            def _():
                for name in ("u2", "f"):
                    load(name, layer - 1).start()

            load("slope", layer).wait()
            wait_weights(0, layer, slot)
            expand_back(layer, slot)
            start_weights(2, layer, slot)

        @pl.when(busy & (part == 3))
        def _():
            wait_weights(1, layer, 1 - slot)
            middle_back(1 - slot)

            @pl.when(more)
            def _():
                start_weights(0, layer - 1, 1 - slot)

            load("u1", layer).wait()
            norm_back(layer, 1, 0, V_GAIN, quad.at[3], S_GAIN, S_SHIFT, S_MIX)
            wait_weights(2, layer, slot)
            context_back(slot)

        @pl.when(busy & (part == 5))
        def _():
            @pl.when(more)
            def _():
                for name in ("pt", "ptq"):
                    load(name, layer - 1).start()

            hidden_back(slot)

            @pl.when(more)
            def _():
                start_weights(1, layer - 1, slot)

            @pl.when(step == LAYERS - 1)
            def _():
                for copy in gradients_out():
                    copy.start()

        for lag, stage in enumerate((after_side, after_near, after_deep, after_back)):

            @pl.when((t > lag + 1) & (t < CHUNKS + lag + 2))
            def _():
                stage(t - lag - 2)

        for place, (target, peer, came) in enumerate(
            (
                (small_core, sibling, small_core),
                (small_side, across, small_side),
                (small_near, beside, small_near),
            )
        ):

            @pl.when(t == CHUNKS - 1 + place)
            def _():
                small_move(place, target, peer).start()

            @pl.when(t == CHUNKS + place)
            def _():
                small_move(place, target, peer).wait()
                small[...] = small[...] + came[...]

        @pl.when(t == CHUNKS + 2)
        def _():
            small_deep[deep] = small[...]
            for k in range(1, depth):
                small_to_deep(k).start()

        @pl.when(t == CHUNKS + 4)
        def _():
            for k in range(1, depth):
                small_to_deep(k).wait()
            summed = small_deep[0]
            for k in range(1, depth):
                summed = summed + small_deep[k]
            small_out[...] = summed

    @pl.loop(0, CHUNKS)
    def _(t):
        for k in range(1, depth):
            back_copy(t, k).wait_send()
        last_copy(t).wait()

    for copy in gradients_out():
        copy.wait()

    @pl.loop(1, reps)
    def _(k):
        to_near(k).wait_send()

    for k in range(1, groups):
        to_far(k).wait_send()


def run_backward(
    margin_bin,
    positive_index,
    cluster_index,
    vectors,
    query_output,
    passage_output,
    query_cotangent,
    passage_cotangent,
    matrices,
    stored,
):
    query_rows, width = query_output.shape
    passage_rows = passage_output.shape[0]
    total = query_rows + passage_rows
    sequences = margin_bin.shape[0]
    everyone = cluster_index.shape[0]
    groups, reps = lax.axis_size("grp"), lax.axis_size("rep")
    depth = reps // 2
    rows = width // 2
    piece_rows = rows // 2 // depth
    bf16, f32 = jnp.bfloat16, jnp.float32
    dma = pltpu.SemaphoreType.DMA
    anywhere = pl.BlockSpec(memory_space=pl.ANY)
    vmem = pl.BlockSpec(memory_space=pltpu.VMEM)
    smem = pl.BlockSpec(memory_space=pltpu.SMEM)
    small_shape = (LAYERS, 16, width)
    pt_shape, ptq_shape = stored[4].shape[1:], stored[5].shape[1:]
    return pl.pallas_call(
        backward_kernel,
        out_shape=(
            jax.ShapeDtypeStruct((CHUNKS, rows, width), bf16),
            jax.ShapeDtypeStruct(small_shape, f32),
            jax.ShapeDtypeStruct((8, 128), f32),
            jax.ShapeDtypeStruct((query_rows, width), f32),
            jax.ShapeDtypeStruct((passage_rows, width), f32),
        ),
        in_specs=[smem, smem, vmem, vmem, vmem] + [anywhere] * 23,
        out_specs=(anywhere, vmem, vmem, anywhere, anywhere),
        scratch_shapes=[
            pltpu.VMEM((2, 2, 2, rows, width), bf16),
            pltpu.VMEM((KEEP_SLOTS, rows, width), bf16),
            pltpu.VMEM((3, rows, width), bf16),
            pltpu.VMEM((CORE_SLOTS, 2, rows, width), bf16),
            pltpu.VMEM((SIDE_SLOTS, rows, width), bf16),
            pltpu.VMEM((NEAR_SLOTS, rows // 2, width), bf16),
            pltpu.VMEM((CHUNKS, depth - 1, piece_rows, width), bf16),
            pltpu.VMEM((CHUNKS, piece_rows, width), bf16),
            pltpu.VMEM(small_shape, f32),
            pltpu.VMEM(small_shape, f32),
            pltpu.VMEM(small_shape, f32),
            pltpu.VMEM(small_shape, f32),
            pltpu.VMEM((depth,) + small_shape, f32),
            pltpu.VMEM((2 * sequences * BLOCK, width), bf16),
            pltpu.VMEM((groups, reps, BLOCK, width), bf16),
            pltpu.VMEM((total, width), f32),
            pltpu.VMEM((total, width), bf16),
            pltpu.VMEM((total, 4 * width), bf16),
            pltpu.VMEM((4, total, width), bf16),
            pltpu.VMEM((2, total, width), bf16),
            pltpu.VMEM((total, width), bf16),
            pltpu.VMEM((2, total, width), bf16),
            pltpu.VMEM((total, 4 * width), bf16),
            pltpu.VMEM((total, width), bf16),
            pltpu.VMEM(pt_shape, bf16),
            pltpu.VMEM(ptq_shape, bf16),
            pltpu.VMEM((HEADS * query_rows, width), bf16),
            pltpu.VMEM((LAYERS, total, 128), f32),
            pltpu.VMEM((2, 4, width, width), bf16),
            dma((2, reps)),
            dma((2, groups)),
            dma((7,)),
            dma((12,)),
            dma((2, 4)),
            dma((2, CHUNKS)),
            dma((2, CHUNKS)),
            dma((2, CHUNKS)),
            dma((depth - 1, CHUNKS)),
            dma((depth - 1, CHUNKS)),
            dma((depth - 1, CHUNKS)),
            dma((depth - 1, CHUNKS)),
            dma((CHUNKS,)),
            dma((2, CHUNKS)),
            dma((6,)),
            dma((depth - 1,)),
            dma((depth - 1,)),
            pltpu.SemaphoreType.REGULAR,
            pltpu.SemaphoreType.REGULAR,
            pltpu.SemaphoreType.REGULAR,
        ],
        compiler_params=pltpu.CompilerParams(
            collective_id=0, has_side_effects=True, vmem_limit_bytes=62 * 1024 * 1024
        ),
    )(
        margin_bin,
        positive_index,
        cluster_index.reshape(1, everyone),
        cluster_index.reshape(everyone, 1),
        vectors,
        query_output,
        passage_output,
        query_cotangent.reshape(query_rows, width),
        passage_cotangent.reshape(passage_rows, width),
        *matrices,
        *stored,
    )


def backward_plain(
    query_output,
    passage_output,
    cluster_index,
    margin_bin,
    positive_index,
    query_cotangent,
    passage_cotangent,
    stored,
    params,
):
    batch_size, query_len, model_width = query_output.shape
    passage_len = passage_output.shape[1]
    layout = ((batch_size, query_len), (batch_size, passage_len))
    query_span = batch_size * query_len
    stored_layers = [tuple(array[layer_index] for array in stored) for layer_index in range(LAYERS)]
    query_first = query_output[:, 0, :]
    passage_first = passage_output[:, 0, :]
    facts = jnp.concatenate(
        [margin_bin, positive_index // 128, positive_index % 128], axis=0
    ).astype(jnp.bfloat16)
    facts = jnp.pad(facts, (0, model_width - facts.shape[0]))
    block = jnp.concatenate([query_first, passage_first, facts[None, :]], axis=0)
    block = jnp.pad(block, ((0, 8 - block.shape[0]), (0, 0)))
    total = cluster_index.shape[0]
    every = gather_blocks(block).reshape(-1, 8, model_width)
    every_query = every[:, :batch_size].reshape(total, model_width)
    every_passage = every[:, batch_size : 2 * batch_size].reshape(total, model_width)
    facts = every[:, 2 * batch_size, : 3 * batch_size].astype(jnp.int32)
    facts = facts.reshape(-1, 3, batch_size)
    every_margin = facts[:, 0].reshape(total)
    every_positive = (facts[:, 1] * 128 + facts[:, 2]).reshape(total)
    start_row = lax.axis_index(("grp", "rep")) * batch_size
    score_scale = 2.0 / math.sqrt(model_width)
    logits = contract_last(every_query, every_passage) * score_scale
    columns = lax.broadcasted_iota(jnp.int32, logits.shape, 1)
    chosen_mask = columns == every_positive[:, None]
    allowed = (cluster_index[None, :] == cluster_index[:, None]) | chosen_mask
    masked = jnp.where(allowed, logits, -1e30)
    peak_score = jnp.max(masked, axis=1, keepdims=True)
    normalizer = peak_score + jnp.log(jnp.sum(jnp.exp(masked - peak_score), axis=1, keepdims=True))
    chosen = jnp.sum(jnp.where(chosen_mask, logits, 0.0), axis=1)
    margin_weight = (every_margin + 1).astype(jnp.float32) / NBINS
    every_loss = margin_weight * (normalizer[:, 0] - chosen)
    query_loss = lax.dynamic_slice_in_dim(every_loss, start_row, batch_size)
    delta_logits = narrow(
        margin_weight[:, None]
        * (jnp.where(allowed, jnp.exp(masked - normalizer), 0.0) - chosen_mask.astype(jnp.float32))
    )
    own_rows = lax.dynamic_slice_in_dim(delta_logits, start_row, batch_size, axis=0)
    own_columns = lax.dynamic_slice_in_dim(delta_logits, start_row, batch_size, axis=1)
    delta_query_first = product(own_rows, every_passage) * score_scale
    delta_passage_first = contract_rows(own_columns, every_query) * score_scale
    query_upstream = query_cotangent.astype(jnp.float32).at[:, 0, :].add(delta_query_first)
    passage_upstream = passage_cotangent.astype(jnp.float32).at[:, 0, :].add(delta_passage_first)
    upstream = jnp.concatenate(
        [
            query_upstream.reshape(query_span, model_width),
            passage_upstream.reshape(batch_size * passage_len, model_width),
        ],
        axis=0,
    )
    operands = []
    small = []
    for layer_index in reversed(range(LAYERS)):
        layer_params = tuple(array[layer_index] for array in params)
        upstream, layer_operands, vectors = layer_backward(
            upstream, stored_layers[layer_index], layout, layer_params
        )
        operands.append(layer_operands)
        small.append([vector.reshape(4, -1) for vector in vectors])
    small = small[::-1]
    matrices = reduce_plain(operands)
    flat = reduce_small(jnp.concatenate(small[0] + small[1], axis=1))
    reduced = [None] * 15
    for slot, matrix in zip(MATRICES, matrices):
        reduced[slot] = matrix
    flat = flat.reshape(LAYERS, -1)
    offset = 0
    for slot, vector in zip(SMALL, small[0]):
        size = vector.shape[1]
        reduced[slot] = flat[:, offset : offset + size]
        offset = offset + size
    return query_loss, upstream[:query_span], upstream[query_span:], reduced


def unpack_gradients(out, small):
    width = out.shape[2]
    quarter = width // 4
    blocks = out.reshape(3, LAYERS, 4, quarter, width)
    reduced = [None] * 15
    reduced[11] = wide(blocks[0].reshape(LAYERS, width, width))
    reduced[9] = wide(jnp.swapaxes(blocks[1], 1, 2).reshape(LAYERS, quarter, 4 * width))
    for place, slot in enumerate((0, 2, 3, 5)):
        reduced[slot] = wide(blocks[2, :, place])
    group = lax.axis_index("grp")
    narrow_rows = lax.dynamic_slice_in_dim(small[:, :8], group * quarter, quarter, axis=2)
    for place, slot in enumerate((1, 4, 6, 7, 8, 12, 13, 14)):
        reduced[slot] = narrow_rows[:, place]
    reduced[10] = lax.dynamic_index_in_dim(small, S_EXPAND + group, 1, keepdims=False)
    return reduced


def per_device(
    query_input,
    passage_input,
    query_length,
    passage_length,
    cluster_index,
    margin_bin,
    positive_index,
    query_cotangent,
    passage_cotangent,
    query_weight,
    query_bias,
    key_weight,
    value_weight,
    value_bias,
    mix_weight,
    mix_bias,
    norm_gain,
    norm_shift,
    expand_weight,
    expand_bias,
    reduce_weight,
    reduce_bias,
    final_gain,
    final_shift,
):
    params = (
        query_weight,
        query_bias,
        key_weight,
        value_weight,
        value_bias,
        mix_weight,
        mix_bias,
        norm_gain,
        norm_shift,
        expand_weight,
        expand_bias,
        reduce_weight,
        reduce_bias,
        final_gain,
        final_shift,
    )
    batch_size, query_len, model_width = query_input.shape
    passage_len = passage_input.shape[1]
    matrices = (query_weight, key_weight, value_weight, mix_weight, expand_weight, reduce_weight)
    vectors = pack_vectors(
        query_bias,
        value_bias,
        mix_bias,
        norm_gain,
        norm_shift,
        reduce_bias,
        final_gain,
        final_shift,
        expand_bias,
    )
    results = run_forward(
        jnp.concatenate([query_length, passage_length]),
        query_input,
        passage_input,
        matrices,
        vectors,
    )
    query_output = results[0].reshape(batch_size, query_len, model_width)
    passage_output = results[1].reshape(batch_size, passage_len, model_width)
    if lax.axis_size("rep") != 8:
        query_loss, query_gradient, passage_gradient, reduced = backward_plain(
            query_output,
            passage_output,
            cluster_index,
            margin_bin,
            positive_index,
            query_cotangent,
            passage_cotangent,
            results[2:],
            params,
        )
    else:
        out, small, loss, query_gradient, passage_gradient = run_backward(
            margin_bin,
            positive_index,
            cluster_index,
            vectors,
            results[0],
            results[1],
            query_cotangent,
            passage_cotangent,
            matrices,
            results[2:],
        )
        query_loss = loss[0, :batch_size]
        reduced = unpack_gradients(out, small)
    return (
        query_output,
        passage_output,
        query_loss,
        query_gradient.reshape(batch_size, query_len, model_width),
        passage_gradient.reshape(batch_size, passage_len, model_width),
        reduced[0],
        reduced[1],
        reduced[2],
        reduced[3],
        reduced[4],
        reduced[5],
        reduced[6],
        reduced[7],
        reduced[8],
        reduced[9],
        reduced[10],
        reduced[11],
        reduced[12],
        reduced[13],
        reduced[14],
    )


def solution(mesh):
    placed = (
        P(("grp", "rep"), None, None),
        P(("grp", "rep"), None, None),
        P(("grp", "rep")),
        P(("grp", "rep")),
        P(),
        P(("grp", "rep")),
        P(("grp", "rep")),
        P(("grp", "rep"), None, None),
        P(("grp", "rep"), None, None),
        P(),
        P(),
        P(),
        P(),
        P(),
        P(),
        P(),
        P(),
        P(),
        P(),
        P(),
        P(),
        P(),
        P(),
        P(),
    )
    return jax.shard_map(
        per_device,
        mesh=mesh,
        in_specs=placed,
        out_specs=(
            P(("grp", "rep"), None, None),
            P(("grp", "rep"), None, None),
            P(("grp", "rep")),
            P(("grp", "rep"), None, None),
            P(("grp", "rep"), None, None),
            P(None, "grp", None),
            P(None, "grp"),
            P(None, "grp", None),
            P(None, "grp", None),
            P(None, "grp"),
            P(None, "grp", None),
            P(None, "grp"),
            P(None, "grp"),
            P(None, "grp"),
            P(None, "grp", None),
            P(None, "grp"),
            P(None, "grp", None),
            P(None, "grp"),
            P(None, "grp"),
            P(None, "grp"),
        ),
        check_vma=False,
    )
```

time: 1240 us -> 334 us (0.27)
  waiting for transfers between devices: 761 us -> 0 us
  Pallas kernels: 0 us -> 303 us
  matrix products: 198 us -> 0 us
  blocking collectives: 122 us -> 0 us
  other arithmetic: 68.7 us -> 8.86 us
  local copies, waits for them, and re-layouts: 68.2 us -> 20.3 us
  between operations: 18.6 us -> 0.71 us
    psum x1 -> x0, waiting for transfers between devices: 385 us -> none  [reduce_layer(): lax.psum((shards[0], shards[1], shards[2], shards[3], shards[4], shards[5...]
    pallas_call x0 -> x2, Pallas kernels: none -> 303 us  [the longest x1 240 us: run_backward(): pl.pallas_call(backward_kernel, out_shape=(jax.ShapeDtypeStruct((CHUNKS,...]
    reduce_scatter x12 -> x0, waiting for transfers between devices: 260 us -> none  [the longest x2 96.2 us: reduce_layer(): lax.psum_scatter(gradients[9].astype(jnp.bfloat16), 'grp', scatter_dimens...]
    dot_general x63 -> x0, matrix products: 198 us -> none  [the longest x13 56.9 us: product(): return jnp.dot(former, latter, preferred_element_type=jnp.float32)]
    unnamed x15 -> x0, waiting for transfers between devices: 116 us -> none
    all_gather x1 -> x0, blocking collectives: 71.1 us -> none  [per_device(): lax.all_gather(passage_first, ('grp', 'rep'), axis=0, tiled=True)]
    another operation x27 -> x0, other arithmetic: 42.6 us -> none  [per_device(): jnp.stack([per_layer[layer_index][slot] for layer_index in range(LAYERS)])]
    psum x1 -> x0, blocking collectives: 39.7 us -> none  [reduce_layer(): lax.psum((shards[0], shards[1], shards[2], shards[3], shards[4], shards[5...]
  transfers between devices with their start and end apart: 14 -> 0, of which waited for: 9 -> 0; matrix products, arithmetic and copies ran while one was open for 14% -> 0% of each run, Pallas kernels for 0% -> 0%
where the time goes in v2:
time: 334 us; the launch traced here: 332 us
  Pallas kernels  303 us (91%)
  local copies, waits for them, and re-layouts  20.3 us (6%)
  other arithmetic  8.86 us (3%)
    pallas_call x1, Pallas kernels, run_backward(): pl.pallas_call(backward_kernel, out_shape=(jax.ShapeDtypeStruct((CHUNKS,...  240 us
    pallas_call x1, Pallas kernels, run_forward(): pl.pallas_call(forward_kernel, out_shape=(jax.ShapeDtypeStruct((query_row...  63.1 us

profile of v2, /device:TPU:0, one launch (start us, length us, event | category | flops | bytes accessed | tf_op | source)
XLA Modules:
  0.0 332.5 jit_solution(5318494593449767607)
XLA Ops:
  0.7 0.7 reshape.97
  1.4 0.7 copy.50
  2.1 0.7 copy.51
  2.8 0.7 copy.52
  3.4 0.7 copy.53
  4.1 0.7 copy.54
  4.8 0.7 copy.55
  5.5 0.7 copy.56
  6.2 0.7 copy.57
  6.9 0.1 concatenate.7
  7.0 0.7 pad_convert_fusion.vec_ref
  7.6 1.3 pad_add_fusion.lengths_ref
  8.9 0.0 copy-start.2
  8.9 63.1 %shard_map.383 = (bf16[64,768]{1,0:T(8,128)(2,1)}, bf16[512,768]{1,0:T(8,128)(2,1)}, bf16[2,576,768]{2,1,0:T(8,128)(2,1)}, bf16[2,576,768]{2,1,0:T(8,128)(2,1)},...) custom-call(s32[4]{0:T(128)} %pad_add_fusion.lengths_ref, ...), custom_call_target="tpu_custom_call" | custom-call | tf_op jit(solution)/shard_map/pallas_call | solution.py:680
  72.0 0.0 copy-done.2
  72.0 0.7 copy.58.cluster_column
  72.7 239.6 %shard_map.384 = (bf16[12,384,768]{2,1,0:T(8,128)(2,1)}, f32[2,16,768]{2,1,0:T(8,128)}, f32[8,128]{1,0:T(8,128)}, f32[64,768]{1,0:T(8,128)}, f32[512,768]{1,0:T(8,128)}) custom-call(s32[2]{0:T(128)} %margin_ref.1, s32[2]{0:T(128)} %positive_ref.1, s32[1,64]{1,0:T(1,128)} %bitcast.99, s32[64,1]{1,0:T(8,128)} %copy.58.cluster_column, ...), custom_call_target="tpu_custom_call" | custom-call | tf_op jit(solution)/shard_map/pallas_call | solution.py:1537
  312.3 0.8 slice.52
  313.1 0.1 constant_dynamic-slice_fusion.8
  313.2 0.6 copy_bitcast_fusion.1
  313.8 2.7 fusion.4
  316.5 0.4 convert_bitcast_fusion
  316.9 2.9 copy.77
  319.8 2.5 bitcast_convert_fusion
  322.3 0.6 copy_bitcast_fusion.3
  322.9 0.6 copy_bitcast_fusion.5
  323.5 0.6 copy_bitcast_fusion.7
  324.1 0.0 copy-start.1
  324.1 0.0 copy-start
  324.1 4.0 %fusion = (f32[2,192,768]{2,1,0:T(8,128)}, f32[2,192,768]{2,1,0:T(8,128)}, f32[2,192,768]{2,1,0:T(8,128)}, f32[2,192,768]{2,1,0:T(8,128)}) fusion(bf16[3,2,4,192,768]{4,3,2,1,0:T(8,128)(2,1)} %bitcast.80), kind=kLoop, calls=%fused_computation.3 | loop fusion | flops 1179648 | bytes 7077888 | tf_op jit(solution)/shard_map/convert_element_type | solution.py:201
  328.1 0.8 constant_dynamic-slice_fusion.7
  328.9 0.6 copy.87
  329.5 1.2 slice_bitcast_fusion.4
  330.7 0.0 copy-done.1
  330.7 0.7 copy.90
  331.3 0.0 copy-done
  331.3 1.1 copy.91
Async XLA Ops:
  8.9 63.1 %copy-start.2 = (s32[64]{0:T(128)S(1)}, s32[64]{0:T(128)}, u32[]{:S(2)}) copy-start(s32[64]{0:T(128)} %param.28) | copy-start | bytes 772
  324.1 6.6 %copy-start.1 = (f32[64,768]{1,0:T(8,128)S(1)}, f32[64,768]{1,0:T(8,128)}, u32[]{:S(2)}) copy-start(f32[64,768]{1,0:T(8,128)} %get-tuple-element.56) | copy-start | bytes 589828
  324.1 7.3 %copy-start = (f32[512,768]{1,0:T(8,128)S(1)}, f32[512,768]{1,0:T(8,128)}, u32[]{:S(2)}) copy-start(f32[512,768]{1,0:T(8,128)} %get-tuple-element.57) | copy-start | bytes 4718596

commit v3 on v2

--- a/solution.py
+++ b/solution.py
@@ -397,7 +397,8 @@
 
 
 def forward_kernel(
-    lengths_ref,
+    query_lengths,
+    passage_lengths,
     query_in,
     passage_in,
     wq_in,
@@ -406,7 +407,15 @@
     wm_in,
     we_in,
     wr_in,
-    vec_ref,
+    query_bias,
+    value_bias,
+    mix_bias,
+    norm_gain,
+    norm_shift,
+    reduce_bias,
+    final_gain,
+    final_shift,
+    expand_bias,
     query_out,
     passage_out,
     hidden_out,
@@ -443,13 +452,14 @@
     r,
     z,
     stack,
+    vec_ref,
     weight_sem,
     in_sem,
     out_sem,
 ):
     width = x.shape[1]
     total = x.shape[0]
-    sequences = lengths_ref.shape[0] // 2
+    sequences = query_lengths.shape[0]
     query_rows = query_in.shape[0]
     query_len = query_rows // sequences
     passage_len = (total - query_rows) // sequences
@@ -498,6 +508,23 @@
     for layer in range(LAYERS):
         for which in range(6):
             weight_copy(which, layer).start()
+    vectors = (
+        query_bias,
+        value_bias,
+        mix_bias,
+        norm_gain,
+        norm_shift,
+        reduce_bias,
+        final_gain,
+        final_shift,
+    )
+    for layer in range(LAYERS):
+        for place, vector in enumerate(vectors):
+            vec_ref[layer, place : place + 1, :] = wide(vector[layer : layer + 1, :])
+        for j in range(4):
+            vec_ref[layer, V_EXPAND + j : V_EXPAND + j + 1, :] = wide(
+                expand_bias[layer : layer + 1, j * width : (j + 1) * width]
+            )
     first.wait()
     rest.wait()
 
@@ -553,7 +580,7 @@
             low = s * query_len
             live = live | (
                 (key_slot >= low)
-                & (key_slot < low + lengths_ref[s])
+                & (key_slot < low + query_lengths[s])
                 & (query_slot >= low)
                 & (query_slot < low + query_len)
             )
@@ -577,7 +604,7 @@
             scores = contract_last(k2, jnp.concatenate([q2 * even, q2 * odd], axis=0))
             slot = lax.broadcasted_iota(jnp.int32, (passage_len, 1), 0)
             shares = softmax_rows(
-                scores, jnp.where(slot < lengths_ref[sequences + s], 0.0, -1e30)
+                scores, jnp.where(slot < passage_lengths[s], 0.0, -1e30)
             )
             pt[i] = shares
             shares = jnp.concatenate([shares[:, :passage_len], shares[:, passage_len:]], axis=0)
@@ -654,7 +681,7 @@
     rest.wait()
 
 
-def run_forward(lengths, query_input, passage_input, matrices, vectors):
+def run_forward(query_length, passage_length, query_input, passage_input, matrices, vectors):
     sequences, query_len, width = query_input.shape
     passage_len = passage_input.shape[1]
     query_rows, passage_rows = sequences * query_len, sequences * passage_len
@@ -684,44 +711,38 @@
             jax.ShapeDtypeStruct((passage_rows, width), bf16),
         )
         + tuple(jax.ShapeDtypeStruct((LAYERS,) + shape, dtype) for shape, dtype in arrays),
-        in_specs=[pl.BlockSpec(memory_space=pltpu.SMEM)]
+        in_specs=[pl.BlockSpec(memory_space=pltpu.SMEM)] * 2
         + [anywhere] * 8
-        + [pl.BlockSpec(memory_space=pltpu.VMEM)],
+        + [pl.BlockSpec(memory_space=pltpu.VMEM)] * 9,
         out_specs=[anywhere] * 15,
         scratch_shapes=[pltpu.VMEM(matrix.shape, bf16) for matrix in matrices]
         + [pltpu.VMEM(shape, dtype) for shape, dtype in arrays]
         + [
             pltpu.VMEM((total, width), f32),
             pltpu.VMEM((HEADS * query_rows, width), bf16),
+            pltpu.VMEM((LAYERS, VECTOR_ROWS, width), f32),
             pltpu.SemaphoreType.DMA((6, LAYERS)),
             pltpu.SemaphoreType.DMA((2,)),
             pltpu.SemaphoreType.DMA((13,)),
         ],
         compiler_params=pltpu.CompilerParams(vmem_limit_bytes=60 * 1024 * 1024),
     )(
-        lengths,
+        query_length,
+        passage_length,
         query_input.reshape(query_rows, width),
         passage_input.reshape(passage_rows, width),
         *matrices,
-        vectors,
-    )
-
-
-def pack_vectors(query_bias, value_bias, mix_bias, norm_gain, norm_shift, reduce_bias, final_gain, final_shift, expand_bias):
-    width = query_bias.shape[1]
-    rows = [query_bias, value_bias, mix_bias, norm_gain, norm_shift, reduce_bias, final_gain, final_shift]
-    packed = jnp.concatenate(
-        [jnp.stack(rows, axis=1), expand_bias.reshape(LAYERS, -1, width)], axis=1
-    )
-    packed = jnp.pad(packed, ((0, 0), (0, VECTOR_ROWS - packed.shape[1]), (0, 0)))
-    return packed.astype(jnp.float32)
-
-
-CHUNKS = 12
-PARTS = 6
+        *vectors,
+    )
+
+
+CHUNKS = 24
+PARTS = 12
 S_QUERY, S_VALUE, S_MIX, S_GAIN, S_SHIFT, S_REDUCE, S_LAST_GAIN, S_LAST_SHIFT, S_EXPAND = range(9)
-CORE_SLOTS, SIDE_SLOTS, NEAR_SLOTS, KEEP_SLOTS = 3, 4, 4, 6
+CORE_SLOTS, SIDE_SLOTS, NEAR_SLOTS, KEEP_SLOTS, SENT_SLOTS = 4, 4, 4, 6, 3
+LAGS = (2, 3, 4, 5, 6)
 BLOCK = 16
+SMALL_AT = 21
 
 
 def one_hot(shape, hit):
@@ -734,8 +755,8 @@
     margin_ref,
     positive_ref,
     cluster_row,
-    cluster_column,
-    vec_ref,
+    norm_gain,
+    final_gain,
     query_out,
     passage_out,
     query_cot,
@@ -779,6 +800,7 @@
     small_deep,
     first,
     blocks,
+    gains,
     dz,
     dy,
     du,
@@ -803,10 +825,8 @@
     near_sem,
     deep_send,
     deep_recv,
-    back_send,
-    back_recv,
+    back_sem,
     local_sem,
-    last_sem,
     small_sem,
     small_send,
     small_recv,
@@ -816,7 +836,8 @@
 ):
     groups, reps = blocks.shape[:2]
     depth = reps // 2
-    rows, width = keep.shape[1:]
+    rows, columns = keep.shape[1:]
+    width = dz.shape[1]
     quarter = width // 4
     half_rows = rows // 2
     piece_rows = half_rows // depth
@@ -838,6 +859,10 @@
 
     def behind(k):
         return (grp, 2 * ((deep + k) % depth) + near)
+
+    deep_low, deep_high = deep % 2, deep // 2
+    beyond = (grp, 2 * (deep + 2 - 4 * deep_high) + near)
+    next_to = (grp, 2 * (deep + 1 - 2 * deep_low) + near)
 
     def signal(semaphore, peer):
         pl.semaphore_signal(
@@ -917,63 +942,133 @@
         copy.start()
     for name in ("u2", "f"):
         load(name, last).start()
+
+    def tally(layer, row_at, lanes_at, values):
+        at = (layer, pl.ds(row_at, 1), lanes_at)
+        small[at] = small[at] + jnp.sum(values, axis=0, keepdims=True)
+
+    every_lane = pl.ds(0, width)
+
+    norm_step = 48
+
+    def norm_back_rows(
+        layer, unit_at, scale_lane, gain_row, target, gain_to, shift_to, bias_to, tile
+    ):
+        gain = gains[layer, pl.ds(gain_row, 1), :]
+        at = sublanes(tile * norm_step, norm_step)
+        upstream = dz[at, :]
+        unit_rows = wide(unit[unit_at, at, :])
+        scaled = r[layer, at, scale_lane : scale_lane + 1]
+        delta_unit = upstream * gain
+        delta = scaled * (
+            delta_unit
+            - jnp.mean(delta_unit, axis=-1, keepdims=True)
+            - unit_rows * jnp.mean(delta_unit * unit_rows, axis=-1, keepdims=True)
+        )
+        dz[at, :] = delta
+        rounded = narrow(delta)
+        target[at, :] = rounded
+        tally(layer, gain_to, every_lane, upstream * unit_rows)
+        tally(layer, shift_to, every_lane, upstream)
+        tally(layer, bias_to, every_lane, wide(rounded))
+
+    def last_norm_back(layer, tile):
+        norm_back_rows(
+            layer, 0, 1, 1, dy, S_LAST_GAIN, S_LAST_SHIFT, S_REDUCE, tile
+        )
+
+    def first_norm_back(layer, tile):
+        norm_back_rows(layer, 1, 0, 0, quad.at[3], S_GAIN, S_SHIFT, S_MIX, tile)
+
+    for copy in firsts:
+        copy.wait()
+    firsts_count = 2 * sequences
+    segments = width // TILE
+    packed = jnp.zeros((BLOCK, TILE), jnp.float32)
+    for j in range(segments):
+        low = j * firsts_count
+        packed = packed + product(
+            one_hot(
+                (BLOCK, first.shape[0]),
+                lambda i, k: (k == (i - low) * BLOCK) & (i >= low) & (i < low + firsts_count),
+            ),
+            first[:, j * TILE : (j + 1) * TILE],
+        )
+    row = lax.broadcasted_iota(jnp.int32, packed.shape, 0)
+    lane = lax.broadcasted_iota(jnp.int32, packed.shape, 1)
+    for s in range(sequences):
+        positive = positive_ref[s]
+        facts = (margin_ref[s], positive // 128, positive % 128)
+        for place, fact in enumerate(facts):
+            at = (row == segments * firsts_count) & (lane == place * sequences + s)
+            packed = jnp.where(at, fact.astype(jnp.float32), packed)
+    blocks[grp, rep] = narrow(packed)
+
+    def to_near(k):
+        mine = blocks.at[grp, rep]
+        return remote(
+            mine, mine, gather_near.at[0, k], gather_near.at[1, k], grp, (rep + k) % reps
+        )
+
+    def to_far(k):
+        line = blocks.at[grp]
+        return remote(
+            line, line, gather_far.at[0, k], gather_far.at[1, k], (grp + k) % groups, rep
+        )
+
+    pl.semaphore_wait(barrier, reps + groups - 2)
+
+    @pl.loop(1, reps)
+    def _(k):
+        to_near(k).start()
+
     start_weights(0, last, 0)
     for name in ("slope", "m", "u1", "c", "q", "k", "v", "pt", "ptq", "x"):
         load(name, last).start()
     start_weights(1, last, 1)
 
-    for copy in firsts:
-        copy.wait()
-    chosen_rows = product(
-        one_hot((BLOCK, first.shape[0]), lambda i, j: j == i * BLOCK), first[...]
-    )
-    row = lax.broadcasted_iota(jnp.int32, chosen_rows.shape, 0)
-    lane = lax.broadcasted_iota(jnp.int32, chosen_rows.shape, 1)
-    for s in range(sequences):
-        positive = positive_ref[s]
-        facts = (margin_ref[s], positive // 128, positive % 128)
-        for place, fact in enumerate(facts):
-            at = (row == 2 * sequences) & (lane == place * sequences + s)
-            chosen_rows = jnp.where(at, fact.astype(jnp.float32), chosen_rows)
-    blocks[grp, rep] = narrow(chosen_rows)
-
-    def to_near(k):
-        mine = blocks.at[grp, rep]
-        return remote(
-            mine, mine, gather_near.at[0, k], gather_near.at[1, k], grp, (rep + k) % reps
-        )
-
-    def to_far(k):
-        line = blocks.at[grp]
-        return remote(
-            line, line, gather_far.at[0, k], gather_far.at[1, k], (grp + k) % groups, rep
-        )
-
-    pl.semaphore_wait(barrier, reps + groups - 2)
-
-    @pl.loop(1, reps)
-    def _(k):
-        to_near(k).start()
-
     for copy in cots:
         copy.wait()
     small[...] = jnp.zeros_like(small)
+    for layer in range(LAYERS):
+        gains[layer, 0:1, :] = wide(norm_gain[layer : layer + 1, :])
+        gains[layer, 1:2, :] = wide(final_gain[layer : layer + 1, :])
 
     @pl.loop(0, total // 96)
     def _(i):
         at = sublanes(i * 96, 96)
         dz[at, :] = wide(dy[at, :])
 
+    first_at = [s * query_len for s in range(sequences)]
+    first_at += [query_rows + s * passage_len for s in range(sequences)]
+    late = sorted({at // norm_step for at in first_at})
+    spans = [span for span in zip([-1] + late, late + [total // norm_step])]
+    load("u2", last).wait()
+
+    def early_norm(low, high):
+        @pl.loop(low, high)
+        def _(tile):
+            last_norm_back(last, tile)
+
+    for low, high in spans[: len(spans) // 2]:
+        if low + 1 < high:
+            early_norm(low + 1, high)
+
     @pl.loop(1, reps)
     def _(k):
         to_near(k).wait_recv()
 
     for k in range(1, groups):
         to_far(k).start()
+
+    for low, high in spans[len(spans) // 2 :]:
+        if low + 1 < high:
+            early_norm(low + 1, high)
+
     for k in range(1, groups):
         to_far(k).wait_recv()
 
-    gathered = blocks[...].reshape(groups * reps * BLOCK, width)
+    gathered = blocks[...].reshape(groups * reps * BLOCK, TILE)
 
     def taken(offset):
         return product(
@@ -984,9 +1079,20 @@
             gathered,
         )
 
-    every_query = narrow(taken(lambda i: i % sequences))
-    every_passage = narrow(taken(lambda i: sequences + i % sequences))
-    facts = taken(lambda i: 2 * sequences)[:, :128]
+    def taken_rows(base):
+        return narrow(
+            jnp.concatenate(
+                [
+                    taken(lambda i: j * firsts_count + base + i % sequences)
+                    for j in range(segments)
+                ],
+                axis=1,
+            )
+        )
+
+    every_query = taken_rows(0)
+    every_passage = taken_rows(sequences)
+    facts = taken(lambda i: segments * firsts_count)[:, :128]
     query_at = lax.broadcasted_iota(jnp.int32, facts.shape, 0) % sequences
     lane_at = lax.broadcasted_iota(jnp.int32, facts.shape, 1)
 
@@ -998,9 +1104,16 @@
     every_positive = fact(1) * 128.0 + fact(2)
     score_scale = 2.0 / math.sqrt(width)
     logits = contract_last(every_query, every_passage) * score_scale
-    columns = lax.broadcasted_iota(jnp.int32, logits.shape, 1).astype(jnp.float32)
-    chosen_mask = columns == every_positive
-    allowed = (cluster_row[...] == cluster_column[...]) | chosen_mask
+    passage_at = lax.broadcasted_iota(jnp.int32, logits.shape, 1).astype(jnp.float32)
+    chosen_mask = passage_at == every_positive
+    clusters = jnp.broadcast_to(cluster_row[...], (everyone, everyone))
+    on_diagonal = lax.broadcasted_iota(jnp.int32, clusters.shape, 0) == (
+        lax.broadcasted_iota(jnp.int32, clusters.shape, 1)
+    )
+    own_clusters = jnp.sum(
+        jnp.where(on_diagonal, clusters.astype(jnp.float32), 0.0), axis=1, keepdims=True
+    )
+    allowed = (clusters.astype(jnp.float32) == own_clusters) | chosen_mask
     masked = jnp.where(allowed, logits, -1e30)
     peak = jnp.max(masked, axis=1, keepdims=True)
     normalizer = peak + jnp.log(jnp.sum(jnp.exp(masked - peak), axis=1, keepdims=True))
@@ -1030,6 +1143,9 @@
                 eight == 0, delta_firsts[place][s : s + 1, :], 0.0
             )
 
+    for tile in late:
+        last_norm_back(last, tile)
+
     def core_copy(t):
         return remote(
             buf.at[t % 2, :, 1 - core],
@@ -1041,7 +1157,7 @@
 
     def side_copy(t):
         return remote(
-            side_out.at[t % 3],
+            side_out.at[t % SENT_SLOTS],
             side_in.at[t % SIDE_SLOTS],
             side_sem.at[0, t],
             side_sem.at[1, t],
@@ -1057,8 +1173,9 @@
             *beside,
         )
 
-    def piece_of(position):
-        return sublanes(near * half_rows + position * piece_rows, piece_rows)
+    def piece_of(place):
+        order = 2 * (place % 2) + place // 2
+        return sublanes(near * half_rows + order * piece_rows, piece_rows)
 
     def deep_copy(t, k):
         return remote(
@@ -1071,25 +1188,48 @@
 
     def chunk_place(t):
         step, part = t // PARTS, t % PARTS
-        return (part // 2) * 4 + (last - step) * 2 + part % 2
-
-    def back_copy(t, k):
+        return (part // 4) * 8 + (last - step) * 4 + part % 4
+
+    def own_piece(t):
+        return out_ref.at[
+            chunk_place(t), near, deep_low, sublanes(deep_high * piece_rows, piece_rows)
+        ]
+
+    def local_copy(t):
+        return pltpu.make_async_copy(piece.at[t], own_piece(t), local_sem.at[t])
+
+    def back_copy(stage, source, peer, t, target=None):
         return remote(
-            piece.at[t],
-            out_ref.at[chunk_place(t), piece_of(deep)],
-            back_send.at[k - 1, t],
-            back_recv.at[k - 1, t],
-            *behind(k),
-        )
-
-    def local_copy(t):
-        return pltpu.make_async_copy(
-            piece.at[t], out_ref.at[chunk_place(t), piece_of(deep)], local_sem.at[t]
-        )
-
-    def last_copy(t):
-        half = out_ref.at[chunk_place(t), sublanes(near * half_rows, half_rows)]
-        return remote(half, half, last_sem.at[0, t], last_sem.at[1, t], *beside)
+            source,
+            source if target is None else target,
+            back_sem.at[0, stage, t],
+            back_sem.at[1, stage, t],
+            *peer,
+        )
+
+    def back_high(t):
+        return back_copy(0, piece.at[t], beyond, t, own_piece(t))
+
+    def even_second(t):
+        return back_copy(1, out_ref.at[chunk_place(t), near, deep_low], next_to, t)
+
+    def even_third(t):
+        return back_copy(2, out_ref.at[chunk_place(t), near], beside, t)
+
+    def odd_second(t):
+        return back_copy(1, out_ref.at[chunk_place(t), near, deep_low], beside, t)
+
+    def odd_third(t):
+        return back_copy(2, out_ref.at[chunk_place(t), :, deep_low], next_to, t)
+
+    def by_parity(t, even, odd):
+        @pl.when(t % 2 == 0)
+        def _():
+            even(t)
+
+        @pl.when(t % 2 == 1)
+        def _():
+            odd(t)
 
     def add_rows(target, former, latter, count):
         step = 48
@@ -1106,7 +1246,7 @@
         core_copy(t).wait()
         slot = t % CORE_SLOTS
         add_rows(
-            (side_out.at[t % 3], 0),
+            (side_out.at[t % SENT_SLOTS], 0),
             (buf.at[t % 2, 1 - side, core], 0),
             (core_in.at[slot, 1 - side], 0),
             rows,
@@ -1167,43 +1307,23 @@
             summed = summed + wide(deep_in[t, k - 1])
         piece[t] = narrow(summed)
         local_copy(t).start()
-        for k in range(1, depth):
-            back_copy(t, k).start()
-
-    def after_back(t):
+        back_high(t).start()
+
+    def after_high(t):
         local_copy(t).wait()
-        for k in range(1, depth):
-            back_copy(t, k).wait_recv()
-        last_copy(t).start()
-
-    def tally(layer, row_at, columns, values):
-        at = (layer, pl.ds(row_at, 1), columns)
-        small[at] = small[at] + jnp.sum(values, axis=0, keepdims=True)
-
-    every_lane = pl.ds(0, width)
-
-    def norm_back(layer, unit_at, scale_lane, gain_row, target, gain_to, shift_to, bias_to):
-        step = 48
-        gain = vec_ref[layer, pl.ds(gain_row, 1), :]
-
-        @pl.loop(0, total // step)
-        def _(i):
-            at = sublanes(i * step, step)
-            upstream = dz[at, :]
-            unit_rows = wide(unit[unit_at, at, :])
-            scaled = r[layer, at, scale_lane : scale_lane + 1]
-            delta_unit = upstream * gain
-            delta = scaled * (
-                delta_unit
-                - jnp.mean(delta_unit, axis=-1, keepdims=True)
-                - unit_rows * jnp.mean(delta_unit * unit_rows, axis=-1, keepdims=True)
-            )
-            dz[at, :] = delta
-            rounded = narrow(delta)
-            target[at, :] = rounded
-            tally(layer, gain_to, every_lane, upstream * unit_rows)
-            tally(layer, shift_to, every_lane, upstream)
-            tally(layer, bias_to, every_lane, wide(rounded))
+        back_high(t).wait()
+        by_parity(t, lambda t: even_second(t).start(), lambda t: odd_second(t).start())
+
+    def after_second(t):
+        def even(t):
+            even_second(t).wait()
+            even_third(t).start()
+
+        def odd(t):
+            odd_second(t).wait()
+            odd_third(t).start()
+
+        by_parity(t, even, odd)
 
     def expand_back(layer, slot):
         tiles = width // TILE
@@ -1248,7 +1368,7 @@
         weighed = shares * delta
         return narrow(weighed - shares * jnp.sum(weighed, axis=0, keepdims=True))
 
-    def attention_back(layer):
+    def query_attention_back(layer):
         query_span = pl.ds(0, query_rows)
         q2, k2, v2 = quad[0, query_span, :], quad[1, query_span, :], quad[2, query_span, :]
 
@@ -1277,7 +1397,8 @@
         tally(layer, S_QUERY, every_lane, wide(delta_query))
         tally(layer, S_VALUE, every_lane, wide(delta_value))
 
-        @pl.loop(0, sequences * pairs)
+    def passage_attention_back(layer, low, high):
+        @pl.loop(low, high)
         def _(i):
             s, pair = i // pairs, i % pairs
             at_rows = sublanes(query_rows + s * passage_len, passage_len)
@@ -1303,44 +1424,40 @@
             tally(layer, S_VALUE, at, wide(delta_value))
 
     def make_terms(t, part):
-        tall = part < 2
-
-        @pl.when(tall)
+        pair, half = (part % 4) // 2, lanes((part % 2) * columns, columns)
+
+        @pl.when(part < 4)
         def _():
             @pl.loop(0, 4)
             def _(i):
-                columns = lanes(i * width + part * rows, rows)
-                buf[t % 2, i // 2, i % 2] = narrow(contract_rows(active[:, columns], dy[...]))
+                taller = active[:, lanes(i * width + pair * rows, rows)]
+                buf[t % 2, i // 2, i % 2] = narrow(contract_rows(taller, dy[:, half]))
 
         def split(i, terms):
-            unit_at, half = i // 2, i % 2
-            place = sublanes(unit_at * quarter, quarter)
+            place = sublanes((i // 2) * quarter, quarter)
             terms = narrow(terms)
-            buf[t % 2, half, 0, place, :] = terms[:quarter]
-            buf[t % 2, half, 1, place, :] = terms[quarter:]
-
-        @pl.when((part == 2) | (part == 3))
+            buf[t % 2, i % 2, 0, place, :] = terms[:quarter]
+            buf[t % 2, i % 2, 1, place, :] = terms[quarter:]
+
+        def two_quarters(i):
+            return lanes((i % 2) * 2 * quarter, 2 * quarter)
+
+        @pl.when((part >= 4) & (part < 8))
         def _():
             @pl.loop(0, 4)
             def _(i):
-                columns = lanes((2 * (part - 2) + i // 2) * width, width)
+                wider = du[:, lanes((2 * pair + i // 2) * width + (part % 2) * columns, columns)]
+                split(i, contract_rows(middle[:, two_quarters(i)], wider))
+
+        @pl.when(part >= 8)
+        def _():
+            @pl.loop(0, 4)
+            def _(i):
+                which = 2 * pair + i // 2
                 split(
                     i,
                     contract_rows(
-                        middle[:, lanes((i % 2) * 2 * quarter, 2 * quarter)], du[:, columns]
-                    ),
-                )
-
-        @pl.when(part >= 4)
-        def _():
-            @pl.loop(0, 4)
-            def _(i):
-                which = 2 * (part - 4) + i // 2
-                split(
-                    i,
-                    contract_rows(
-                        pair_in[which // 3, :, lanes((i % 2) * 2 * quarter, 2 * quarter)],
-                        quad[which],
+                        pair_in[which // 3, :, two_quarters(i)], quad[which, :, half]
                     ),
                 )
 
@@ -1365,7 +1482,7 @@
             pltpu.make_async_copy(dz.at[passage_rows], passage_grad, first_sem.at[5]),
         )
 
-    @pl.loop(0, CHUNKS + 5)
+    @pl.loop(0, CHUNKS + LAGS[-1])
     def _(t):
         step, part = t // PARTS, t % PARTS
         layer = last - step
@@ -1384,42 +1501,39 @@
                 for name in ("c", "q", "k", "v", "x"):
                     load(name, layer).start()
 
-            load("u2", layer).wait()
-            norm_back(layer, 0, 1, V_LAST_GAIN, dy, S_LAST_GAIN, S_LAST_SHIFT, S_REDUCE)
+                load("u2", layer).wait()
+
+                @pl.loop(0, total // norm_step)
+                def _(tile):
+                    last_norm_back(layer, tile)
+
             load("f", layer).wait()
 
         @pl.when(busy & (part == 4))
+        def _():
+            load("m", layer).wait()
+
+        @pl.when(busy & (part == 8))
+        def _():
+            for name in ("c", "x"):
+                load(name, layer).wait()
+
+        @pl.when(busy)
+        def _():
+            make_terms(t, part)
+
+        @pl.when(busy & (part == 1))
         def _():
             @pl.when(more)
             def _():
-                for name in ("slope", "m", "u1"):
-                    load(name, layer - 1).start()
-
-            for name in ("c", "q", "k", "v", "pt", "ptq", "x"):
-                load(name, layer).wait()
-            attention_back(layer)
-
-        @pl.when(busy & (part == 2))
-        def _():
-            load("m", layer).wait()
-
-        @pl.when(busy)
-        def _():
-            make_terms(t, part)
-
-        @pl.when(busy & (part == 1))
-        def _():
-            @pl.when(more)
-            def _():
-                for name in ("u2", "f"):
-                    load(name, layer - 1).start()
+                load("u2", layer - 1).start()
 
             load("slope", layer).wait()
             wait_weights(0, layer, slot)
             expand_back(layer, slot)
             start_weights(2, layer, slot)
 
-        @pl.when(busy & (part == 3))
+        @pl.when(busy & (part == 2))
         def _():
             wait_weights(1, layer, 1 - slot)
             middle_back(1 - slot)
@@ -1428,16 +1542,47 @@
             def _():
                 start_weights(0, layer - 1, 1 - slot)
 
+        @pl.when(busy & (part == 3))
+        def _():
             load("u1", layer).wait()
-            norm_back(layer, 1, 0, V_GAIN, quad.at[3], S_GAIN, S_SHIFT, S_MIX)
+
+            @pl.loop(0, total // norm_step)
+            def _(tile):
+                first_norm_back(layer, tile)
+
             wait_weights(2, layer, slot)
             context_back(slot)
 
-        @pl.when(busy & (part == 5))
-        def _():
             @pl.when(more)
             def _():
-                for name in ("pt", "ptq"):
+                for name in ("f", "u1"):
+                    load(name, layer - 1).start()
+
+        @pl.when(busy & (part == 4))
+        def _():
+            for name in ("q", "k", "v", "pt", "ptq"):
+                load(name, layer).wait()
+            query_attention_back(layer)
+
+        passages = sequences * pairs
+
+        @pl.when(busy & (part == 5))
+        def _():
+            passage_attention_back(layer, 0, passages // 3)
+
+        @pl.when(busy & (part == 6))
+        def _():
+            passage_attention_back(layer, passages // 3, 2 * passages // 3)
+
+        @pl.when(busy & (part == 7))
+        def _():
+            passage_attention_back(layer, 2 * passages // 3, passages)
+
+        @pl.when(busy & (part == 8))
+        def _():
+            @pl.when(more)
+            def _():
+                for name in ("pt", "ptq", "slope", "m"):
                     load(name, layer - 1).start()
 
             hidden_back(slot)
@@ -1451,11 +1596,11 @@
                 for copy in gradients_out():
                     copy.start()
 
-        for lag, stage in enumerate((after_side, after_near, after_deep, after_back)):
-
-            @pl.when((t > lag + 1) & (t < CHUNKS + lag + 2))
+        for lag, stage in zip(LAGS, (after_side, after_near, after_deep, after_high, after_second)):
+
+            @pl.when((t >= lag) & (t < CHUNKS + lag))
             def _():
-                stage(t - lag - 2)
+                stage(t - lag)
 
         for place, (target, peer, came) in enumerate(
             (
@@ -1465,22 +1610,22 @@
             )
         ):
 
-            @pl.when(t == CHUNKS - 1 + place)
+            @pl.when(t == SMALL_AT + place)
             def _():
                 small_move(place, target, peer).start()
 
-            @pl.when(t == CHUNKS + place)
+            @pl.when(t == SMALL_AT + 1 + place)
             def _():
                 small_move(place, target, peer).wait()
                 small[...] = small[...] + came[...]
 
-        @pl.when(t == CHUNKS + 2)
+        @pl.when(t == SMALL_AT + 3)
         def _():
             small_deep[deep] = small[...]
             for k in range(1, depth):
                 small_to_deep(k).start()
 
-        @pl.when(t == CHUNKS + 4)
+        @pl.when(t == SMALL_AT + 5)
         def _():
             for k in range(1, depth):
                 small_to_deep(k).wait()
@@ -1491,9 +1636,7 @@
 
     @pl.loop(0, CHUNKS)
     def _(t):
-        for k in range(1, depth):
-            back_copy(t, k).wait_send()
-        last_copy(t).wait()
+        by_parity(t, lambda t: even_third(t).wait(), lambda t: odd_third(t).wait())
 
     for copy in gradients_out():
         copy.wait()
@@ -1510,7 +1653,8 @@
     margin_bin,
     positive_index,
     cluster_index,
-    vectors,
+    norm_gain,
+    final_gain,
     query_output,
     passage_output,
     query_cotangent,
@@ -1534,10 +1678,11 @@
     smem = pl.BlockSpec(memory_space=pltpu.SMEM)
     small_shape = (LAYERS, 16, width)
     pt_shape, ptq_shape = stored[4].shape[1:], stored[5].shape[1:]
+    columns = width // 2
     return pl.pallas_call(
         backward_kernel,
         out_shape=(
-            jax.ShapeDtypeStruct((CHUNKS, rows, width), bf16),
+            jax.ShapeDtypeStruct((CHUNKS, 2, 2, rows // 4, columns), bf16),
             jax.ShapeDtypeStruct(small_shape, f32),
             jax.ShapeDtypeStruct((8, 128), f32),
             jax.ShapeDtypeStruct((query_rows, width), f32),
@@ -1546,21 +1691,22 @@
         in_specs=[smem, smem, vmem, vmem, vmem] + [anywhere] * 23,
         out_specs=(anywhere, vmem, vmem, anywhere, anywhere),
         scratch_shapes=[
-            pltpu.VMEM((2, 2, 2, rows, width), bf16),
-            pltpu.VMEM((KEEP_SLOTS, rows, width), bf16),
-            pltpu.VMEM((3, rows, width), bf16),
-            pltpu.VMEM((CORE_SLOTS, 2, rows, width), bf16),
-            pltpu.VMEM((SIDE_SLOTS, rows, width), bf16),
-            pltpu.VMEM((NEAR_SLOTS, rows // 2, width), bf16),
-            pltpu.VMEM((CHUNKS, depth - 1, piece_rows, width), bf16),
-            pltpu.VMEM((CHUNKS, piece_rows, width), bf16),
+            pltpu.VMEM((2, 2, 2, rows, columns), bf16),
+            pltpu.VMEM((KEEP_SLOTS, rows, columns), bf16),
+            pltpu.VMEM((SENT_SLOTS, rows, columns), bf16),
+            pltpu.VMEM((CORE_SLOTS, 2, rows, columns), bf16),
+            pltpu.VMEM((SIDE_SLOTS, rows, columns), bf16),
+            pltpu.VMEM((NEAR_SLOTS, rows // 2, columns), bf16),
+            pltpu.VMEM((CHUNKS, depth - 1, piece_rows, columns), bf16),
+            pltpu.VMEM((CHUNKS, piece_rows, columns), bf16),
             pltpu.VMEM(small_shape, f32),
             pltpu.VMEM(small_shape, f32),
             pltpu.VMEM(small_shape, f32),
             pltpu.VMEM(small_shape, f32),
             pltpu.VMEM((depth,) + small_shape, f32),
             pltpu.VMEM((2 * sequences * BLOCK, width), bf16),
-            pltpu.VMEM((groups, reps, BLOCK, width), bf16),
+            pltpu.VMEM((groups, reps, BLOCK, TILE), bf16),
+            pltpu.VMEM((LAYERS, 8, width), f32),
             pltpu.VMEM((total, width), f32),
             pltpu.VMEM((total, width), bf16),
             pltpu.VMEM((total, 4 * width), bf16),
@@ -1585,10 +1731,8 @@
             dma((2, CHUNKS)),
             dma((depth - 1, CHUNKS)),
             dma((depth - 1, CHUNKS)),
-            dma((depth - 1, CHUNKS)),
-            dma((depth - 1, CHUNKS)),
+            dma((2, 3, CHUNKS)),
             dma((CHUNKS,)),
-            dma((2, CHUNKS)),
             dma((6,)),
             dma((depth - 1,)),
             dma((depth - 1,)),
@@ -1603,8 +1747,8 @@
         margin_bin,
         positive_index,
         cluster_index.reshape(1, everyone),
-        cluster_index.reshape(everyone, 1),
-        vectors,
+        norm_gain,
+        final_gain,
         query_output,
         passage_output,
         query_cotangent.reshape(query_rows, width),
@@ -1700,21 +1844,139 @@
     return query_loss, upstream[:query_span], upstream[query_span:], reduced
 
 
-def unpack_gradients(out, small):
-    width = out.shape[2]
-    quarter = width // 4
-    blocks = out.reshape(3, LAYERS, 4, quarter, width)
+def finish_kernel(
+    out_ref,
+    small_in,
+    loss_in,
+    query_in,
+    passage_in,
+    reduce_out,
+    expand_out,
+    *rest,
+):
+    square_outs = rest[:4]
+    vector_outs = rest[4:12]
+    expand_bias_out, query_out, passage_out, loss_out = rest[12:16]
+    sums, tall, flat, squares, query, passage, small_ref, loss, in_sem, out_sem = rest[16:]
+    rows, columns = sums.shape[1:]
+    quarter = rows // 2
+    width = 2 * columns
+    each = sums.shape[0] // (3 * LAYERS)
+    moves = [
+        pltpu.make_async_copy(query_in, query, in_sem.at[3 * LAYERS]),
+        pltpu.make_async_copy(passage_in, passage, in_sem.at[3 * LAYERS + 1]),
+    ]
+    little = [
+        pltpu.make_async_copy(small_in, small_ref, in_sem.at[3 * LAYERS + 2]),
+        pltpu.make_async_copy(loss_in, loss, in_sem.at[3 * LAYERS + 3]),
+    ]
+    loads = []
+    for i in range(3 * LAYERS):
+        span = pl.ds(i * each, each)
+        loads.append(pltpu.make_async_copy(out_ref.at[span], sums.at[span], in_sem.at[i]))
+    for copy in little + loads + moves:
+        copy.start()
+    for copy in little:
+        copy.wait()
+    for i in range(loss_out.shape[0]):
+        loss_out[i] = jnp.sum(loss[0:1, i : i + 1])
+    group = lax.axis_index("grp")
+    vectors = small_ref[:, :8, 0:quarter]
+    expand_bias = small_ref[:, S_EXPAND, :]
+    for g in range(1, 4):
+        vectors = jnp.where(
+            group == g, small_ref[:, :8, g * quarter : (g + 1) * quarter], vectors
+        )
+        expand_bias = jnp.where(group == g, small_ref[:, S_EXPAND + g, :], expand_bias)
+    for i in range(8):
+        vector_outs[i][...] = vectors[:, i, :]
+    expand_bias_out[...] = expand_bias
+    stores = []
+
+    def store(source, target):
+        copy = pltpu.make_async_copy(source, target, out_sem.at[len(stores)])
+        stores.append(copy)
+        copy.start()
+
+    for layer in range(LAYERS):
+        loads[layer].wait()
+        for part in range(4):
+            at = pl.ds((part // 2) * rows, rows), pl.ds((part % 2) * columns, columns)
+            tall[layer, at[0], at[1]] = wide(sums[layer * each + part])
+        store(tall.at[layer], reduce_out.at[layer])
+    for move, (source, target) in zip(moves, ((query, query_out), (passage, passage_out))):
+        move.wait()
+        store(source, target)
+    for layer in range(LAYERS):
+        loads[LAYERS + layer].wait()
+        for part in range(4):
+            value = wide(sums[(LAYERS + layer) * each + part])
+            for unit in range(2):
+                start = (2 * (part // 2) + unit) * width + (part % 2) * columns
+                flat[layer, :, start : start + columns] = value[
+                    unit * quarter : (unit + 1) * quarter
+                ]
+        store(flat.at[layer], expand_out.at[layer])
+    for layer in range(LAYERS):
+        loads[2 * LAYERS + layer].wait()
+        for part in range(4):
+            value = wide(sums[(2 * LAYERS + layer) * each + part])
+            for unit in range(2):
+                at = pl.ds((part % 2) * columns, columns)
+                squares[2 * (part // 2) + unit, layer, :, at] = value[
+                    unit * quarter : (unit + 1) * quarter
+                ]
+        for which in range(4):
+            store(squares.at[which, layer], square_outs[which].at[layer])
+    for copy in stores:
+        copy.wait()
+
+
+def finish(out, small, loss, query_gradient, passage_gradient, sequences):
+    out = out.reshape(out.shape[0], -1, out.shape[-1])
+    rows, columns = out.shape[1:]
+    quarter, width = rows // 2, 2 * columns
+    f32 = jnp.float32
+    anywhere = pl.BlockSpec(memory_space=pl.ANY)
+    vmem = pl.BlockSpec(memory_space=pltpu.VMEM)
+    tall, flat = (LAYERS, width, width), (LAYERS, quarter, 4 * width)
+    square, vector = (LAYERS, quarter, width), (LAYERS, quarter)
+    results = pl.pallas_call(
+        finish_kernel,
+        out_shape=[
+            jax.ShapeDtypeStruct(shape, f32)
+            for shape in [tall, flat]
+            + [square] * 4
+            + [vector] * 8
+            + [(LAYERS, width), query_gradient.shape, passage_gradient.shape, (sequences,)]
+        ],
+        in_specs=[anywhere] * 5,
+        out_specs=[anywhere] * 6
+        + [vmem] * 9
+        + [anywhere] * 2
+        + [pl.BlockSpec(memory_space=pltpu.SMEM)],
+        scratch_shapes=[
+            pltpu.VMEM(out.shape, jnp.bfloat16),
+            pltpu.VMEM(tall, f32),
+            pltpu.VMEM(flat, f32),
+            pltpu.VMEM((4,) + square, f32),
+            pltpu.VMEM(query_gradient.shape, f32),
+            pltpu.VMEM(passage_gradient.shape, f32),
+            pltpu.VMEM(small.shape, f32),
+            pltpu.VMEM(loss.shape, f32),
+            pltpu.SemaphoreType.DMA((3 * LAYERS + 4,)),
+            pltpu.SemaphoreType.DMA((6 * LAYERS + 2,)),
+        ],
+        compiler_params=pltpu.CompilerParams(vmem_limit_bytes=60 * 1024 * 1024),
+    )(out, small, loss, query_gradient, passage_gradient)
     reduced = [None] * 15
-    reduced[11] = wide(blocks[0].reshape(LAYERS, width, width))
-    reduced[9] = wide(jnp.swapaxes(blocks[1], 1, 2).reshape(LAYERS, quarter, 4 * width))
+    reduced[11], reduced[9] = results[0], results[1]
     for place, slot in enumerate((0, 2, 3, 5)):
-        reduced[slot] = wide(blocks[2, :, place])
-    group = lax.axis_index("grp")
-    narrow_rows = lax.dynamic_slice_in_dim(small[:, :8], group * quarter, quarter, axis=2)
+        reduced[slot] = results[2 + place]
     for place, slot in enumerate((1, 4, 6, 7, 8, 12, 13, 14)):
-        reduced[slot] = narrow_rows[:, place]
-    reduced[10] = lax.dynamic_index_in_dim(small, S_EXPAND + group, 1, keepdims=False)
-    return reduced
+        reduced[slot] = results[6 + place]
+    reduced[10] = results[14]
+    return results[15], results[16], results[17], reduced
 
 
 def per_device(
@@ -1763,7 +2025,7 @@
     batch_size, query_len, model_width = query_input.shape
     passage_len = passage_input.shape[1]
     matrices = (query_weight, key_weight, value_weight, mix_weight, expand_weight, reduce_weight)
-    vectors = pack_vectors(
+    vectors = (
         query_bias,
         value_bias,
         mix_bias,
@@ -1775,7 +2037,8 @@
         expand_bias,
     )
     results = run_forward(
-        jnp.concatenate([query_length, passage_length]),
+        query_length,
+        passage_length,
         query_input,
         passage_input,
         matrices,
@@ -1800,7 +2063,8 @@
             margin_bin,
             positive_index,
             cluster_index,
-            vectors,
+            norm_gain,
+            final_gain,
             results[0],
             results[1],
             query_cotangent,
@@ -1808,8 +2072,9 @@
             matrices,
             results[2:],
         )
-        query_loss = loss[0, :batch_size]
-        reduced = unpack_gradients(out, small)
+        query_gradient, passage_gradient, query_loss, reduced = finish(
+            out, small, loss, query_gradient, passage_gradient, batch_size
+        )
     return (
         query_output,
         passage_output,

time: 334 us -> 286 us (0.86)
  local copies, waits for them, and re-layouts: 20.3 us -> 0 us
  Pallas kernels: 303 us -> 285 us
  other arithmetic: 8.86 us -> 0 us
    pallas_call x1, Pallas kernels: 240 us -> 213 us  [run_backward(): pl.pallas_call(backward_kernel, out_shape=(jax.ShapeDtypeStruct((CHUNKS,...]
    pallas_call x0 -> x1, Pallas kernels: none -> 10.3 us  [finish(): pl.pallas_call(finish_kernel, out_shape=[jax.ShapeDtypeStruct(shape, f32)...]
    convert_element_type x3 -> x0, other arithmetic: 7.19 us -> none  [the longest x2 6.54 us: wide(): return values.astype(jnp.float32)]
    another operation x8 -> x0, local copies, waits for them, and re-layouts: 5.51 us -> none  [pack_vectors(): jnp.stack(rows, axis=1)]
    unnamed x13 -> x0, local copies, waits for them, and re-layouts: 4.77 us -> none
    slice x3 -> x0, local copies, waits for them, and re-layouts: 3.59 us -> none  [the longest x1 2.68 us: unpack_gradients(): reduced[11] = wide(blocks[0].reshape(LAYERS, width, width))]
where the time goes in v3:
time: 286 us
  Pallas kernels  285 us (100%)
    pallas_call x1, Pallas kernels, run_backward(): pl.pallas_call(backward_kernel, out_shape=(jax.ShapeDtypeStruct((CHUNKS,...  213 us
    pallas_call x1, Pallas kernels, run_forward(): pl.pallas_call(forward_kernel, out_shape=(jax.ShapeDtypeStruct((query_row...  61.7 us
    pallas_call x1, Pallas kernels, finish(): pl.pallas_call(finish_kernel, out_shape=[jax.ShapeDtypeStruct(shape, f32)...  10.3 us

profile of v3, /device:TPU:0, one launch (start us, length us, event | category | flops | bytes accessed | tf_op | source)
XLA Modules:
  0.0 285.7 jit_solution(13921973424400306335)
XLA Ops:
  0.7 61.7 %shard_map.383 = (bf16[64,768]{1,0:T(8,128)(2,1)}, bf16[512,768]{1,0:T(8,128)(2,1)}, bf16[2,576,768]{2,1,0:T(8,128)(2,1)}, bf16[2,576,768]{2,1,0:T(8,128)(2,1)},...) custom-call(s32[2]{0:T(128)} %query_lengths.1, ...), custom_call_target="tpu_custom_call" | custom-call | tf_op jit(solution)/shard_map/pallas_call | solution.py:707
  62.3 213.0 %shard_map.384 = (bf16[24,2,2,96,384]{4,3,2,1,0:T(8,128)(2,1)}, f32[2,16,768]{2,1,0:T(8,128)}, f32[8,128]{1,0:T(8,128)}, f32[64,768]{1,0:T(8,128)}, f32[512,768]{1,0:T(8,128)}) custom-call(s32[2]{0:T(128)} %margin_ref.1, s32[2]{0:T(128)} %positive_ref.1, s32[1,64]{1,0:T(1,128)} %bitcast.17, bf16[2,768]{1,0:T(2,128)(2,1)} %norm_gain.3, ...), custom_call_target="tpu_custom_call" | custom-call | tf_op jit(solution)/shard_map/pallas_call | solution.py:1682
  275.3 10.3 %shard_map.385 = (f32[2,768,768]{2,1,0:T(8,128)}, f32[2,192,3072]{2,1,0:T(8,128)}, f32[2,192,768]{2,1,0:T(8,128)}, f32[2,192,768]{2,1,0:T(8,128)}, f32[2,192,768...) custom-call(bf16[24,384,384]{2,1,0:T(8,128)(2,1)} %bitcast.10, ...), custom_call_target="tpu_custom_call" | custom-call | tf_op jit(solution)/shard_map/pallas_call | solution.py:1944

commit v4 on v3

--- a/solution.py
+++ b/solution.py
@@ -127,7 +127,8 @@
     scale_one, scale_two = scales[:, 0:1], scales[:, 1:2]
     unit_one, unit_two = wide(unit_one), wide(unit_two)
     (count, query_len), (_, passage_len) = layout
-    pair_shares = shares.reshape(count, HEADS // 2, passage_len, 2, passage_len)
+    pair_shares = jnp.pad(shares, ((0, 0), (0, passage_len - shares.shape[1]), (0, 0)))
+    pair_shares = pair_shares.reshape(count, HEADS // 2, passage_len, 2, passage_len)
     pair_shares = pair_shares.transpose(0, 1, 3, 4, 2).reshape(
         count, HEADS, passage_len, passage_len
     )
@@ -380,6 +381,10 @@
 def head_mask(head, width):
     lane = lax.broadcasted_iota(jnp.int32, (1, width), 1)
     return ((lane >= head * DH) & (lane < (head + 1) * DH))
+
+
+def live_keys(passage_len):
+    return -(-(passage_len * 25 // 32) // 16) * 16
 
 
 def lanes(start, size=TILE):
@@ -464,6 +469,7 @@
     query_len = query_rows // sequences
     passage_len = (total - query_rows) // sequences
     pairs = width // (2 * DH)
+    kept = live_keys(passage_len)
 
     weights = ((wq_in, wq), (wk_in, wk), (wv_in, wv), (wm_in, wm), (we_in, we), (wr_in, wr))
 
@@ -505,9 +511,8 @@
     )
     first.start()
     rest.start()
-    for layer in range(LAYERS):
-        for which in range(6):
-            weight_copy(which, layer).start()
+    for which in range(3):
+        weight_copy(which, 0).start()
     vectors = (
         query_bias,
         value_bias,
@@ -529,7 +534,7 @@
     rest.wait()
 
     def project(source, weight, layer, bias_row, target):
-        @pl.loop(0, width // TILE)
+        @pl.loop(0, width // TILE, unroll=3)
         def _(i):
             value = product(source[...], weight[layer, :, lanes(i * TILE)])
             if bias_row is not None:
@@ -541,7 +546,7 @@
         gain = vec_ref[layer, pl.ds(gain_row, 1), :]
         shift = vec_ref[layer, pl.ds(shift_row, 1), :]
 
-        @pl.loop(0, total // step)
+        @pl.loop(0, total // step, unroll=2)
         def _(i):
             at = sublanes(i * step, step)
             full, unit_rows, scaled = norm_forward(z[at, :], gain, shift)
@@ -553,6 +558,12 @@
     def _(layer):
         store(X, layer).start()
         weight_copy(0, layer).wait()
+
+        @pl.when(layer == 0)
+        def _():
+            for which in range(3, 6):
+                weight_copy(which, 0).start()
+
         reuse(Q, layer)
         project(x, wq, layer, V_QUERY, q)
         store(Q, layer).start()
@@ -594,15 +605,17 @@
             )
         c[:query_rows, :] = narrow(context)
 
-        @pl.loop(0, sequences * pairs)
+        @pl.loop(0, sequences * pairs, unroll=3)
         def _(i):
             s, pair = i // pairs, i % pairs
             rows = sublanes(query_rows + s * passage_len, passage_len)
             at = lanes(pair * 2 * DH, 2 * DH)
+            key_rows = sublanes(query_rows + s * passage_len, kept)
             even, odd = lane_masks(passage_len)
-            q2, k2, v2 = q[rows, at], k[rows, at], v[rows, at]
+            q2, k2, v2 = q[rows, at], k[key_rows, at], v[key_rows, at]
             scores = contract_last(k2, jnp.concatenate([q2 * even, q2 * odd], axis=0))
-            slot = lax.broadcasted_iota(jnp.int32, (passage_len, 1), 0)
+            even, odd = even[:kept], odd[:kept]
+            slot = lax.broadcasted_iota(jnp.int32, (kept, 1), 0)
             shares = softmax_rows(
                 scores, jnp.where(slot < passage_lengths[s], 0.0, -1e30)
             )
@@ -616,6 +629,11 @@
         store(C, layer).start()
 
         weight_copy(3, layer).wait()
+
+        @pl.when(layer + 1 < LAYERS)
+        def _():
+            for which in range(6):
+                weight_copy(which, layer + 1).start()
 
         @pl.loop(0, width // TILE)
         def _(i):
@@ -637,7 +655,7 @@
         reuse(SLOPE, layer)
         reuse(F, layer)
 
-        @pl.loop(0, 4 * width // TILE)
+        @pl.loop(0, 4 * width // TILE, unroll=2)
         def _(i):
             at = lanes(i * TILE)
             tiles = width // TILE
@@ -693,7 +711,7 @@
         ((total, width), bf16),
         ((total, width), bf16),
         ((total, width), bf16),
-        ((sequences * pairs, passage_len, 2 * passage_len), bf16),
+        ((sequences * pairs, live_keys(passage_len), 2 * passage_len), bf16),
         ((query_rows, HEADS * query_rows), bf16),
         ((total, width), bf16),
         ((total, width), bf16),
@@ -740,7 +758,8 @@
 PARTS = 12
 S_QUERY, S_VALUE, S_MIX, S_GAIN, S_SHIFT, S_REDUCE, S_LAST_GAIN, S_LAST_SHIFT, S_EXPAND = range(9)
 CORE_SLOTS, SIDE_SLOTS, NEAR_SLOTS, KEEP_SLOTS, SENT_SLOTS = 4, 4, 4, 6, 3
-LAGS = (2, 3, 4, 5, 6)
+TURNS = 8
+LAGS = (2, 3, 4, 5, 6, 9)
 BLOCK = 16
 SMALL_AT = 21
 
@@ -847,6 +866,7 @@
     query_len = query_rows // sequences
     passage_len = (total - query_rows) // sequences
     pairs = width // (2 * DH)
+    live = live_keys(passage_len)
     passage_rows = pl.ds(query_rows, total - query_rows)
     everyone = cluster_row.shape[1]
 
@@ -940,8 +960,7 @@
     ]
     for copy in cots:
         copy.start()
-    for name in ("u2", "f"):
-        load(name, last).start()
+    load("u2", last).start()
 
     def tally(layer, row_at, lanes_at, values):
         at = (layer, pl.ds(row_at, 1), lanes_at)
@@ -1022,10 +1041,9 @@
     def _(k):
         to_near(k).start()
 
+    load("f", last).start()
+    load("slope", last).start()
     start_weights(0, last, 0)
-    for name in ("slope", "m", "u1", "c", "q", "k", "v", "pt", "ptq", "x"):
-        load(name, last).start()
-    start_weights(1, last, 1)
 
     for copy in cots:
         copy.wait()
@@ -1150,8 +1168,8 @@
         return remote(
             buf.at[t % 2, :, 1 - core],
             core_in.at[t % CORE_SLOTS],
-            core_sem.at[0, t],
-            core_sem.at[1, t],
+            core_sem.at[0, t % CORE_SLOTS],
+            core_sem.at[1, t % CORE_SLOTS],
             *sibling,
         )
 
@@ -1159,8 +1177,8 @@
         return remote(
             side_out.at[t % SENT_SLOTS],
             side_in.at[t % SIDE_SLOTS],
-            side_sem.at[0, t],
-            side_sem.at[1, t],
+            side_sem.at[0, t % SIDE_SLOTS],
+            side_sem.at[1, t % SIDE_SLOTS],
             *across,
         )
 
@@ -1168,8 +1186,8 @@
         return remote(
             keep.at[t % KEEP_SLOTS, sublanes((1 - near) * half_rows, half_rows)],
             near_in.at[t % NEAR_SLOTS],
-            near_sem.at[0, t],
-            near_sem.at[1, t],
+            near_sem.at[0, t % NEAR_SLOTS],
+            near_sem.at[1, t % NEAR_SLOTS],
             *beside,
         )
 
@@ -1180,9 +1198,9 @@
     def deep_copy(t, k):
         return remote(
             keep.at[t % KEEP_SLOTS, piece_of((deep + k) % depth)],
-            deep_in.at[t, k - 1],
-            deep_send.at[k - 1, t],
-            deep_recv.at[k - 1, t],
+            deep_in.at[t % TURNS, k - 1],
+            deep_send.at[k - 1, t % TURNS],
+            deep_recv.at[k - 1, t % TURNS],
             *behind(k),
         )
 
@@ -1196,19 +1214,19 @@
         ]
 
     def local_copy(t):
-        return pltpu.make_async_copy(piece.at[t], own_piece(t), local_sem.at[t])
+        return pltpu.make_async_copy(piece.at[t % TURNS], own_piece(t), local_sem.at[t % TURNS])
 
     def back_copy(stage, source, peer, t, target=None):
         return remote(
             source,
             source if target is None else target,
-            back_sem.at[0, stage, t],
-            back_sem.at[1, stage, t],
+            back_sem.at[0, stage, t % TURNS],
+            back_sem.at[1, stage, t % TURNS],
             *peer,
         )
 
     def back_high(t):
-        return back_copy(0, piece.at[t], beyond, t, own_piece(t))
+        return back_copy(0, piece.at[t % TURNS], beyond, t, own_piece(t))
 
     def even_second(t):
         return back_copy(1, out_ref.at[chunk_place(t), near, deep_low], next_to, t)
@@ -1304,8 +1322,8 @@
         for k in range(1, depth):
             deep_copy(t, k).wait()
         for k in range(1, depth):
-            summed = summed + wide(deep_in[t, k - 1])
-        piece[t] = narrow(summed)
+            summed = summed + wide(deep_in[t % TURNS, k - 1])
+        piece[t % TURNS] = narrow(summed)
         local_copy(t).start()
         back_high(t).start()
 
@@ -1324,6 +1342,9 @@
             odd_third(t).start()
 
         by_parity(t, even, odd)
+
+    def after_third(t):
+        by_parity(t, lambda t: even_third(t).wait(), lambda t: odd_third(t).wait())
 
     def expand_back(layer, slot):
         tiles = width // TILE
@@ -1403,8 +1424,10 @@
             s, pair = i // pairs, i % pairs
             at_rows = sublanes(query_rows + s * passage_len, passage_len)
             at = lanes(pair * 2 * DH, 2 * DH)
+            live_rows = sublanes(query_rows + s * passage_len, live)
+            dead_rows = sublanes(query_rows + s * passage_len + live, passage_len - live)
             even, odd = lane_masks(passage_len)
-            q2, k2, v2 = quad[0, at_rows, at], quad[1, at_rows, at], quad[2, at_rows, at]
+            q2, k2, v2 = quad[0, at_rows, at], quad[1, live_rows, at], quad[2, live_rows, at]
             d2 = dc[at_rows, at]
             shares = pt[i]
             deltas = jnp.concatenate([d2 * even, d2 * odd], axis=0)
@@ -1412,14 +1435,17 @@
             delta_scores = score_back(shares, contract_last(v2, deltas))
             queries = jnp.concatenate([q2 * even, q2 * odd], axis=0)
             delta_key = narrow(product(delta_scores, queries) * 0.125)
-            keys = jnp.concatenate([k2 * even, k2 * odd], axis=0)
+            keys = jnp.concatenate([k2 * even[:live], k2 * odd[:live]], axis=0)
             piled = jnp.concatenate(
                 [delta_scores[:, :passage_len], delta_scores[:, passage_len:]], axis=0
             )
             delta_query = narrow((contract_rows(keys, piled) * 0.125).T)
             quad[0, at_rows, at] = delta_query
-            quad[1, at_rows, at] = delta_key
-            quad[2, at_rows, at] = delta_value
+            quad[1, live_rows, at] = delta_key
+            quad[2, live_rows, at] = delta_value
+            nothing = jnp.zeros((passage_len - live, 2 * DH), jnp.bfloat16)
+            quad[1, dead_rows, at] = nothing
+            quad[2, dead_rows, at] = nothing
             tally(layer, S_QUERY, at, wide(delta_query))
             tally(layer, S_VALUE, at, wide(delta_value))
 
@@ -1498,9 +1524,6 @@
         def _():
             @pl.when(step > 0)
             def _():
-                for name in ("c", "q", "k", "v", "x"):
-                    load(name, layer).start()
-
                 load("u2", layer).wait()
 
                 @pl.loop(0, total // norm_step)
@@ -1508,6 +1531,17 @@
                     last_norm_back(layer, tile)
 
             load("f", layer).wait()
+
+            @pl.when(step == 0)
+            def _():
+                start_weights(1, layer, 1)
+
+        for at, names in ((1, ("u1",)), (2, ("q", "k", "v", "ptq")), (3, ("pt", "m")), (5, ("c", "x"))):
+
+            @pl.when(busy & (part == at))
+            def _():
+                for name in names:
+                    load(name, layer).start()
 
         @pl.when(busy & (part == 4))
         def _():
@@ -1555,8 +1589,7 @@
 
             @pl.when(more)
             def _():
-                for name in ("f", "u1"):
-                    load(name, layer - 1).start()
+                load("f", layer - 1).start()
 
         @pl.when(busy & (part == 4))
         def _():
@@ -1582,8 +1615,7 @@
         def _():
             @pl.when(more)
             def _():
-                for name in ("pt", "ptq", "slope", "m"):
-                    load(name, layer - 1).start()
+                load("slope", layer - 1).start()
 
             hidden_back(slot)
 
@@ -1596,7 +1628,7 @@
                 for copy in gradients_out():
                     copy.start()
 
-        for lag, stage in zip(LAGS, (after_side, after_near, after_deep, after_high, after_second)):
+        for lag, stage in zip(LAGS, (after_side, after_near, after_deep, after_high, after_second, after_third)):
 
             @pl.when((t >= lag) & (t < CHUNKS + lag))
             def _():
@@ -1633,10 +1665,6 @@
             for k in range(1, depth):
                 summed = summed + small_deep[k]
             small_out[...] = summed
-
-    @pl.loop(0, CHUNKS)
-    def _(t):
-        by_parity(t, lambda t: even_third(t).wait(), lambda t: odd_third(t).wait())
 
     for copy in gradients_out():
         copy.wait()
@@ -1697,8 +1725,8 @@
             pltpu.VMEM((CORE_SLOTS, 2, rows, columns), bf16),
             pltpu.VMEM((SIDE_SLOTS, rows, columns), bf16),
             pltpu.VMEM((NEAR_SLOTS, rows // 2, columns), bf16),
-            pltpu.VMEM((CHUNKS, depth - 1, piece_rows, columns), bf16),
-            pltpu.VMEM((CHUNKS, piece_rows, columns), bf16),
+            pltpu.VMEM((TURNS, depth - 1, piece_rows, columns), bf16),
+            pltpu.VMEM((TURNS, piece_rows, columns), bf16),
             pltpu.VMEM(small_shape, f32),
             pltpu.VMEM(small_shape, f32),
             pltpu.VMEM(small_shape, f32),
@@ -1726,13 +1754,13 @@
             dma((7,)),
             dma((12,)),
             dma((2, 4)),
-            dma((2, CHUNKS)),
-            dma((2, CHUNKS)),
-            dma((2, CHUNKS)),
-            dma((depth - 1, CHUNKS)),
-            dma((depth - 1, CHUNKS)),
-            dma((2, 3, CHUNKS)),
-            dma((CHUNKS,)),
+            dma((2, CORE_SLOTS)),
+            dma((2, SIDE_SLOTS)),
+            dma((2, NEAR_SLOTS)),
+            dma((depth - 1, TURNS)),
+            dma((depth - 1, TURNS)),
+            dma((2, 3, TURNS)),
+            dma((TURNS,)),
             dma((6,)),
             dma((depth - 1,)),
             dma((depth - 1,)),
@@ -1874,23 +1902,8 @@
     for i in range(3 * LAYERS):
         span = pl.ds(i * each, each)
         loads.append(pltpu.make_async_copy(out_ref.at[span], sums.at[span], in_sem.at[i]))
-    for copy in little + loads + moves:
+    for copy in loads + moves + little:
         copy.start()
-    for copy in little:
-        copy.wait()
-    for i in range(loss_out.shape[0]):
-        loss_out[i] = jnp.sum(loss[0:1, i : i + 1])
-    group = lax.axis_index("grp")
-    vectors = small_ref[:, :8, 0:quarter]
-    expand_bias = small_ref[:, S_EXPAND, :]
-    for g in range(1, 4):
-        vectors = jnp.where(
-            group == g, small_ref[:, :8, g * quarter : (g + 1) * quarter], vectors
-        )
-        expand_bias = jnp.where(group == g, small_ref[:, S_EXPAND + g, :], expand_bias)
-    for i in range(8):
-        vector_outs[i][...] = vectors[:, i, :]
-    expand_bias_out[...] = expand_bias
     stores = []
 
     def store(source, target):
@@ -1928,6 +1941,21 @@
                 ]
         for which in range(4):
             store(squares.at[which, layer], square_outs[which].at[layer])
+    for copy in little:
+        copy.wait()
+    for i in range(loss_out.shape[0]):
+        loss_out[i] = jnp.sum(loss[0:1, i : i + 1])
+    group = lax.axis_index("grp")
+    vectors = small_ref[:, :8, 0:quarter]
+    expand_bias = small_ref[:, S_EXPAND, :]
+    for g in range(1, 4):
+        vectors = jnp.where(
+            group == g, small_ref[:, :8, g * quarter : (g + 1) * quarter], vectors
+        )
+        expand_bias = jnp.where(group == g, small_ref[:, S_EXPAND + g, :], expand_bias)
+    for i in range(8):
+        vector_outs[i][...] = vectors[:, i, :]
+    expand_bias_out[...] = expand_bias
     for copy in stores:
         copy.wait()
 

time: 286 us -> 268 us (0.937)
  Pallas kernels: 285 us -> 267 us
    pallas_call x1, Pallas kernels: 61.7 us -> 46.8 us  [run_forward(): pl.pallas_call(forward_kernel, out_shape=(jax.ShapeDtypeStruct((query_row...]
    pallas_call x1, Pallas kernels: 213 us -> 210 us  [run_backward(): pl.pallas_call(backward_kernel, out_shape=(jax.ShapeDtypeStruct((CHUNKS,...]
where the time goes in v4:
time: 268 us
  Pallas kernels  267 us (100%)
    pallas_call x1, Pallas kernels, run_backward(): pl.pallas_call(backward_kernel, out_shape=(jax.ShapeDtypeStruct((CHUNKS,...  210 us
    pallas_call x1, Pallas kernels, run_forward(): pl.pallas_call(forward_kernel, out_shape=(jax.ShapeDtypeStruct((query_row...  46.8 us
    pallas_call x1, Pallas kernels, finish(): pl.pallas_call(finish_kernel, out_shape=[jax.ShapeDtypeStruct(shape, f32)...  10.3 us

profile of v4, /device:TPU:0, one launch (start us, length us, event | category | flops | bytes accessed | tf_op | source)
XLA Modules:
  0.0 267.9 jit_solution(1394549571119026278)
XLA Ops:
  0.7 46.8 %shard_map.383 = (bf16[64,768]{1,0:T(8,128)(2,1)}, bf16[512,768]{1,0:T(8,128)(2,1)}, bf16[2,576,768]{2,1,0:T(8,128)(2,1)}, bf16[2,576,768]{2,1,0:T(8,128)(2,1)},...) custom-call(s32[2]{0:T(128)} %query_lengths.1, ...), custom_call_target="tpu_custom_call" | custom-call | tf_op jit(solution)/shard_map/pallas_call | solution.py:725
  47.4 210.1 %shard_map.384 = (bf16[24,2,2,96,384]{4,3,2,1,0:T(8,128)(2,1)}, f32[2,16,768]{2,1,0:T(8,128)}, f32[8,128]{1,0:T(8,128)}, f32[64,768]{1,0:T(8,128)}, f32[512,768]{1,0:T(8,128)}) custom-call(s32[2]{0:T(128)} %margin_ref.1, s32[2]{0:T(128)} %positive_ref.1, s32[1,64]{1,0:T(1,128)} %bitcast.17, bf16[2,768]{1,0:T(2,128)(2,1)} %norm_gain.3, ...), custom_call_target="tpu_custom_call" | custom-call | tf_op jit(solution)/shard_map/pallas_call | solution.py:1710
  257.5 10.3 %shard_map.385 = (f32[2,768,768]{2,1,0:T(8,128)}, f32[2,192,3072]{2,1,0:T(8,128)}, f32[2,192,768]{2,1,0:T(8,128)}, f32[2,192,768]{2,1,0:T(8,128)}, f32[2,192,768...) custom-call(bf16[24,384,384]{2,1,0:T(8,128)(2,1)} %bitcast.10, ...), custom_call_target="tpu_custom_call" | custom-call | tf_op jit(solution)/shard_map/pallas_call | solution.py:1972

commit v5 on v4

--- a/solution.py
+++ b/solution.py
@@ -546,7 +546,7 @@
         gain = vec_ref[layer, pl.ds(gain_row, 1), :]
         shift = vec_ref[layer, pl.ds(shift_row, 1), :]
 
-        @pl.loop(0, total // step, unroll=2)
+        @pl.loop(0, total // step, unroll=6)
         def _(i):
             at = sublanes(i * step, step)
             full, unit_rows, scaled = norm_forward(z[at, :], gain, shift)
@@ -635,7 +635,7 @@
             for which in range(6):
                 weight_copy(which, layer + 1).start()
 
-        @pl.loop(0, width // TILE)
+        @pl.loop(0, width // TILE, unroll=3)
         def _(i):
             at = lanes(i * TILE)
             z[:, at] = (
@@ -655,7 +655,7 @@
         reuse(SLOPE, layer)
         reuse(F, layer)
 
-        @pl.loop(0, 4 * width // TILE, unroll=2)
+        @pl.loop(0, 4 * width // TILE, unroll=6)
         def _(i):
             at = lanes(i * TILE)
             tiles = width // TILE
@@ -671,7 +671,7 @@
 
         weight_copy(5, layer).wait()
 
-        @pl.loop(0, width // TILE)
+        @pl.loop(0, width // TILE, unroll=3)
         def _(i):
             at = lanes(i * TILE)
             z[:, at] = (
@@ -1252,7 +1252,7 @@
     def add_rows(target, former, latter, count):
         step = 48
 
-        @pl.loop(0, count // step)
+        @pl.loop(0, count // step, unroll=2)
         def _(i):
             def at(first_row):
                 return sublanes(first_row + i * step, step)
@@ -1349,7 +1349,7 @@
     def expand_back(layer, slot):
         tiles = width // TILE
 
-        @pl.loop(0, 4 * tiles)
+        @pl.loop(0, 4 * tiles, unroll=2)
         def _(i):
             at = lanes(i * TILE)
             block, tile = i // tiles, i % tiles
@@ -1359,7 +1359,7 @@
             tally(layer, S_EXPAND + block, lanes(tile * TILE), wide(value))
 
     def middle_back(slot):
-        @pl.loop(0, width // TILE)
+        @pl.loop(0, width // TILE, unroll=3)
         def _(i):
             at = lanes(i * TILE)
             value = dz[:, at]
@@ -1369,13 +1369,13 @@
             dz[:, at] = value
 
     def context_back(slot):
-        @pl.loop(0, width // TILE)
+        @pl.loop(0, width // TILE, unroll=3)
         def _(i):
             weight = w[slot, 3, sublanes(i * TILE, TILE), :]
             dc[:, lanes(i * TILE)] = narrow(contract_last(quad[3], weight))
 
     def hidden_back(slot):
-        @pl.loop(0, width // TILE)
+        @pl.loop(0, width // TILE, unroll=3)
         def _(i):
             at = lanes(i * TILE)
             value = dz[:, at]
@@ -1419,7 +1419,7 @@
         tally(layer, S_VALUE, every_lane, wide(delta_value))
 
     def passage_attention_back(layer, low, high):
-        @pl.loop(low, high)
+        @pl.loop(low, high, unroll=2)
         def _(i):
             s, pair = i // pairs, i % pairs
             at_rows = sublanes(query_rows + s * passage_len, passage_len)
@@ -1454,7 +1454,7 @@
 
         @pl.when(part < 4)
         def _():
-            @pl.loop(0, 4)
+            @pl.loop(0, 4, unroll=2)
             def _(i):
                 taller = active[:, lanes(i * width + pair * rows, rows)]
                 buf[t % 2, i // 2, i % 2] = narrow(contract_rows(taller, dy[:, half]))
@@ -1470,14 +1470,14 @@
 
         @pl.when((part >= 4) & (part < 8))
         def _():
-            @pl.loop(0, 4)
+            @pl.loop(0, 4, unroll=2)
             def _(i):
                 wider = du[:, lanes((2 * pair + i // 2) * width + (part % 2) * columns, columns)]
                 split(i, contract_rows(middle[:, two_quarters(i)], wider))
 
         @pl.when(part >= 8)
         def _():
-            @pl.loop(0, 4)
+            @pl.loop(0, 4, unroll=2)
             def _(i):
                 which = 2 * pair + i // 2
                 split(
@@ -1580,7 +1580,7 @@
         def _():
             load("u1", layer).wait()
 
-            @pl.loop(0, total // norm_step)
+            @pl.loop(0, total // norm_step, unroll=2)
             def _(tile):
                 first_norm_back(layer, tile)
 

time: 268 us -> 262 us (0.978)
  Pallas kernels: 267 us -> 261 us
    pallas_call x1, Pallas kernels: 46.8 us -> 43.1 us  [run_forward(): pl.pallas_call(forward_kernel, out_shape=(jax.ShapeDtypeStruct((query_row...]
where the time goes in v5:
time: 262 us
  Pallas kernels  261 us (100%)
    pallas_call x1, Pallas kernels, run_backward(): pl.pallas_call(backward_kernel, out_shape=(jax.ShapeDtypeStruct((CHUNKS,...  208 us
    pallas_call x1, Pallas kernels, run_forward(): pl.pallas_call(forward_kernel, out_shape=(jax.ShapeDtypeStruct((query_row...  43.1 us
    pallas_call x1, Pallas kernels, finish(): pl.pallas_call(finish_kernel, out_shape=[jax.ShapeDtypeStruct(shape, f32)...  10.3 us

profile of v5, /device:TPU:0, one launch (start us, length us, event | category | flops | bytes accessed | tf_op | source)
XLA Modules:
  0.0 261.9 jit_solution(6143714161676998692)
XLA Ops:
  0.7 43.1 %shard_map.383 = (bf16[64,768]{1,0:T(8,128)(2,1)}, bf16[512,768]{1,0:T(8,128)(2,1)}, bf16[2,576,768]{2,1,0:T(8,128)(2,1)}, bf16[2,576,768]{2,1,0:T(8,128)(2,1)},...) custom-call(s32[2]{0:T(128)} %query_lengths.1, ...), custom_call_target="tpu_custom_call" | custom-call | tf_op jit(solution)/shard_map/pallas_call | solution.py:725
  43.8 207.7 %shard_map.384 = (bf16[24,2,2,96,384]{4,3,2,1,0:T(8,128)(2,1)}, f32[2,16,768]{2,1,0:T(8,128)}, f32[8,128]{1,0:T(8,128)}, f32[64,768]{1,0:T(8,128)}, f32[512,768]{1,0:T(8,128)}) custom-call(s32[2]{0:T(128)} %margin_ref.1, s32[2]{0:T(128)} %positive_ref.1, s32[1,64]{1,0:T(1,128)} %bitcast.17, bf16[2,768]{1,0:T(2,128)(2,1)} %norm_gain.3, ...), custom_call_target="tpu_custom_call" | custom-call | tf_op jit(solution)/shard_map/pallas_call | solution.py:1710
  251.5 10.3 %shard_map.385 = (f32[2,768,768]{2,1,0:T(8,128)}, f32[2,192,3072]{2,1,0:T(8,128)}, f32[2,192,768]{2,1,0:T(8,128)}, f32[2,192,768]{2,1,0:T(8,128)}, f32[2,192,768...) custom-call(bf16[24,384,384]{2,1,0:T(8,128)(2,1)} %bitcast.10, ...), custom_call_target="tpu_custom_call" | custom-call | tf_op jit(solution)/shard_map/pallas_call | solution.py:1972

commit v6 on v5

--- a/solution.py
+++ b/solution.py
@@ -757,7 +757,7 @@
 CHUNKS = 24
 PARTS = 12
 S_QUERY, S_VALUE, S_MIX, S_GAIN, S_SHIFT, S_REDUCE, S_LAST_GAIN, S_LAST_SHIFT, S_EXPAND = range(9)
-CORE_SLOTS, SIDE_SLOTS, NEAR_SLOTS, KEEP_SLOTS, SENT_SLOTS = 4, 4, 4, 6, 3
+CORE_SLOTS, SIDE_SLOTS, NEAR_SLOTS, KEEP_SLOTS, SENT_SLOTS = 6, 6, 6, 8, 4
 TURNS = 8
 LAGS = (2, 3, 4, 5, 6, 9)
 BLOCK = 16

time: 262 us -> 262 us (level)
  no operation moved by 1% of the time
where the time goes in v6:
time: 262 us
  Pallas kernels  261 us (100%)
    pallas_call x1, Pallas kernels, run_backward(): pl.pallas_call(backward_kernel, out_shape=(jax.ShapeDtypeStruct((CHUNKS,...  208 us
    pallas_call x1, Pallas kernels, run_forward(): pl.pallas_call(forward_kernel, out_shape=(jax.ShapeDtypeStruct((query_row...  43.1 us
    pallas_call x1, Pallas kernels, finish(): pl.pallas_call(finish_kernel, out_shape=[jax.ShapeDtypeStruct(shape, f32)...  10.3 us

profile of v6, /device:TPU:0, one launch (start us, length us, event | category | flops | bytes accessed | tf_op | source)
XLA Modules:
  0.0 262.0 jit_solution(14511682723409761201)
XLA Ops:
  0.7 43.1 %shard_map.383 = (bf16[64,768]{1,0:T(8,128)(2,1)}, bf16[512,768]{1,0:T(8,128)(2,1)}, bf16[2,576,768]{2,1,0:T(8,128)(2,1)}, bf16[2,576,768]{2,1,0:T(8,128)(2,1)},...) custom-call(s32[2]{0:T(128)} %query_lengths.1, ...), custom_call_target="tpu_custom_call" | custom-call | tf_op jit(solution)/shard_map/pallas_call | solution.py:725
  43.8 207.8 %shard_map.384 = (bf16[24,2,2,96,384]{4,3,2,1,0:T(8,128)(2,1)}, f32[2,16,768]{2,1,0:T(8,128)}, f32[8,128]{1,0:T(8,128)}, f32[64,768]{1,0:T(8,128)}, f32[512,768]{1,0:T(8,128)}) custom-call(s32[2]{0:T(128)} %margin_ref.1, s32[2]{0:T(128)} %positive_ref.1, s32[1,64]{1,0:T(1,128)} %bitcast.17, bf16[2,768]{1,0:T(2,128)(2,1)} %norm_gain.3, ...), custom_call_target="tpu_custom_call" | custom-call | tf_op jit(solution)/shard_map/pallas_call | solution.py:1710
  251.6 10.3 %shard_map.385 = (f32[2,768,768]{2,1,0:T(8,128)}, f32[2,192,3072]{2,1,0:T(8,128)}, f32[2,192,768]{2,1,0:T(8,128)}, f32[2,192,768]{2,1,0:T(8,128)}, f32[2,192,768...) custom-call(bf16[24,384,384]{2,1,0:T(8,128)(2,1)} %bitcast.10, ...), custom_call_target="tpu_custom_call" | custom-call | tf_op jit(solution)/shard_map/pallas_call | solution.py:1972
